TPU v7x, 256 devices: a whole 4x4x8 slice. The times are simulated.
256 devices in a mesh: gx: 16 (over x, z_hi, core), gy: 16 (over y, z_lo).
Axes of the slice: x: 4, y: 4, z: 8 (z_hi: 2, z_lo: 4; z = z_hi * 4 + z_lo), core: 2. Of those that a mesh axis runs over, the one named last changes fastest.
Arguments:
- east_velocity: float32 [48, 128, 4096], P(None, 'gx', 'gy'), may hold values from -3 to 3
- north_velocity: float32 [48, 128, 4096], P(None, 'gx', 'gy'), may hold values from -3 to 3
- salinity: float32 [48, 128, 4096], P(None, 'gx', 'gy'), may hold values from -6 to 6
- surface: float32 [128, 4096], P('gx', 'gy'), may hold values from -6 to 6
- column_depth: float32 [128, 4096], P('gx', 'gy'), may hold values from 0.5 to 4
- wet_column: int32 [128, 4096], P('gx', 'gy'), may hold values 0 or 1
- active_levels: int32 [128, 4096], P('gx', 'gy'), may hold values from 1 to 48
Outputs:
- east_flow: float32 [48, 128, 4096], P(None, 'gx', 'gy')
- north_flow: float32 [48, 128, 4096], P(None, 'gx', 'gy')
- salt_next: float32 [48, 128, 4096], P(None, 'gx', 'gy')
- surface_next: float32 [128, 4096], P('gx', 'gy')
All inputs are finite; a program needn't handle non-finite values. No bound on the sum of `wet_column` on one device may be relied on, other than what follows from the above.
Results may differ from a plain program's by a relative error of at most 0.000024.
Values sent between devices are 32-bit elements; how exact they have to be, the bound alone decides.
No kernel may reach another device: no remote copies, remote signals or barrier semaphores. Data moves between devices by JAX's collectives and lax.ppermute only.
A program may use at most 64 MiB of HBM per device.

v0:
```python
import jax
import jax.numpy as jnp
from jax import lax
from jax.sharding import PartitionSpec as P

ITERS = 16


TIME_STEP = 0.2
CORIOLIS = 0.3
PRESS_COEF = 0.05
VISCOSITY = 0.1
DIFFUSIVITY = 0.1
SIGMA_SHIFT = 0.25
CHEB_CENTER = 3.625
CHEB_HALF = 3.375
DIVERGENCE_COEF = 8.0


def padded_2(cells, sides, width):
    for axis, dim in sides:
        count = lax.axis_size(axis)
        ends = count - 1
        head = lax.slice_in_dim(cells, 0, width, axis=dim)
        tail = lax.slice_in_dim(cells, cells.shape[dim] - width, cells.shape[dim], axis=dim)
        cells = jnp.concatenate(
            [
                lax.ppermute(tail, axis, [(i, (i + 1) % count) for i in range(ends)]),
                cells,
                lax.ppermute(head, axis, [((i + 1) % count, i) for i in range(ends)]),
            ],
            axis=dim,
        )
    return cells


def extended(array, sides, width):
    edges = {}
    for axis, dim in sides:
        devices, length = (lax.axis_size(axis), array.shape[dim])
        up = [(i, (i + 1) % devices) for i in range(devices - 1)]
        last = lax.slice_in_dim(array, length - width, length, axis=dim)
        leading = lax.slice_in_dim(array, 0, width, axis=dim)
        edges[dim] = (
            lax.ppermute(last, axis, up),
            lax.ppermute(leading, axis, [(b, a) for a, b in up]),
        )
    done = []
    for _, dim in sides:
        low, high = edges[dim]
        around = [(width, width) if d in done else (0, 0) for d in range(array.ndim)]
        array = jnp.concatenate([jnp.pad(low, around), array, jnp.pad(high, around)], axis=dim)
        done.append(dim)
    return array


def cheb_table(count):
    first = CHEB_CENTER / CHEB_HALF
    ratio = 1.0 / first
    keeps = []
    gains = []
    for index in range(count):
        ratio_next = 1.0 / (2.0 * first - ratio)
        keeps.append(ratio_next * ratio)
        gains.append(2.0 * ratio_next / CHEB_HALF)
        ratio = ratio_next
    return (keeps, gains)


def crop(array, width):
    if width == 0:
        return array
    return array[..., width : array.shape[-2] - width, width : array.shape[-1] - width]


def centre(field):
    return field[:, 2:-2, 2:-2]


def along_east(field):
    return (
        8.0 * (field[:, 3:-1, 2:-2] - field[:, 1:-3, 2:-2])
        - (field[:, 4:, 2:-2] - field[:, :-4, 2:-2])
    ) / 12.0


def along_north(field):
    return (
        8.0 * (field[:, 2:-2, 3:-1] - field[:, 2:-2, 1:-3])
        - (field[:, 2:-2, 4:] - field[:, 2:-2, :-4])
    ) / 12.0


def laplace(field):
    return (
        field[:, 3:-1, 2:-2]
        + field[:, 1:-3, 2:-2]
        + field[:, 2:-2, 3:-1]
        + field[:, 2:-2, 1:-3]
        - 4.0 * centre(field)
    )


def tendency(padded):
    east, north, tracer = (padded[0], padded[1], padded[2])
    pressure = PRESS_COEF * jnp.cumsum(tracer, axis=0)
    east_mid = centre(east)
    north_mid = centre(north)

    def advect(field):
        return -(east_mid * along_east(field) + north_mid * along_north(field))

    east_rate = (
        advect(east) + CORIOLIS * north_mid - along_east(pressure) + VISCOSITY * laplace(east)
    )
    north_rate = (
        advect(north) - CORIOLIS * east_mid - along_north(pressure) + VISCOSITY * laplace(north)
    )
    salt_rate = advect(tracer) + DIFFUSIVITY * laplace(tracer)
    return jnp.stack([east_rate, north_rate, salt_rate])


def nine_point(field, wet):
    weighted = wet * field
    edges = weighted[2:, 1:-1] + weighted[:-2, 1:-1] + weighted[1:-1, 2:] + weighted[1:-1, :-2]
    corners = weighted[2:, 2:] + weighted[2:, :-2] + weighted[:-2, 2:] + weighted[:-2, :-2]
    stencil = (20.0 * weighted[1:-1, 1:-1] - 4.0 * edges - corners) / 6.0
    wet_mid = wet[1:-1, 1:-1]
    field_mid = field[1:-1, 1:-1]
    return wet_mid * (SIGMA_SHIFT * field_mid + stencil) + (1.0 - wet_mid) * field_mid


def solver_rim(stacked, width):
    return padded_2(stacked, (("gx", 1), ("gy", 2)), width)


def chebyshev(right_side, start, wet):
    depth_rim = 4
    padded = solver_rim(jnp.stack([start, wet]), depth_rim)
    wet_pad = padded[1]
    residual = right_side - nine_point(crop(padded[0], depth_rim - 1), crop(wet_pad, depth_rim - 1))
    direction = residual / CHEB_CENTER
    keeps, gains = cheb_table(ITERS)
    keep_table = jnp.array(keeps, dtype=jnp.float32)
    gain_table = jnp.array(gains, dtype=jnp.float32)

    def sweep(outer, carry):
        solution, residual, direction = carry
        padded = solver_rim(jnp.stack([residual, direction]), depth_rim)
        res_pad, dir_pad = (padded[0], padded[1])
        for inner in range(depth_rim):
            solution = solution + crop(dir_pad, depth_rim - inner)
            image = nine_point(dir_pad, crop(wet_pad, inner))
            res_pad = crop(res_pad, 1) - image
            position = outer * depth_rim + inner
            dir_pad = keep_table[position] * crop(dir_pad, 1) + gain_table[position] * res_pad
        return (solution, res_pad, dir_pad)

    solution, residual, direction = lax.fori_loop(
        0, ITERS // depth_rim, sweep, (start, residual, direction)
    )
    return solution


def local(
    east_velocity, north_velocity, salinity, surface, column_depth, wet_column, active_levels
):
    wet = wet_column.astype(jnp.float32)
    levels = jnp.arange(east_velocity.shape[0], dtype=jnp.int32)
    mask3 = (levels[:, None, None] < active_levels[None]).astype(jnp.float32) * wet[None]

    def rate(state):
        padded = extended(state, (("gx", 2), ("gy", 3)), 2)
        return tendency(padded) * mask3

    state0 = jnp.stack([east_velocity, north_velocity, salinity]) * mask3
    state1 = state0 + TIME_STEP * rate(state0)
    state2 = 0.75 * state0 + 0.25 * (state1 + TIME_STEP * rate(state1))
    state3 = state0 / 3.0 + 2.0 / 3.0 * (state2 + TIME_STEP * rate(state2))
    level_count = east_velocity.shape[0]
    flow_east = column_depth * (jnp.sum(state3[0], axis=0) / level_count)
    flow_north = column_depth * (jnp.sum(state3[1], axis=0) / level_count)
    flows = extended(jnp.stack([flow_east, flow_north]), (("gx", 1), ("gy", 2)), 1)
    divergence = (flows[0, 2:, 1:-1] - flows[0, :-2, 1:-1]) * 0.5 + (
        flows[1, 1:-1, 2:] - flows[1, 1:-1, :-2]
    ) * 0.5
    right_side = wet * (SIGMA_SHIFT * surface - DIVERGENCE_COEF * divergence)
    solution = chebyshev(right_side, surface, wet)
    surface_pad = extended(solution, (("gx", 0), ("gy", 1)), 1)
    slope_east = (surface_pad[2:, 1:-1] - surface_pad[:-2, 1:-1]) * 0.5
    slope_north = (surface_pad[1:-1, 2:] - surface_pad[1:-1, :-2]) * 0.5
    east_flow = mask3 * (state3[0] - slope_east[None])
    north_flow = mask3 * (state3[1] - slope_north[None])
    return (east_flow, north_flow, state3[2], solution)


def solution(mesh):
    return jax.shard_map(
        local,
        mesh=mesh,
        in_specs=(
            P(None, "gx", "gy"),
            P(None, "gx", "gy"),
            P(None, "gx", "gy"),
            P("gx", "gy"),
            P("gx", "gy"),
            P("gx", "gy"),
            P("gx", "gy"),
        ),
        out_specs=(P(None, "gx", "gy"), P(None, "gx", "gy"), P(None, "gx", "gy"), P("gx", "gy")),
        check_vma=False,
    )
```

profile of v0, /device:TPU:31, one launch (start us, length us, event | category | flops | bytes accessed | tf_op | source)
XLA Modules:
  0.0 283.8 jit_solution(15104870486544828865)
XLA Ops:
  4.6 8.7 %collective-permute-start.20 = (f32[2,4,256]{2,1,0:T(4,128)S(1)}, f32[2,4,256]{2,1,0:T(4,128)S(1)}, u32[]{:S(2)}, u32[]{:S(2)}) collective-permute-start(f32[2,4,256]{2,1,0:T(4,128)S(1)} %get-tuple-element.279), channel_id=1, source_target_pairs={{0,16},{16,32},{32,48},{48,64},{64,80},{80,96},{96,112},{112,128},... | collective-permute-start | bytes 24584 | tf_op jit(solution)/shard_map/ppermute | solution.py:28
  18.4 7.5 %collective-permute-start.5 = (f32[3,48,2,256]{3,2,1,0:T(2,128)}, f32[3,48,2,256]{3,2,1,0:T(2,128)S(1)}, u32[]{:S(2)}, u32[]{:S(2)}) collective-permute-start(f32[3,48,2,256]{3,2,1,0:T(2,128)} %get-tuple-element.267), channel_id=1, source_target_pairs={{0,16},{16,32},{32,48},{48,64},{64,80},{80,96},{96,112},{112,128},... | collective-permute-start | bytes 884744 | tf_op jit(solution)/shard_map/ppermute | solution.py:45
  26.0 4.6 %collective-permute-start.23 = (f32[2,16,4]{2,1,0:T(8,128)S(1)}, f32[2,16,4]{2,1,0:T(8,128)S(1)}, u32[]{:S(2)}, u32[]{:S(2)}) collective-permute-start(f32[2,16,4]{2,1,0:T(8,128)S(1)} %get-tuple-element.274), channel_id=1, source_target_pairs={{1,0},{2,1},{3,2},{4,3},{5,4},{6,5},{7,6},{8,7},{9,8},{10,9},{11,1... | collective-permute-start | bytes 1544 | tf_op jit(solution)/shard_map/ppermute | solution.py:30
  33.3 6.1 %collective-permute-start.7 = (f32[3,48,8,2]{1,2,3,0:T(8,128)S(1)}, f32[3,48,8,2]{1,2,3,0:T(8,128)S(1)}, u32[]{:S(2)}, u32[]{:S(2)}) collective-permute-start(f32[3,48,8,2]{1,2,3,0:T(8,128)S(1)} %copy.15), channel_id=1, source_target_pairs={{1,0},{2,1},{3,2},{4,3},{5,4},{6,5},{7,6},{8,7},{9,8},{10,9},{11,1... | collective-permute-start | bytes 27656 | tf_op jit(solution)/shard_map/ppermute | solution.py:46
  43.6 4.2 %collective-permute-done.4 = f32[3,48,8,2]{1,2,3,0:T(8,128)S(1)} collective-permute-done((f32[3,48,8,2]{1,2,3,0:T(8,128)S(1)}, f32[3,48,8,2]{1,2,3,0:T(8,128)S(1)}, u32[]{:S(2)}, u32[]{:S(2)}) %collective-permute-start.4) | collective-permute-done | bytes 9248 | tf_op jit(solution)/shard_map/ppermute | solution.py:45
  59.0 6.6 %collective-permute-start.9 = (f32[3,48,2,256]{3,2,1,0:T(2,128)}, f32[3,48,2,256]{3,2,1,0:T(2,128)}, u32[]{:S(2)}, u32[]{:S(2)}) collective-permute-start(f32[3,48,2,256]{3,2,1,0:T(2,128)} %get-tuple-element.263), channel_id=1, source_target_pairs={{0,16},{16,32},{32,48},{48,64},{64,80},{80,96},{96,112},{112,128},... | collective-permute-start | bytes 884744 | tf_op jit(solution)/shard_map/ppermute | solution.py:45
  72.5 3.5 %collective-permute-start.8 = (f32[3,48,8,2]{1,2,3,0:T(8,128)}, f32[3,48,8,2]{1,2,3,0:T(8,128)}, u32[]{:S(2)}, u32[]{:S(2)}) collective-permute-start(f32[3,48,8,2]{1,2,3,0:T(8,128)} %copy.17), channel_id=1, source_target_pairs={{0,1},{1,2},{2,3},{3,4},{4,5},{5,6},{6,7},{7,8},{8,9},{9,10},{10,1... | collective-permute-start | bytes 27656 | tf_op jit(solution)/shard_map/ppermute | solution.py:45
  81.9 3.8 %select_maximum_fusion.2 = f32[3,48,12,260]{3,2,1,0:T(8,128)S(1)} fusion(f32[3,48,8,2]{3,2,1,0:T(8,128)} %copy.20, f32[3,48,8,2]{3,2,1,0:T(8,128)} %copy.18, f32[3,48,2,256]{3,2,1,0:T(2,128)S(1)} %collective-permute-done.10, f32[3,48,8,256]{3,2,1,0:T(8,128)S(1)} %fusion.36, f32[3,48,2,256]{3,2,1,0:T(2,128)} %collective-permute-done.9), kind=kLoop, calls=%fused_computation.82 | loop fusion | flops 3594240 | bytes 3585024 | tf_op jit(solution)/shard_map/concatenate | solution.py:52
  95.0 6.3 %collective-permute-start.13 = (f32[3,48,2,256]{3,2,1,0:T(2,128)}, f32[3,48,2,256]{3,2,1,0:T(2,128)}, u32[]{:S(2)}, u32[]{:S(2)}) collective-permute-start(f32[3,48,2,256]{3,2,1,0:T(2,128)} %get-tuple-element.259), channel_id=1, source_target_pairs={{0,16},{16,32},{32,48},{48,64},{64,80},{80,96},{96,112},{112,128},... | collective-permute-start | bytes 884744 | tf_op jit(solution)/shard_map/ppermute | solution.py:45
  117.7 3.8 %select_maximum_fusion = f32[3,48,12,260]{3,2,1,0:T(8,128)S(1)} fusion(f32[3,48,8,2]{3,2,1,0:T(8,128)} %copy.24, f32[3,48,8,2]{3,2,1,0:T(8,128)} %copy.22, f32[3,48,2,256]{3,2,1,0:T(2,128)S(1)} %collective-permute-done.14, f32[3,48,8,256]{3,2,1,0:T(8,128)S(1)} %fusion.40, f32[3,48,2,256]{3,2,1,0:T(2,128)} %collective-permute-done.13), kind=kLoop, calls=%fused_computation.80 | loop fusion | flops 3594240 | bytes 3585024 | tf_op jit(solution)/shard_map/concatenate | solution.py:52
  127.7 4.1 %collective-permute-start.16 = (f32[2,1,256]{2,1,0:T(1,128)S(1)}, f32[2,1,256]{2,1,0:T(1,128)S(1)}, u32[]{:S(2)}, u32[]{:S(2)}) collective-permute-start(f32[2,1,256]{2,1,0:T(1,128)S(1)} %get-tuple-element.278), channel_id=1, source_target_pairs={{16,0},{32,16},{48,32},{64,48},{80,64},{96,80},{112,96},{128,112},... | collective-permute-start | bytes 6152 | tf_op jit(solution)/shard_map/ppermute | solution.py:46
  131.8 5.4 %collective-permute-start.17 = (f32[2,1,256]{2,1,0:T(1,128)S(1)}, f32[2,1,256]{2,1,0:T(1,128)S(1)}, u32[]{:S(2)}, u32[]{:S(2)}) collective-permute-start(f32[2,1,256]{2,1,0:T(1,128)S(1)} %get-tuple-element.277), channel_id=1, source_target_pairs={{0,16},{16,32},{32,48},{48,64},{64,80},{80,96},{96,112},{112,128},... | collective-permute-start | bytes 6152 | tf_op jit(solution)/shard_map/ppermute | solution.py:45
  139.2 6.1 %collective-permute-start.18 = (f32[2,8,1]{2,1,0:T(8,128)S(1)}, f32[2,8,1]{2,1,0:T(8,128)S(1)}, u32[]{:S(2)}, u32[]{:S(2)}) collective-permute-start(f32[2,8,1]{2,1,0:T(8,128)S(1)} %get-tuple-element.275), channel_id=1, source_target_pairs={{1,0},{2,1},{3,2},{4,3},{5,4},{6,5},{7,6},{8,7},{9,8},{10,9},{11,1... | collective-permute-start | bytes 200 | tf_op jit(solution)/shard_map/ppermute | solution.py:46
  146.2 116.0 %while.20 = (s32[]{:T(128)}, f32[8,256]{1,0:T(8,128)S(1)}, f32[8,256]{1,0:T(8,128)S(1)}, f32[8,256]{1,0:T(8,128)S(1)}, f32[16,264]{1,0:T(8,128)S(1)}, /*index=5*...) while((s32[]{:T(128)}, f32[8,256]{1,0:T(8,128)S(1)}, ...), condition=%wide.region_6.7_spmd.clone, body=%wide.region_5.6_spmd.sunk.clone.sunk | while | flops 332450 | bytes 1074181 | solution.py:159
  146.2 4.7 %collective-permute-start = (f32[2,4,256]{2,1,0:T(4,128)S(1)}, f32[2,4,256]{2,1,0:T(4,128)S(1)}, u32[]{:S(2)}, u32[]{:S(2)}) collective-permute-start(f32[2,4,256]{2,1,0:T(4,128)S(1)} %get-tuple-element.351), channel_id=1, source_target_pairs={{16,0},{32,16},{48,32},{64,48},{80,64},{96,80},{112,96},{128,112},... | collective-permute-start | bytes 24584 | tf_op jit(solution)/shard_map/while/body/eval_jaxpr/ppermute | solution.py:30
  150.9 4.8 %collective-permute-start.1 = (f32[2,4,256]{2,1,0:T(4,128)S(1)}, f32[2,4,256]{2,1,0:T(4,128)S(1)}, u32[]{:S(2)}, u32[]{:S(2)}) collective-permute-start(f32[2,4,256]{2,1,0:T(4,128)S(1)} %get-tuple-element.352), channel_id=1, source_target_pairs={{0,16},{16,32},{32,48},{48,64},{64,80},{80,96},{96,112},{112,128},... | collective-permute-start | bytes 24584 | tf_op jit(solution)/shard_map/while/body/eval_jaxpr/ppermute | solution.py:28
  158.9 6.3 %collective-permute-start.2 = (f32[2,16,4]{2,1,0:T(8,128)S(1)}, f32[2,16,4]{2,1,0:T(8,128)S(1)}, u32[]{:S(2)}, u32[]{:S(2)}) collective-permute-start(f32[2,16,4]{2,1,0:T(8,128)S(1)} %get-tuple-element.353), channel_id=1, source_target_pairs={{1,0},{2,1},{3,2},{4,3},{5,4},{6,5},{7,6},{8,7},{9,8},{10,9},{11,1... | collective-permute-start | bytes 1544 | tf_op jit(solution)/shard_map/while/body/eval_jaxpr/ppermute | solution.py:30
  167.9 4.6 %collective-permute-done.3 = f32[2,16,4]{2,1,0:T(8,128)S(1)} collective-permute-done((f32[2,16,4]{2,1,0:T(8,128)S(1)}, f32[2,16,4]{2,1,0:T(8,128)S(1)}, u32[]{:S(2)}, u32[]{:S(2)}) %collective-permute-start.3) | collective-permute-done | bytes 544 | tf_op jit(solution)/shard_map/while/body/eval_jaxpr/ppermute | solution.py:28
  178.1 10.5 %collective-permute-start = (f32[2,4,256]{2,1,0:T(4,128)S(1)}, f32[2,4,256]{2,1,0:T(4,128)S(1)}, u32[]{:S(2)}, u32[]{:S(2)}) collective-permute-start(f32[2,4,256]{2,1,0:T(4,128)S(1)} %get-tuple-element.351), channel_id=1, source_target_pairs={{16,0},{32,16},{48,32},{64,48},{80,64},{96,80},{112,96},{128,112},... | collective-permute-start | bytes 24584 | tf_op jit(solution)/shard_map/while/body/eval_jaxpr/ppermute | solution.py:30
  193.8 3.4 %collective-permute-start.3 = (f32[2,16,4]{2,1,0:T(8,128)S(1)}, f32[2,16,4]{2,1,0:T(8,128)S(1)}, u32[]{:S(2)}, u32[]{:S(2)}) collective-permute-start(f32[2,16,4]{2,1,0:T(8,128)S(1)} %get-tuple-element.354), channel_id=1, source_target_pairs={{0,1},{1,2},{2,3},{3,4},{4,5},{5,6},{6,7},{7,8},{8,9},{9,10},{10,1... | collective-permute-start | bytes 1544 | tf_op jit(solution)/shard_map/while/body/eval_jaxpr/ppermute | solution.py:28
  206.7 9.8 %collective-permute-start = (f32[2,4,256]{2,1,0:T(4,128)S(1)}, f32[2,4,256]{2,1,0:T(4,128)S(1)}, u32[]{:S(2)}, u32[]{:S(2)}) collective-permute-start(f32[2,4,256]{2,1,0:T(4,128)S(1)} %get-tuple-element.351), channel_id=1, source_target_pairs={{16,0},{32,16},{48,32},{64,48},{80,64},{96,80},{112,96},{128,112},... | collective-permute-start | bytes 24584 | tf_op jit(solution)/shard_map/while/body/eval_jaxpr/ppermute | solution.py:30
  234.4 9.8 %collective-permute-start = (f32[2,4,256]{2,1,0:T(4,128)S(1)}, f32[2,4,256]{2,1,0:T(4,128)S(1)}, u32[]{:S(2)}, u32[]{:S(2)}) collective-permute-start(f32[2,4,256]{2,1,0:T(4,128)S(1)} %get-tuple-element.351), channel_id=1, source_target_pairs={{16,0},{32,16},{48,32},{64,48},{80,64},{96,80},{112,96},{128,112},... | collective-permute-start | bytes 24584 | tf_op jit(solution)/shard_map/while/body/eval_jaxpr/ppermute | solution.py:30
  262.2 9.8 %collective-permute-start.24 = (f32[1,256]{1,0:T(1,128)S(1)}, f32[1,256]{1,0:T(1,128)S(1)}, u32[]{:S(2)}, u32[]{:S(2)}) collective-permute-start(f32[1,256]{1,0:T(1,128)S(1)} %get-tuple-element.285), channel_id=1, source_target_pairs={{16,0},{32,16},{48,32},{64,48},{80,64},{96,80},{112,96},{128,112},... | collective-permute-start | bytes 3080 | tf_op jit(solution)/shard_map/ppermute | solution.py:46
  275.9 6.1 %collective-permute-start.26 = (f32[8,1]{1,0:T(8,128)S(1)}, f32[8,1]{1,0:T(8,128)S(1)}, u32[]{:S(2)}, u32[]{:S(2)}) collective-permute-start(f32[8,1]{1,0:T(8,128)S(1)} %get-tuple-element.283), channel_id=1, source_target_pairs={{1,0},{2,1},{3,2},{4,3},{5,4},{6,5},{7,6},{8,7},{9,8},{10,9},{11,1... | collective-permute-start | bytes 104 | tf_op jit(solution)/shard_map/ppermute | solution.py:46
  (197 shorter events, 141.6 us)
Async XLA Ops:
  2.0 23.9 %collective-permute-start.21 = (f32[2,4,256]{2,1,0:T(4,128)S(1)}, f32[2,4,256]{2,1,0:T(4,128)S(1)}, u32[]{:S(2)}, u32[]{:S(2)}) collective-permute-start(f32[2,4,256]{2,1,0:T(4,128)S(1)} %get-tuple-element.280), channel_id=1, source_target_pairs={{16,0},{32,16},{48,32},{64,48},{80,64},{96,80},{112,96},{128,112},... | collective-permute-start | bytes 24584 | tf_op jit(solution)/shard_map/ppermute | solution.py:30
  4.6 21.3 %collective-permute-start.20 = (f32[2,4,256]{2,1,0:T(4,128)S(1)}, f32[2,4,256]{2,1,0:T(4,128)S(1)}, u32[]{:S(2)}, u32[]{:S(2)}) collective-permute-start(f32[2,4,256]{2,1,0:T(4,128)S(1)} %get-tuple-element.279), channel_id=1, source_target_pairs={{0,16},{16,32},{32,48},{48,64},{64,80},{80,96},{96,112},{112,128},... | collective-permute-start | bytes 24584 | tf_op jit(solution)/shard_map/ppermute | solution.py:28
  16.4 31.7 %collective-permute-start.6 = (f32[3,48,2,256]{3,2,1,0:T(2,128)}, f32[3,48,2,256]{3,2,1,0:T(2,128)S(1)}, u32[]{:S(2)}, u32[]{:S(2)}) collective-permute-start(f32[3,48,2,256]{3,2,1,0:T(2,128)} %get-tuple-element.268), channel_id=1, source_target_pairs={{16,0},{32,16},{48,32},{64,48},{80,64},{96,80},{112,96},{128,112},... | collective-permute-start | bytes 884744 | tf_op jit(solution)/shard_map/ppermute | solution.py:46
  18.4 29.7 %collective-permute-start.5 = (f32[3,48,2,256]{3,2,1,0:T(2,128)}, f32[3,48,2,256]{3,2,1,0:T(2,128)S(1)}, u32[]{:S(2)}, u32[]{:S(2)}) collective-permute-start(f32[3,48,2,256]{3,2,1,0:T(2,128)} %get-tuple-element.267), channel_id=1, source_target_pairs={{0,16},{16,32},{32,48},{48,64},{64,80},{80,96},{96,112},{112,128},... | collective-permute-start | bytes 884744 | tf_op jit(solution)/shard_map/ppermute | solution.py:45
  26.0 14.6 %collective-permute-start.23 = (f32[2,16,4]{2,1,0:T(8,128)S(1)}, f32[2,16,4]{2,1,0:T(8,128)S(1)}, u32[]{:S(2)}, u32[]{:S(2)}) collective-permute-start(f32[2,16,4]{2,1,0:T(8,128)S(1)} %get-tuple-element.274), channel_id=1, source_target_pairs={{1,0},{2,1},{3,2},{4,3},{5,4},{6,5},{7,6},{8,7},{9,8},{10,9},{11,1... | collective-permute-start | bytes 1544 | tf_op jit(solution)/shard_map/ppermute | solution.py:30
  30.6 11.9 %collective-permute-start.22 = (f32[2,16,4]{2,1,0:T(8,128)S(1)}, f32[2,16,4]{2,1,0:T(8,128)}, u32[]{:S(2)}, u32[]{:S(2)}) collective-permute-start(f32[2,16,4]{2,1,0:T(8,128)S(1)} %get-tuple-element.273), channel_id=1, source_target_pairs={{0,1},{1,2},{2,3},{3,4},{4,5},{5,6},{6,7},{7,8},{8,9},{9,10},{10,1... | collective-permute-start | bytes 1544 | tf_op jit(solution)/shard_map/ppermute | solution.py:28
  33.3 10.0 %collective-permute-start.7 = (f32[3,48,8,2]{1,2,3,0:T(8,128)S(1)}, f32[3,48,8,2]{1,2,3,0:T(8,128)S(1)}, u32[]{:S(2)}, u32[]{:S(2)}) collective-permute-start(f32[3,48,8,2]{1,2,3,0:T(8,128)S(1)} %copy.15), channel_id=1, source_target_pairs={{1,0},{2,1},{3,2},{4,3},{5,4},{6,5},{7,6},{8,7},{9,8},{10,9},{11,1... | collective-permute-start | bytes 27656 | tf_op jit(solution)/shard_map/ppermute | solution.py:46
  56.1 25.8 %collective-permute-start.10 = (f32[3,48,2,256]{3,2,1,0:T(2,128)}, f32[3,48,2,256]{3,2,1,0:T(2,128)S(1)}, u32[]{:S(2)}, u32[]{:S(2)}) collective-permute-start(f32[3,48,2,256]{3,2,1,0:T(2,128)} %get-tuple-element.264), channel_id=1, source_target_pairs={{16,0},{32,16},{48,32},{64,48},{80,64},{96,80},{112,96},{128,112},... | collective-permute-start | bytes 884744 | tf_op jit(solution)/shard_map/ppermute | solution.py:46
  59.0 23.0 %collective-permute-start.9 = (f32[3,48,2,256]{3,2,1,0:T(2,128)}, f32[3,48,2,256]{3,2,1,0:T(2,128)}, u32[]{:S(2)}, u32[]{:S(2)}) collective-permute-start(f32[3,48,2,256]{3,2,1,0:T(2,128)} %get-tuple-element.263), channel_id=1, source_target_pairs={{0,16},{16,32},{32,48},{48,64},{64,80},{80,96},{96,112},{112,128},... | collective-permute-start | bytes 884744 | tf_op jit(solution)/shard_map/ppermute | solution.py:45
  91.9 25.8 %collective-permute-start.14 = (f32[3,48,2,256]{3,2,1,0:T(2,128)}, f32[3,48,2,256]{3,2,1,0:T(2,128)S(1)}, u32[]{:S(2)}, u32[]{:S(2)}) collective-permute-start(f32[3,48,2,256]{3,2,1,0:T(2,128)} %get-tuple-element.260), channel_id=1, source_target_pairs={{16,0},{32,16},{48,32},{64,48},{80,64},{96,80},{112,96},{128,112},... | collective-permute-start | bytes 884744 | tf_op jit(solution)/shard_map/ppermute | solution.py:46
  95.0 22.6 %collective-permute-start.13 = (f32[3,48,2,256]{3,2,1,0:T(2,128)}, f32[3,48,2,256]{3,2,1,0:T(2,128)}, u32[]{:S(2)}, u32[]{:S(2)}) collective-permute-start(f32[3,48,2,256]{3,2,1,0:T(2,128)} %get-tuple-element.259), channel_id=1, source_target_pairs={{0,16},{16,32},{32,48},{48,64},{64,80},{80,96},{96,112},{112,128},... | collective-permute-start | bytes 884744 | tf_op jit(solution)/shard_map/ppermute | solution.py:45
  108.3 7.6 %collective-permute-start.12 = (f32[3,48,8,2]{1,2,3,0:T(8,128)}, f32[3,48,8,2]{1,2,3,0:T(8,128)}, u32[]{:S(2)}, u32[]{:S(2)}) collective-permute-start(f32[3,48,8,2]{1,2,3,0:T(8,128)} %copy.21), channel_id=1, source_target_pairs={{0,1},{1,2},{2,3},{3,4},{4,5},{5,6},{6,7},{7,8},{8,9},{9,10},{10,1... | collective-permute-start | bytes 27656 | tf_op jit(solution)/shard_map/ppermute | solution.py:45
  127.7 18.3 %collective-permute-start.16 = (f32[2,1,256]{2,1,0:T(1,128)S(1)}, f32[2,1,256]{2,1,0:T(1,128)S(1)}, u32[]{:S(2)}, u32[]{:S(2)}) collective-permute-start(f32[2,1,256]{2,1,0:T(1,128)S(1)} %get-tuple-element.278), channel_id=1, source_target_pairs={{16,0},{32,16},{48,32},{64,48},{80,64},{96,80},{112,96},{128,112},... | collective-permute-start | bytes 6152 | tf_op jit(solution)/shard_map/ppermute | solution.py:46
  131.8 14.2 %collective-permute-start.17 = (f32[2,1,256]{2,1,0:T(1,128)S(1)}, f32[2,1,256]{2,1,0:T(1,128)S(1)}, u32[]{:S(2)}, u32[]{:S(2)}) collective-permute-start(f32[2,1,256]{2,1,0:T(1,128)S(1)} %get-tuple-element.277), channel_id=1, source_target_pairs={{0,16},{16,32},{32,48},{48,64},{64,80},{80,96},{96,112},{112,128},... | collective-permute-start | bytes 6152 | tf_op jit(solution)/shard_map/ppermute | solution.py:45
  137.3 8.0 %collective-permute-start.19 = (f32[2,8,1]{2,1,0:T(8,128)S(1)}, f32[2,8,1]{2,1,0:T(8,128)S(1)}, u32[]{:S(2)}, u32[]{:S(2)}) collective-permute-start(f32[2,8,1]{2,1,0:T(8,128)S(1)} %get-tuple-element.276), channel_id=1, source_target_pairs={{0,1},{1,2},{2,3},{3,4},{4,5},{5,6},{6,7},{7,8},{8,9},{9,10},{10,1... | collective-permute-start | bytes 200 | tf_op jit(solution)/shard_map/ppermute | solution.py:45
  146.2 9.5 %collective-permute-start = (f32[2,4,256]{2,1,0:T(4,128)S(1)}, f32[2,4,256]{2,1,0:T(4,128)S(1)}, u32[]{:S(2)}, u32[]{:S(2)}) collective-permute-start(f32[2,4,256]{2,1,0:T(4,128)S(1)} %get-tuple-element.351), channel_id=1, source_target_pairs={{16,0},{32,16},{48,32},{64,48},{80,64},{96,80},{112,96},{128,112},... | collective-permute-start | bytes 24584 | tf_op jit(solution)/shard_map/while/body/eval_jaxpr/ppermute | solution.py:30
  150.9 8.0 %collective-permute-start.1 = (f32[2,4,256]{2,1,0:T(4,128)S(1)}, f32[2,4,256]{2,1,0:T(4,128)S(1)}, u32[]{:S(2)}, u32[]{:S(2)}) collective-permute-start(f32[2,4,256]{2,1,0:T(4,128)S(1)} %get-tuple-element.352), channel_id=1, source_target_pairs={{0,16},{16,32},{32,48},{48,64},{64,80},{80,96},{96,112},{112,128},... | collective-permute-start | bytes 24584 | tf_op jit(solution)/shard_map/while/body/eval_jaxpr/ppermute | solution.py:28
  158.9 8.9 %collective-permute-start.2 = (f32[2,16,4]{2,1,0:T(8,128)S(1)}, f32[2,16,4]{2,1,0:T(8,128)S(1)}, u32[]{:S(2)}, u32[]{:S(2)}) collective-permute-start(f32[2,16,4]{2,1,0:T(8,128)S(1)} %get-tuple-element.353), channel_id=1, source_target_pairs={{1,0},{2,1},{3,2},{4,3},{5,4},{6,5},{7,6},{8,7},{9,8},{10,9},{11,1... | collective-permute-start | bytes 1544 | tf_op jit(solution)/shard_map/while/body/eval_jaxpr/ppermute | solution.py:30
  178.1 12.5 %collective-permute-start = (f32[2,4,256]{2,1,0:T(4,128)S(1)}, f32[2,4,256]{2,1,0:T(4,128)S(1)}, u32[]{:S(2)}, u32[]{:S(2)}) collective-permute-start(f32[2,4,256]{2,1,0:T(4,128)S(1)} %get-tuple-element.351), channel_id=1, source_target_pairs={{16,0},{32,16},{48,32},{64,48},{80,64},{96,80},{112,96},{128,112},... | collective-permute-start | bytes 24584 | tf_op jit(solution)/shard_map/while/body/eval_jaxpr/ppermute | solution.py:30
  206.7 11.7 %collective-permute-start = (f32[2,4,256]{2,1,0:T(4,128)S(1)}, f32[2,4,256]{2,1,0:T(4,128)S(1)}, u32[]{:S(2)}, u32[]{:S(2)}) collective-permute-start(f32[2,4,256]{2,1,0:T(4,128)S(1)} %get-tuple-element.351), channel_id=1, source_target_pairs={{16,0},{32,16},{48,32},{64,48},{80,64},{96,80},{112,96},{128,112},... | collective-permute-start | bytes 24584 | tf_op jit(solution)/shard_map/while/body/eval_jaxpr/ppermute | solution.py:30
  234.4 11.7 %collective-permute-start = (f32[2,4,256]{2,1,0:T(4,128)S(1)}, f32[2,4,256]{2,1,0:T(4,128)S(1)}, u32[]{:S(2)}, u32[]{:S(2)}) collective-permute-start(f32[2,4,256]{2,1,0:T(4,128)S(1)} %get-tuple-element.351), channel_id=1, source_target_pairs={{16,0},{32,16},{48,32},{64,48},{80,64},{96,80},{112,96},{128,112},... | collective-permute-start | bytes 24584 | tf_op jit(solution)/shard_map/while/body/eval_jaxpr/ppermute | solution.py:30
  262.2 20.5 %collective-permute-start.24 = (f32[1,256]{1,0:T(1,128)S(1)}, f32[1,256]{1,0:T(1,128)S(1)}, u32[]{:S(2)}, u32[]{:S(2)}) collective-permute-start(f32[1,256]{1,0:T(1,128)S(1)} %get-tuple-element.285), channel_id=1, source_target_pairs={{16,0},{32,16},{48,32},{64,48},{80,64},{96,80},{112,96},{128,112},... | collective-permute-start | bytes 3080 | tf_op jit(solution)/shard_map/ppermute | solution.py:46
  272.0 10.7 %collective-permute-start.25 = (f32[1,256]{1,0:T(1,128)S(1)}, f32[1,256]{1,0:T(1,128)S(1)}, u32[]{:S(2)}, u32[]{:S(2)}) collective-permute-start(f32[1,256]{1,0:T(1,128)S(1)} %get-tuple-element.286), channel_id=1, source_target_pairs={{0,16},{16,32},{32,48},{48,64},{64,80},{80,96},{96,112},{112,128},... | collective-permute-start | bytes 3080 | tf_op jit(solution)/shard_map/ppermute | solution.py:45
  274.0 8.0 %collective-permute-start.27 = (f32[8,1]{1,0:T(8,128)S(1)}, f32[8,1]{1,0:T(8,128)S(1)}, u32[]{:S(2)}, u32[]{:S(2)}) collective-permute-start(f32[8,1]{1,0:T(8,128)S(1)} %get-tuple-element.284), channel_id=1, source_target_pairs={{0,1},{1,2},{2,3},{3,4},{4,5},{5,6},{6,7},{7,8},{8,9},{9,10},{10,1... | collective-permute-start | bytes 104 | tf_op jit(solution)/shard_map/ppermute | solution.py:45
  (35 other events, 332.6 us)
where the time goes:
time: 288 us; the launch traced here: 284 us
  starting transfers between devices  172 us (60%)
  other arithmetic  51.6 us (18%)
  waiting for transfers between devices  32.1 us (11%)
  local copies, waits for them, and re-layouts  26.7 us (9%)
    ppermute x10, starting transfers between devices, padded_2(): lax.ppermute(head, axis, [((i + 1) % count, i) for i in range(ends)])  54 us
    ppermute x10, starting transfers between devices, extended(): lax.ppermute(leading, axis, [(b, a) for a, b in up])  44.3 us
    ppermute x10, starting transfers between devices, extended(): lax.ppermute(last, axis, up)  40 us
    ppermute x10, starting transfers between devices, padded_2(): lax.ppermute(tail, axis, [(i, (i + 1) % count) for i in range(ends)])  33.2 us
    ppermute x10, waiting for transfers between devices, padded_2(): lax.ppermute(tail, axis, [(i, (i + 1) % count) for i in range(ends)])  20.3 us
    mul x17, other arithmetic, nine_point(): weighted = wet * field  16.6 us
    another operation x9, other arithmetic, tendency(): return jnp.stack([east_rate, north_rate, salt_rate])  11.3 us
    concatenate x3, other arithmetic, extended(): jnp.concatenate([jnp.pad(low, around), array, jnp.pad(high, around)], axi...  9.94 us
  transfers between devices with their start and end apart: 40, of which 14 were waited for; matrix products, arithmetic and copies ran while one was open for 9% of the time, Pallas kernels for 0%

commit v1 on v0

v1 whole, which is shorter than its diff:
```python
import functools

import jax
import jax.numpy as jnp
from jax import lax
from jax.experimental import pallas as pl
from jax.experimental.pallas import tpu as pltpu
from jax.sharding import PartitionSpec as P

ITERS = 16
TIME_STEP = 0.2
CORIOLIS = 0.3
PRESS_COEF = 0.05
VISCOSITY = 0.1
DIFFUSIVITY = 0.1
SIGMA_SHIFT = 0.25
CHEB_CENTER = 3.625
CHEB_HALF = 3.375
DIVERGENCE_COEF = 8.0

LEV = 48
ROWS = 8
COLS = 256
EXT = 128
WIDE = COLS + EXT
HALO = 6
CHUNKS = 1
F32 = jnp.float32


def cheb_table(count):
    first = CHEB_CENTER / CHEB_HALF
    ratio = 1.0 / first
    keeps = []
    gains = []
    for index in range(count):
        ratio_next = 1.0 / (2.0 * first - ratio)
        keeps.append(ratio_next * ratio)
        gains.append(2.0 * ratio_next / CHEB_HALF)
        ratio = ratio_next
    return (keeps, gains)


def lanes(shape):
    return lax.broadcasted_iota(jnp.int32, shape, len(shape) - 1)


def pack_kernel(sc, u, v, s, wet, act, surf, depth, st, *outs):
    core = sc[1]
    north_odd = sc[2]
    mains = outs[:CHUNKS]
    edge_a, edge_b = outs[CHUNKS:]
    levels = LEV // CHUNKS
    count = (act[...] * wet[...]).astype(F32)
    for f, ref in enumerate((u, v, s)):
        for lev in range(LEV):
            tile = jnp.where(count > lev, ref[lev], 0.0)
            for h in range(2):
                st[f, h, pl.ds(lev, ROWS, stride=LEV), :] = tile[:, h * 128 : (h + 1) * 128]
    base = 2 * core
    for f in range(3):
        for j in range(HALO):
            for c in range(CHUNKS):
                for h in range(2):
                    start = pl.multiple_of((base + j) * LEV + c * levels, 8)
                    mains[c][f, h, j * levels : (j + 1) * levels, :] = st[f, h, pl.ds(start, levels), :]
    lane = lanes((LEV, 128)) // 32
    odd = jnp.full((LEV, 128), north_odd, jnp.int32) == 1
    for f in range(3):
        for g in range(2):
            left = jnp.zeros((LEV, 128), F32)
            right = jnp.zeros((LEV, 128), F32)
            for q in range(4):
                at = (4 * g + q) * LEV
                low = st[f, 0, at : at + LEV, :]
                high = st[f, 1, at : at + LEV, :]
                low = low if q == 0 else pltpu.roll(low, 32 * q, 1)
                high = high if q == 3 else pltpu.roll(high, 32 * q + 32, 1)
                left = jnp.where(lane == q, low, left)
                right = jnp.where(lane == q, high, right)
            at = (2 * f + g) * LEV
            edge_a[at : at + LEV, :] = jnp.where(odd, left, right)
            edge_b[at : at + LEV, :] = jnp.where(odd, right, left)
    flat = (surf[...], count, depth[...])
    lane = lanes((ROWS, 128)) // 32
    left = jnp.zeros((ROWS, 128), F32)
    right = jnp.zeros((ROWS, 128), F32)
    for q, field in enumerate(flat):
        low = field[:, :128]
        high = field[:, 128:]
        low = low if q == 0 else pltpu.roll(low, 32 * q, 1)
        high = high if q == 3 else pltpu.roll(high, 32 * q + 32, 1)
        left = jnp.where(lane == q, low, left)
        right = jnp.where(lane == q, high, right)
    odd = jnp.full((ROWS, 128), north_odd, jnp.int32) == 1
    edge_a[6 * LEV :, :] = jnp.where(odd, left, right)
    edge_b[6 * LEV :, :] = jnp.where(odd, right, left)


def ext_kernel(sc, edge_a, edge_b, wet, act, surf, depth, own, corner, flat):
    core = sc[1]
    north_odd = sc[2]

    def halves(at, size):
        a = edge_a[at : at + size, :]
        b = edge_b[at : at + size, :]
        odd = jnp.full((size, 128), north_odd, jnp.int32) == 1
        return jnp.where(odd, b, a), jnp.where(odd, a, b)

    def unpack(high, low, q):
        lane = lanes(high.shape)
        high = high if q == 0 else pltpu.roll(high, 128 - 32 * q, 1)
        low = low if q == 3 else pltpu.roll(low, 96 - 32 * q, 1)
        return jnp.where(lane < 32, high, jnp.where(lane >= 96, low, 0.0))

    for f in range(3):
        for g in range(2):
            high, low = halves((2 * f + g) * LEV, LEV)
            for q in range(4):
                at = (8 * f + 4 * g + q) * LEV
                own[at : at + LEV, :] = unpack(high, low, q)
    high, low = halves(6 * LEV, ROWS)
    count = (act[...] * wet[...]).astype(F32)
    counts = (count[:, :128], count[:, 128:], unpack(high, low, 1))
    for h in range(3):
        own[24 * LEV + 8 * h : 24 * LEV + 8 * h + 8, :] = counts[h]
        corner[9 * LEV + 8 * h : 9 * LEV + 8 * h + 8, :] = counts[h]
    flat[0, :, :COLS] = surf[...]
    flat[0, :, COLS:] = unpack(high, low, 0)
    flat[1, :, :COLS] = count
    flat[1, :, COLS:] = counts[2]
    flat[2, :, :COLS] = depth[...]
    flat[2, :, COLS:] = unpack(high, low, 2)
    lane = lanes((LEV, 128))
    inner = (lane >= 32) & (lane < 96)
    for f in range(3):
        for j in range(3):
            start = pl.multiple_of((8 * f + 2 * core + 2 * j) * LEV, 8)
            first = own[pl.ds(start, LEV), :]
            second = own[pl.ds(start + LEV, LEV), :]
            at = (3 * f + j) * LEV
            corner[at : at + LEV, :] = jnp.where(inner, pltpu.roll(second, 64, 1), first)


def shifts(q):
    return (
        pltpu.roll(q, WIDE - 1, 1),
        pltpu.roll(q, 1, 1),
        pltpu.roll(q, WIDE - 2, 1),
        pltpu.roll(q, 2, 1),
    )


def slope(ahead, behind, ahead2, behind2):
    return (8.0 / 12.0) * (ahead - behind) - (1.0 / 12.0) * (ahead2 - behind2)


def running(x, sub):
    for step in (1, 2, 4):
        x = x + jnp.where(sub >= step, pltpu.roll(x, step, 0), 0.0)
    return x


def rk_kernel(chunk, sc, st, stp, own, ownp, main, corner, flat, *rest):
    levels = LEV // CHUNKS
    if chunk:
        carry_in, sums_in = rest[:2]
        rest = rest[2:]
    out, carry, sums, flows, ext, one, two, counts = rest
    core = sc[1]
    lev0 = chunk * levels
    for f in range(3):
        for r in range(ROWS):
            for h in range(2):
                ext[f, HALO + r, :, h * 128 : (h + 1) * 128] = st[f, h, r * LEV + lev0 : r * LEV + lev0 + levels, :]
            at = (8 * f + r) * LEV + lev0
            ext[f, HALO + r, :, COLS:] = own[at : at + levels, :]
        for j in range(HALO):
            row = 14 * (1 - core) + j
            start = pl.multiple_of((2 * core + j) * LEV + lev0, 8)
            for h in range(2):
                ext[f, row, :, h * 128 : (h + 1) * 128] = stp[f, h, pl.ds(start, levels), :]
            ext[f, row, :, COLS:] = ownp[pl.ds(pl.multiple_of(start + 8 * f * LEV, 8), levels), :]
            row = 14 * core + j
            for h in range(2):
                ext[f, row, :, h * 128 : (h + 1) * 128] = main[f, h, j * levels : (j + 1) * levels, :]
        lane = lanes((levels, 128))
        outer = (lane < 32) | (lane >= 96)
        for j in range(3):
            at = (3 * f + j) * LEV + lev0
            pair = corner[at : at + levels, :]
            row = 14 * core + 2 * j
            ext[f, row, :, COLS:] = jnp.where(outer, pair, 0.0)
            ext[f, row + 1, :, COLS:] = jnp.where(outer, pltpu.roll(pair, 64, 1), 0.0)
    for h in range(3):
        tile = own[24 * LEV + 8 * h : 24 * LEV + 8 * h + 8, :]
        for r in range(ROWS):
            counts[HALO + r, :, h * 128 : (h + 1) * 128] = jnp.broadcast_to(tile[r : r + 1, :], (8, 128))
        for j in range(HALO):
            line = ownp[pl.ds(24 * LEV + 8 * h + 2 * core + j, 1), :]
            counts[14 * (1 - core) + j, :, h * 128 : (h + 1) * 128] = jnp.broadcast_to(line, (8, 128))
            line = corner[pl.ds(9 * LEV + 8 * h + 2 * (1 - core) + j, 1), :]
            counts[14 * core + j, :, h * 128 : (h + 1) * 128] = jnp.broadcast_to(line, (8, 128))

    sub = lax.broadcasted_iota(jnp.int32, (8, WIDE), 0)

    def stage(source, rows, inset, write, slot):
        def row(o, _):
            count = counts[o + inset]
            if chunk:
                sum_x = carry_in[slot + 2 * o]
                sum_y = carry_in[slot + 2 * o + 1]
            else:
                sum_x = jnp.zeros((8, WIDE), F32)
                sum_y = jnp.zeros((8, WIDE), F32)
            for t in range(levels // 8):
                here = slice(8 * t, 8 * t + 8)
                mid = []
                dxs = []
                dys = []
                laps = []
                for f in range(3):
                    q = source[f, o + 2, here, :]
                    back2, back = source[f, o, here, :], source[f, o + 1, here, :]
                    fore, fore2 = source[f, o + 3, here, :], source[f, o + 4, here, :]
                    right, left, right2, left2 = shifts(q)
                    mid.append(q)
                    dxs.append(slope(fore, back, fore2, back2))
                    dys.append(slope(right, left, right2, left2))
                    laps.append((fore + back) + (right + left) - 4.0 * q)
                press_x = running(dxs[2], sub) + sum_x
                press_y = running(dys[2], sub) + sum_y
                sum_x = jnp.broadcast_to(press_x[7:8, :], (8, WIDE))
                sum_y = jnp.broadcast_to(press_y[7:8, :], (8, WIDE))
                u, v, _s = mid
                rates = [VISCOSITY * laps[f] - (u * dxs[f] + v * dys[f]) for f in range(3)]
                rates[0] = rates[0] + (CORIOLIS * v - PRESS_COEF * press_x)
                rates[1] = rates[1] - (CORIOLIS * u + PRESS_COEF * press_y)
                keep = count > (sub + (lev0 + 8 * t)).astype(F32)
                write(o, here, t, mid, [jnp.where(keep, r, 0.0) for r in rates])
            carry[slot + 2 * o] = sum_x
            carry[slot + 2 * o + 1] = sum_y
            return 0

        lax.fori_loop(0, rows, row, 0)

    def write1(o, here, t, mid, rates):
        for f in range(3):
            one[f, o, here, :] = mid[f] + TIME_STEP * rates[f]

    def write2(o, here, t, mid, rates):
        for f in range(3):
            first = ext[f, o + 4, here, :]
            two[f, o, here, :] = 0.75 * first + (0.25 * mid[f] + (0.25 * TIME_STEP) * rates[f])

    def write3(o, here, t, mid, rates):
        for f in range(3):
            first = ext[f, o + 6, here, :]
            value = (1.0 / 3.0) * first + ((2.0 / 3.0) * mid[f] + (2.0 / 3.0 * TIME_STEP) * rates[f])
            at = pl.multiple_of(o * levels + 8 * t, 8)
            for h in range(2):
                out[f, h, pl.ds(at, 8), :] = value[:, h * 128 : (h + 1) * 128]
            if f < 2:
                if t == 0:
                    sums[f, o] = value + sums_in[f, o] if chunk else value
                else:
                    sums[f, o] = sums[f, o] + value

    stage(ext, 16, 2, write1, 0)
    stage(one, 12, 4, write2, 32)
    stage(two, 8, 6, write3, 56)
    for f in range(2):
        for o in range(ROWS):
            flows[f, o : o + 1, :] = jnp.sum(sums[f, o], axis=0, keepdims=True)
        flows[f] = flat[2] * (flows[f] * (1.0 / LEV))
        flows[2 + f] = flat[f]


def solve_kernel(peers, sc, table, flat, *rest):
    states = rest[:CHUNKS]
    east, north, salt, level = rest[CHUNKS : CHUNKS + 4]
    wide = rest[CHUNKS + 4]
    levels = LEV // CHUNKS
    me = sc[0]
    for k in range(-3, 4):
        peer = me + k
        inside = (peer >= 0) & (peer < peers)
        factor = jnp.where(inside, 1.0, 0.0).astype(F32)
        block = table[jnp.clip(peer, 0, peers - 1)]
        wide[:, 8 * (k + 3) : 8 * (k + 3) + 8, :] = block * factor
    high = 56

    def up(x):
        return pltpu.roll(x, high - 1, 0)

    def down(x):
        return pltpu.roll(x, 1, 0)

    def right(x):
        return pltpu.roll(x, WIDE - 1, 1)

    def left(x):
        return pltpu.roll(x, 1, 1)

    wet = jnp.where(wide[3] > 0.0, 1.0, 0.0)
    dry = 1.0 - wet

    def apply(e):
        w = wet * e
        rows = up(w) + down(w)
        mix = 4.0 * w + rows
        sides = right(mix) + left(mix)
        stencil = (20.0 / 6.0) * w - (4.0 / 6.0) * rows - (1.0 / 6.0) * sides
        return wet * (SIGMA_SHIFT * e + stencil) + dry * e

    flow_east = wide[0]
    flow_north = wide[1]
    x = wide[2]
    div = 0.5 * (up(flow_east) - down(flow_east)) + 0.5 * (right(flow_north) - left(flow_north))
    res = wet * (SIGMA_SHIFT * x - DIVERGENCE_COEF * div) - apply(x)
    step = res * (1.0 / CHEB_CENTER)
    keeps, gains = cheb_table(ITERS)
    for index in range(ITERS):
        x = x + step
        if index < ITERS - 1:
            res = res - apply(step)
            step = keeps[index] * step + gains[index] * res
    slope_east = (0.5 * (up(x) - down(x)))[24:32, :COLS]
    slope_north = (0.5 * (right(x) - left(x)))[24:32, :COLS]
    level[...] = x[24:32, :COLS]
    count = flat[1][:, :COLS]
    for lev in range(LEV):
        c, at = divmod(lev, levels)
        keep = count > lev
        for h in range(2):
            cols = slice(h * 128, (h + 1) * 128)
            parts = [states[c][f, h, pl.ds(at, ROWS, stride=levels), :] for f in range(3)]
            east[lev, :, cols] = jnp.where(keep[:, cols], parts[0] - slope_east[:, cols], 0.0)
            north[lev, :, cols] = jnp.where(keep[:, cols], parts[1] - slope_north[:, cols], 0.0)
            salt[lev, :, cols] = parts[2]


def swap(pairs):
    return [p for a, b in pairs for p in ((a, b), (b, a))]


def call(body, outs, scratch=(), ins=0):
    vmem = pl.BlockSpec(memory_space=pltpu.VMEM)
    smem = pl.BlockSpec(memory_space=pltpu.SMEM)
    return pl.pallas_call(
        body,
        out_shape=[jax.ShapeDtypeStruct(s, F32) for s in outs],
        in_specs=[smem] + [vmem] * ins,
        out_specs=[vmem] * len(outs),
        scratch_shapes=[pltpu.VMEM(s, F32) for s in scratch],
        compiler_params=pltpu.CompilerParams(vmem_limit_bytes=48 * 1024 * 1024),
    )


def local(u, v, s, surface, depth, wet, active):
    gx = lax.axis_size("gx")
    gy = lax.axis_size("gy")
    levels = LEV // CHUNKS
    me = lax.axis_index("gx")
    scalars = jnp.stack([me, me % 2, lax.axis_index("gy") % 2]).astype(jnp.int32)
    on_chip = swap([(i, i + 1) for i in range(0, gx, 2)])
    next_chip = swap([(i, i + 1) for i in range(1, gx - 1, 2)])
    even = swap([(i, i + 1) for i in range(0, gy, 2)])
    odd = swap([(i, i + 1) for i in range(1, gy - 1, 2)])

    st, *packed = call(
        pack_kernel,
        [(3, 2, ROWS * LEV, 128)]
        + [(3, 2, HALO * levels, 128)] * CHUNKS
        + [(6 * LEV + 8, 128)] * 2,
        ins=7,
    )(scalars, u, v, s, wet, active, surface, depth)
    mains = packed[:CHUNKS]
    edge_a = lax.ppermute(packed[CHUNKS], "gy", even)
    edge_b = lax.ppermute(packed[CHUNKS + 1], "gy", odd)
    mains = [lax.ppermute(m, "gx", next_chip) for m in mains]
    stp = lax.ppermute(st, "gx", on_chip)
    own, corner, flat = call(
        ext_kernel,
        [(24 * LEV + 24, 128), (9 * LEV + 24, 128), (3, ROWS, WIDE)],
        ins=6,
    )(scalars, edge_a, edge_b, wet, active, surface, depth)
    corner = lax.ppermute(corner, "gx", next_chip)
    ownp = lax.ppermute(own, "gx", on_chip)

    states = []
    tail = []
    for c in range(CHUNKS):
        out, carry, sums, flows = call(
            functools.partial(rk_kernel, c),
            [(3, 2, ROWS * levels, 128), (72, 8, WIDE), (2, ROWS, 8, WIDE), (4, ROWS, WIDE)],
            [(3, 20, levels, WIDE), (3, 16, levels, WIDE), (3, 12, levels, WIDE), (20, 8, WIDE)],
            ins=7 + len(tail),
        )(scalars, st, stp, own, ownp, mains[c], corner, flat, *tail)
        tail = [carry, sums]
        states.append(out)
    table = lax.all_to_all(jnp.broadcast_to(flows[None], (gx,) + flows.shape), "gx", 0, 0)
    east, north, salt, level = call(
        functools.partial(solve_kernel, gx),
        [(LEV, ROWS, COLS)] * 3 + [(ROWS, COLS)],
        [(4, 56, WIDE)],
        ins=2 + CHUNKS,
    )(scalars, table, flat, *states)
    return east, north, salt, level


def solution(mesh):
    cube = P(None, "gx", "gy")
    flat = P("gx", "gy")
    return jax.shard_map(
        local,
        mesh=mesh,
        in_specs=(cube, cube, cube, flat, flat, flat, flat),
        out_specs=(cube, cube, cube, flat),
        check_vma=False,
    )
```

time: 288 us -> 131 us (0.45)
  the two profiles are of different devices: /device:TPU:31 before, /device:TPU:56 now
where the time goes in v1:
time: 131 us; the launch traced here: 130 us
  blocking collectives  67 us (51%)
  Pallas kernels  21.1 us (16%)
  starting transfers between devices  18.3 us (14%)
  waiting for transfers between devices  16.4 us (13%)
  local copies, waits for them, and re-layouts  6.9 us (5%)
    all_to_all x1, blocking collectives, local(): lax.all_to_all(jnp.broadcast_to(flows[None], (gx,) + flows.shape), 'gx',...  67 us
    ppermute x1, waiting for transfers between devices, local(): edge_b = lax.ppermute(packed[CHUNKS + 1], 'gy', odd)  15.4 us
    pallas_call x1, Pallas kernels, local(): call(functools.partial(rk_kernel, c), [(3, 2, ROWS * levels, 128), (72, 8...  15 us
    ppermute x1, starting transfers between devices, local(): ownp = lax.ppermute(own, 'gx', on_chip)  11 us
    unnamed x18, local copies, waits for them, and re-layouts  6.82 us
    ppermute x1, starting transfers between devices, local(): edge_b = lax.ppermute(packed[CHUNKS + 1], 'gy', odd)  5.62 us
    pallas_call x1, Pallas kernels, local(): call(functools.partial(solve_kernel, gx), [(LEV, ROWS, COLS)] * 3 + [(ROW...  3.94 us
  transfers between devices with their start and end apart: 6, of which 2 were waited for; matrix products, arithmetic and copies ran while one was open for 0% of the time, Pallas kernels for 1%

profile of v1, /device:TPU:56, one launch (start us, length us, event | category | flops | bytes accessed | tf_op | source)
XLA Modules:
  0.0 130.5 jit_solution(13468259720766974982)
XLA Ops:
  0.6 0.0 copy-start.7
  0.7 0.1 pad_add_fusion.sc
  0.7 1.0 copy-done
  1.7 1.0 copy-done.1
  2.7 1.0 copy-done.2
  3.7 0.7 copy-done.3
  4.4 0.7 copy-done.4
  5.1 0.7 copy-done.5
  5.8 0.7 copy-done.6
  6.5 1.2 shard_map.102
  7.7 0.1 collective-permute-start
  7.8 0.7 collective-permute-start.4
  8.6 0.2 collective-permute-start.1
  8.7 5.6 %collective-permute-start.2 = (f32[296,128]{1,0:T(8,128)S(1)}, f32[296,128]{1,0:T(8,128)S(1)}, u32[]{:S(2)}, u32[]{:S(2)}) collective-permute-start(f32[296,128]{1,0:T(8,128)S(1)} %get-tuple-element.15), channel_id=1, source_target_pairs={{1,2},{2,1},{3,4},{4,3},{5,6},{6,5},{7,8},{8,7},{9,10},{10,9},{11,... | collective-permute-start | bytes 454664 | tf_op jit(solution)/shard_map/ppermute | solution.py:380
  14.4 15.4 %collective-permute-done.2.edge_b = f32[296,128]{1,0:T(8,128)S(1)} collective-permute-done((f32[296,128]{1,0:T(8,128)S(1)}, f32[296,128]{1,0:T(8,128)S(1)}, u32[]{:S(2)}, u32[]{:S(2)}) %collective-permute-start.2) | collective-permute-done | bytes 151584 | tf_op jit(solution)/shard_map/ppermute | solution.py:380
  29.8 1.0 shard_map.103
  30.8 11.0 %collective-permute-start.3 = (f32[1176,128]{1,0:T(8,128)S(1)}, f32[1176,128]{1,0:T(8,128)S(1)}, u32[]{:S(2)}, u32[]{:S(2)}) collective-permute-start(f32[1176,128]{1,0:T(8,128)S(1)} %get-tuple-element.16.own), channel_id=1, source_target_pairs={{0,16},{16,0},{32,48},{48,32},{64,80},{80,64},{96,112},{112,96},{1... | collective-permute-start | bytes 1806344 | tf_op jit(solution)/shard_map/ppermute | solution.py:389
  41.8 0.7 collective-permute-start.5
  42.5 1.0 collective-permute-done.3.ownp
  43.5 1.0 copy-done.8
  44.5 15.0 %shard_map.104 = (f32[3,2,384,128]{3,2,1,0:T(8,128)S(1)}, f32[72,8,384]{2,1,0:T(8,128)}, f32[2,8,8,384]{3,2,1,0:T(8,128)}, f32[4,8,384]{2,1,0:T(8,128)S(1)}) custom-call(s32[3]{0:T(128)S(1)} %pad_add_fusion.sc, f32[3,2,384,128]{3,2,1,0:T(8,128)S(1)} %get-tuple-element.13.st, f32[3,2,384,128]{3,2,1,0:T(8,128)} %copy-done.8, ...), custom_call_target="tpu_custom_call" | custom-call | tf_op jit(solution)/shard_map/pallas_call | solution.py:394
  59.5 0.1 broadcast_in_dim.2
  59.5 67.0 %all_to_all.5.table = f32[16,4,8,384]{3,2,1,0:T(8,128)S(1)} all-to-all(f32[16,4,8,384]{3,2,1,0:T(8,128)S(1)} %broadcast_in_dim.2), channel_id=1, replica_groups=mesh['gx'=16,'gy'=16] {'gx'}, dimensions={0} | all-to-all | bytes 1572864 | tf_op jit(solution)/shard_map/all_to_all | solution.py:402
  126.6 3.9 %shard_map.105 = (f32[48,8,256]{2,1,0:T(8,128)}, f32[48,8,256]{2,1,0:T(8,128)}, f32[48,8,256]{2,1,0:T(8,128)}, f32[8,256]{1,0:T(8,128)}) custom-call(s32[3]{0:T(128)S(1)} %pad_add_fusion.sc, f32[16,4,8,384]{3,2,1,0:T(8,128)S(1)} %all_to_all.5.table, f32[3,8,384]{2,1,0:T(8,128)S(1)} %get-tuple-element.19.flat, f32[3,2,384,128]{3,2,1,0:T(8,128)S(1)} %get-tuple-element.21.rest_0_), custom_call_target="tpu_custom_call" | custom-call | tf_op jit(solution)/shard_map/pallas_call | solution.py:403
  (13 shorter events, 0.0 us)
Async XLA Ops:
  0.6 29.2 %copy-start.7 = (f32[8,256]{1,0:T(8,128)S(1)}, f32[8,256]{1,0:T(8,128)}, u32[]{:S(2)}) copy-start(f32[8,256]{1,0:T(8,128)} %depth.3) | copy-start | bytes 24580
  0.7 1.0 copy-start
  1.7 1.0 copy-start.1
  2.7 1.0 copy-start.2
  3.7 0.7 copy-start.3
  4.4 0.7 copy-start.4
  5.1 0.7 copy-start.5
  5.8 0.7 copy-start.6
  7.7 35.7 %collective-permute-start = (f32[3,2,384,128]{3,2,1,0:T(8,128)S(1)}, f32[3,2,384,128]{3,2,1,0:T(8,128)S(1)}, u32[]{:S(2)}, u32[]{:S(2)}) collective-permute-start(f32[3,2,384,128]{3,2,1,0:T(8,128)S(1)} %get-tuple-element.13.st), channel_id=1, source_target_pairs={{0,16},{16,0},{32,48},{48,32},{64,80},{80,64},{96,112},{112,96},{1... | collective-permute-start | bytes 3538952 | tf_op jit(solution)/shard_map/ppermute | solution.py:382
  7.8 35.6 %collective-permute-start.4 = (f32[3,2,288,128]{3,2,1,0:T(8,128)S(1)}, f32[3,2,288,128]{3,2,1,0:T(8,128)S(1)}, u32[]{:S(2)}, u32[]{:S(2)}) collective-permute-start(f32[3,2,288,128]{3,2,1,0:T(8,128)S(1)} %get-tuple-element.17), channel_id=1, source_target_pairs={{16,32},{32,16},{48,64},{64,48},{80,96},{96,80},{112,128},{128,112... | collective-permute-start | bytes 2654216 | tf_op jit(solution)/shard_map/ppermute | solution.py:381
  8.6 5.8 %collective-permute-start.1 = (f32[296,128]{1,0:T(8,128)S(1)}, f32[296,128]{1,0:T(8,128)S(1)}, u32[]{:S(2)}, u32[]{:S(2)}) collective-permute-start(f32[296,128]{1,0:T(8,128)S(1)} %get-tuple-element.14), channel_id=1, source_target_pairs={{0,1},{1,0},{2,3},{3,2},{4,5},{5,4},{6,7},{7,6},{8,9},{9,8},{10,11... | collective-permute-start | bytes 454664 | tf_op jit(solution)/shard_map/ppermute | solution.py:379
  8.7 21.1 %collective-permute-start.2 = (f32[296,128]{1,0:T(8,128)S(1)}, f32[296,128]{1,0:T(8,128)S(1)}, u32[]{:S(2)}, u32[]{:S(2)}) collective-permute-start(f32[296,128]{1,0:T(8,128)S(1)} %get-tuple-element.15), channel_id=1, source_target_pairs={{1,2},{2,1},{3,4},{4,3},{5,6},{6,5},{7,8},{8,7},{9,10},{10,9},{11,... | collective-permute-start | bytes 454664 | tf_op jit(solution)/shard_map/ppermute | solution.py:380
  30.8 12.7 %collective-permute-start.3 = (f32[1176,128]{1,0:T(8,128)S(1)}, f32[1176,128]{1,0:T(8,128)S(1)}, u32[]{:S(2)}, u32[]{:S(2)}) collective-permute-start(f32[1176,128]{1,0:T(8,128)S(1)} %get-tuple-element.16.own), channel_id=1, source_target_pairs={{0,16},{16,0},{32,48},{48,32},{64,80},{80,64},{96,112},{112,96},{1... | collective-permute-start | bytes 1806344 | tf_op jit(solution)/shard_map/ppermute | solution.py:389
  41.8 0.7 collective-permute-start.5
  43.5 1.0 copy-start.8

commit v2 on v1

--- a/solution.py
+++ b/solution.py
@@ -24,7 +24,9 @@
 EXT = 128
 WIDE = COLS + EXT
 HALO = 6
-CHUNKS = 1
+SIZES = (24, 16, 8)
+CHUNKS = len(SIZES)
+STARTS = tuple(sum(SIZES[:c]) for c in range(CHUNKS))
 F32 = jnp.float32
 
 
@@ -45,24 +47,37 @@
     return lax.broadcasted_iota(jnp.int32, shape, len(shape) - 1)
 
 
-def pack_kernel(sc, u, v, s, wet, act, surf, depth, st, *outs):
+def pack_kernel(sc, u, v, s, wet, act, surf, depth, edge_a, edge_b, *rest):
+    mains = rest[:CHUNKS]
+    st, plane = rest[CHUNKS : CHUNKS + 2]
+    buffers = rest[CHUNKS + 2 : CHUNKS + 9]
+    sems = rest[CHUNKS + 9]
     core = sc[1]
     north_odd = sc[2]
-    mains = outs[:CHUNKS]
-    edge_a, edge_b = outs[CHUNKS:]
-    levels = LEV // CHUNKS
+    sources = (wet, act, surf, depth, u, v, s)
+    copies = [pltpu.make_async_copy(a, b, sems.at[i]) for i, (a, b) in enumerate(zip(sources, buffers))]
+    for copy in copies:
+        copy.start()
+    for copy in copies[:4]:
+        copy.wait()
+    wet, act, surf, depth, *cubes = buffers
     count = (act[...] * wet[...]).astype(F32)
-    for f, ref in enumerate((u, v, s)):
+    plane[0] = surf[...]
+    plane[1] = count
+    plane[2] = depth[...]
+    for f in range(3):
+        copies[4 + f].wait()
         for lev in range(LEV):
-            tile = jnp.where(count > lev, ref[lev], 0.0)
+            tile = jnp.where(count > lev, cubes[f][lev], 0.0)
             for h in range(2):
                 st[f, h, pl.ds(lev, ROWS, stride=LEV), :] = tile[:, h * 128 : (h + 1) * 128]
     base = 2 * core
     for f in range(3):
         for j in range(HALO):
             for c in range(CHUNKS):
+                levels = SIZES[c]
                 for h in range(2):
-                    start = pl.multiple_of((base + j) * LEV + c * levels, 8)
+                    start = pl.multiple_of((base + j) * LEV + STARTS[c], 8)
                     mains[c][f, h, j * levels : (j + 1) * levels, :] = st[f, h, pl.ds(start, levels), :]
     lane = lanes((LEV, 128)) // 32
     odd = jnp.full((LEV, 128), north_odd, jnp.int32) == 1
@@ -97,7 +112,7 @@
     edge_b[6 * LEV :, :] = jnp.where(odd, right, left)
 
 
-def ext_kernel(sc, edge_a, edge_b, wet, act, surf, depth, own, corner, flat):
+def ext_kernel(sc, edge_a, edge_b, plane, own, corner, flat):
     core = sc[1]
     north_odd = sc[2]
 
@@ -120,16 +135,16 @@
                 at = (8 * f + 4 * g + q) * LEV
                 own[at : at + LEV, :] = unpack(high, low, q)
     high, low = halves(6 * LEV, ROWS)
-    count = (act[...] * wet[...]).astype(F32)
+    count = plane[1]
     counts = (count[:, :128], count[:, 128:], unpack(high, low, 1))
     for h in range(3):
         own[24 * LEV + 8 * h : 24 * LEV + 8 * h + 8, :] = counts[h]
         corner[9 * LEV + 8 * h : 9 * LEV + 8 * h + 8, :] = counts[h]
-    flat[0, :, :COLS] = surf[...]
+    flat[0, :, :COLS] = plane[0]
     flat[0, :, COLS:] = unpack(high, low, 0)
     flat[1, :, :COLS] = count
     flat[1, :, COLS:] = counts[2]
-    flat[2, :, :COLS] = depth[...]
+    flat[2, :, :COLS] = plane[2]
     flat[2, :, COLS:] = unpack(high, low, 2)
     lane = lanes((LEV, 128))
     inner = (lane >= 32) & (lane < 96)
@@ -162,13 +177,13 @@
 
 
 def rk_kernel(chunk, sc, st, stp, own, ownp, main, corner, flat, *rest):
-    levels = LEV // CHUNKS
+    levels = SIZES[chunk]
     if chunk:
         carry_in, sums_in = rest[:2]
         rest = rest[2:]
     out, carry, sums, flows, ext, one, two, counts = rest
     core = sc[1]
-    lev0 = chunk * levels
+    lev0 = STARTS[chunk]
     for f in range(3):
         for r in range(ROWS):
             for h in range(2):
@@ -276,18 +291,21 @@
         flows[2 + f] = flat[f]
 
 
-def solve_kernel(peers, sc, table, flat, *rest):
+def solve_kernel(sc, mine, pair, remote, remote_pair, far, flat, *rest):
     states = rest[:CHUNKS]
     east, north, salt, level = rest[CHUNKS : CHUNKS + 4]
     wide = rest[CHUNKS + 4]
-    levels = LEV // CHUNKS
-    me = sc[0]
-    for k in range(-3, 4):
-        peer = me + k
-        inside = (peer >= 0) & (peer < peers)
-        factor = jnp.where(inside, 1.0, 0.0).astype(F32)
-        block = table[jnp.clip(peer, 0, peers - 1)]
-        wide[:, 8 * (k + 3) : 8 * (k + 3) + 8, :] = block * factor
+    core = sc[1]
+    wide[:, 24:32, :] = mine[...]
+    for slot, block in (
+        (4 - 2 * core, pair[...]),
+        (2 + 2 * core, remote[0]),
+        (1 + 4 * core, remote[1]),
+        (5 - 4 * core, remote_pair[0]),
+        (6 - 6 * core, remote_pair[1]),
+        (6 * core, far[...]),
+    ):
+        wide[:, pl.ds(pl.multiple_of(8 * slot, 8), 8), :] = block
     high = 56
 
     def up(x):
@@ -330,7 +348,9 @@
     level[...] = x[24:32, :COLS]
     count = flat[1][:, :COLS]
     for lev in range(LEV):
-        c, at = divmod(lev, levels)
+        c = max(i for i in range(CHUNKS) if STARTS[i] <= lev)
+        levels = SIZES[c]
+        at = lev - STARTS[c]
         keep = count > lev
         for h in range(2):
             cols = slice(h * 128, (h + 1) * 128)
@@ -344,68 +364,79 @@
     return [p for a, b in pairs for p in ((a, b), (b, a))]
 
 
-def call(body, outs, scratch=(), ins=0):
+def call(body, outs, scratch=(), ins=0, space=pltpu.VMEM):
     vmem = pl.BlockSpec(memory_space=pltpu.VMEM)
     smem = pl.BlockSpec(memory_space=pltpu.SMEM)
     return pl.pallas_call(
         body,
         out_shape=[jax.ShapeDtypeStruct(s, F32) for s in outs],
-        in_specs=[smem] + [vmem] * ins,
+        in_specs=[smem] + [pl.BlockSpec(memory_space=space)] * ins,
         out_specs=[vmem] * len(outs),
-        scratch_shapes=[pltpu.VMEM(s, F32) for s in scratch],
-        compiler_params=pltpu.CompilerParams(vmem_limit_bytes=48 * 1024 * 1024),
+        scratch_shapes=[pltpu.VMEM(s, F32) if isinstance(s, tuple) else s for s in scratch],
+        compiler_params=pltpu.CompilerParams(vmem_limit_bytes=16 * 1024 * 1024),
     )
 
 
 def local(u, v, s, surface, depth, wet, active):
     gx = lax.axis_size("gx")
     gy = lax.axis_size("gy")
-    levels = LEV // CHUNKS
     me = lax.axis_index("gx")
     scalars = jnp.stack([me, me % 2, lax.axis_index("gy") % 2]).astype(jnp.int32)
     on_chip = swap([(i, i + 1) for i in range(0, gx, 2)])
     next_chip = swap([(i, i + 1) for i in range(1, gx - 1, 2)])
+    far_chip = swap([(i, i + 3) for i in range(1, gx - 3, 2)])
     even = swap([(i, i + 1) for i in range(0, gy, 2)])
     odd = swap([(i, i + 1) for i in range(1, gy - 1, 2)])
 
-    st, *packed = call(
+    edge_a, edge_b, *packed = call(
         pack_kernel,
-        [(3, 2, ROWS * LEV, 128)]
-        + [(3, 2, HALO * levels, 128)] * CHUNKS
-        + [(6 * LEV + 8, 128)] * 2,
+        [(6 * LEV + 8, 128)] * 2
+        + [(3, 2, HALO * levels, 128) for levels in SIZES]
+        + [(3, 2, ROWS * LEV, 128), (3, ROWS, COLS)],
+        [pltpu.VMEM((ROWS, COLS), jnp.int32)] * 2
+        + [(ROWS, COLS)] * 2
+        + [(LEV, ROWS, COLS)] * 3
+        + [pltpu.SemaphoreType.DMA((7,))],
         ins=7,
-    )(scalars, u, v, s, wet, active, surface, depth)
+        space=pltpu.HBM,
+    )(scalars, *(pltpu.with_memory_space_constraint(x, pltpu.HBM) for x in (u, v, s, wet, active, surface, depth)))
     mains = packed[:CHUNKS]
-    edge_a = lax.ppermute(packed[CHUNKS], "gy", even)
-    edge_b = lax.ppermute(packed[CHUNKS + 1], "gy", odd)
-    mains = [lax.ppermute(m, "gx", next_chip) for m in mains]
+    st, plane = packed[CHUNKS:]
+    edge_a = lax.ppermute(edge_a, "gy", even)
+    edge_b = lax.ppermute(edge_b, "gy", odd)
+    main = [lax.ppermute(mains[0], "gx", next_chip)]
     stp = lax.ppermute(st, "gx", on_chip)
     own, corner, flat = call(
         ext_kernel,
         [(24 * LEV + 24, 128), (9 * LEV + 24, 128), (3, ROWS, WIDE)],
-        ins=6,
-    )(scalars, edge_a, edge_b, wet, active, surface, depth)
+        ins=3,
+    )(scalars, edge_a, edge_b, plane)
+    corner, own, *mains = lax.optimization_barrier((corner, own, *mains[1:]))
     corner = lax.ppermute(corner, "gx", next_chip)
     ownp = lax.ppermute(own, "gx", on_chip)
+    main += [lax.ppermute(m, "gx", next_chip) for m in mains]
 
     states = []
     tail = []
-    for c in range(CHUNKS):
+    for c, levels in enumerate(SIZES):
         out, carry, sums, flows = call(
             functools.partial(rk_kernel, c),
             [(3, 2, ROWS * levels, 128), (72, 8, WIDE), (2, ROWS, 8, WIDE), (4, ROWS, WIDE)],
             [(3, 20, levels, WIDE), (3, 16, levels, WIDE), (3, 12, levels, WIDE), (20, 8, WIDE)],
             ins=7 + len(tail),
-        )(scalars, st, stp, own, ownp, mains[c], corner, flat, *tail)
+        )(scalars, st, stp, own, ownp, main[c], corner, flat, *tail)
         tail = [carry, sums]
         states.append(out)
-    table = lax.all_to_all(jnp.broadcast_to(flows[None], (gx,) + flows.shape), "gx", 0, 0)
+    far = lax.ppermute(flows, "gx", far_chip)
+    pair = lax.ppermute(flows, "gx", on_chip)
+    remote = lax.ppermute(jnp.stack([flows, pair]), "gx", next_chip)
+    remote_pair = lax.ppermute(remote, "gx", on_chip)
     east, north, salt, level = call(
-        functools.partial(solve_kernel, gx),
+        solve_kernel,
         [(LEV, ROWS, COLS)] * 3 + [(ROWS, COLS)],
         [(4, 56, WIDE)],
-        ins=2 + CHUNKS,
-    )(scalars, table, flat, *states)
+        ins=6 + CHUNKS,
+    )(scalars, flows, pair, remote, remote_pair, far, flat, *states)
     return east, north, salt, level
 
 

time: 131 us -> 117 us (0.89)
  the two profiles are of different devices: /device:TPU:56 before, /device:TPU:53 now
where the time goes in v2:
time: 117 us; the launch traced here: 116 us
  waiting for transfers between devices  47.6 us (41%)
  starting transfers between devices  38.9 us (33%)
  Pallas kernels  29 us (25%)
    ppermute x1, waiting for transfers between devices, local(): corner = lax.ppermute(corner, 'gx', next_chip)  29.8 us
    pallas_call x3, Pallas kernels, local(): call(functools.partial(rk_kernel, c), [(3, 2, ROWS * levels, 128), (72, 8...  21.7 us
    ppermute x2, starting transfers between devices, local(): main += [lax.ppermute(m, 'gx', next_chip) for m in mains]  12.9 us
    ppermute x1, waiting for transfers between devices, local(): remote = lax.ppermute(jnp.stack([flows, pair]), 'gx', next_chip)  7.21 us
    ppermute x1, waiting for transfers between devices, local(): edge_b = lax.ppermute(edge_b, 'gy', odd)  6.95 us
    ppermute x1, starting transfers between devices, local(): main = [lax.ppermute(mains[0], 'gx', next_chip)]  6.73 us
    ppermute x1, starting transfers between devices, local(): edge_b = lax.ppermute(edge_b, 'gy', odd)  5.19 us
    pallas_call x1, Pallas kernels, local(): call(solve_kernel, [(LEV, ROWS, COLS)] * 3 + [(ROWS, COLS)], [(4, 56, WID...  3.91 us
  transfers between devices with their start and end apart: 12, of which 6 were waited for; matrix products, arithmetic and copies ran while one was open for 0% of the time, Pallas kernels for 14%

profile of v2, /device:TPU:53, one launch (start us, length us, event | category | flops | bytes accessed | tf_op | source)
XLA Modules:
  0.0 116.3 jit_solution(2072400135366937708)
XLA Ops:
  0.6 0.1 pad_add_fusion.sc
  0.7 2.4 %shard_map.102 = (f32[296,128]{1,0:T(8,128)S(1)}, f32[296,128]{1,0:T(8,128)S(1)}, f32[3,2,144,128]{3,2,1,0:T(8,128)S(1)}, f32[3,2,96,128]{3,2,1,0:T(8,128)S(1)},...) custom-call(s32[3]{0:T(128)S(1)} %pad_add_fusion.sc, f32[48,8,256]{2,1,0:T(8,128)} %u.1, ...), custom_call_target="tpu_custom_call" | custom-call | tf_op jit(solution)/shard_map/pallas_call | solution.py:391
  3.2 0.8 collective-permute-start
  3.9 5.2 %collective-permute-start.2 = (f32[296,128]{1,0:T(8,128)S(1)}, f32[296,128]{1,0:T(8,128)S(1)}, u32[]{:S(2)}, u32[]{:S(2)}) collective-permute-start(f32[296,128]{1,0:T(8,128)S(1)} %get-tuple-element.28), channel_id=1, source_target_pairs={{1,2},{2,1},{3,4},{4,3},{5,6},{6,5},{7,8},{8,7},{9,10},{10,9},{11,... | collective-permute-start | bytes 454664 | tf_op jit(solution)/shard_map/ppermute | solution.py:406
  9.1 0.3 collective-permute-done.1.edge_a
  9.4 6.9 %collective-permute-done.2.edge_b = f32[296,128]{1,0:T(8,128)S(1)} collective-permute-done((f32[296,128]{1,0:T(8,128)S(1)}, f32[296,128]{1,0:T(8,128)S(1)}, u32[]{:S(2)}, u32[]{:S(2)}) %collective-permute-start.2) | collective-permute-done | bytes 151584 | tf_op jit(solution)/shard_map/ppermute | solution.py:406
  16.4 1.0 shard_map.103
  17.4 1.0 collective-permute-start.3
  18.3 6.7 %collective-permute-start.7 = (f32[3,2,144,128]{3,2,1,0:T(8,128)S(1)}, f32[3,2,144,128]{3,2,1,0:T(8,128)S(1)}, u32[]{:S(2)}, u32[]{:S(2)}) collective-permute-start(f32[3,2,144,128]{3,2,1,0:T(8,128)S(1)} %get-tuple-element.39), channel_id=1, source_target_pairs={{16,32},{32,16},{48,64},{64,48},{80,96},{96,80},{112,128},{128,112... | collective-permute-start | bytes 1327112 | tf_op jit(solution)/shard_map/ppermute | solution.py:407
  25.0 2.7 %collective-permute-start.5 = (f32[456,128]{1,0:T(8,128)S(1)}, f32[456,128]{1,0:T(8,128)S(1)}, u32[]{:S(2)}, u32[]{:S(2)}) collective-permute-start(f32[456,128]{1,0:T(8,128)S(1)} %get-tuple-element.36), channel_id=1, source_target_pairs={{16,32},{32,16},{48,64},{64,48},{80,96},{96,80},{112,128},{128,112... | collective-permute-start | bytes 700424 | tf_op jit(solution)/shard_map/ppermute | solution.py:415
  27.8 6.7 %collective-permute-start.6 = (f32[3,2,96,128]{3,2,1,0:T(8,128)S(1)}, f32[3,2,96,128]{3,2,1,0:T(8,128)S(1)}, u32[]{:S(2)}, u32[]{:S(2)}) collective-permute-start(f32[3,2,96,128]{3,2,1,0:T(8,128)S(1)} %get-tuple-element.38), channel_id=1, source_target_pairs={{16,32},{32,16},{48,64},{64,48},{80,96},{96,80},{112,128},{128,112... | collective-permute-start | bytes 884744 | tf_op jit(solution)/shard_map/ppermute | solution.py:417
  34.5 29.8 %collective-permute-done.5.corner = f32[456,128]{1,0:T(8,128)S(1)} collective-permute-done((f32[456,128]{1,0:T(8,128)S(1)}, f32[456,128]{1,0:T(8,128)S(1)}, u32[]{:S(2)}, u32[]{:S(2)}) %collective-permute-start.5) | collective-permute-done | bytes 233504 | tf_op jit(solution)/shard_map/ppermute | solution.py:415
  64.3 6.2 %collective-permute-start.4 = (f32[3,2,48,128]{3,2,1,0:T(8,128)S(1)}, f32[3,2,48,128]{3,2,1,0:T(8,128)S(1)}, u32[]{:S(2)}, u32[]{:S(2)}) collective-permute-start(f32[3,2,48,128]{3,2,1,0:T(8,128)S(1)} %get-tuple-element.35), channel_id=1, source_target_pairs={{16,32},{32,16},{48,64},{64,48},{80,96},{96,80},{112,128},{128,112... | collective-permute-start | bytes 442376 | tf_op jit(solution)/shard_map/ppermute | solution.py:417
  70.6 8.7 %shard_map.104 = (f32[3,2,192,128]{3,2,1,0:T(8,128)S(1)}, f32[72,8,384]{2,1,0:T(8,128)S(1)}, f32[2,8,8,384]{3,2,1,0:T(8,128)S(1)}, f32[4,8,384]{2,1,0:T(8,128)}) custom-call(s32[3]{0:T(128)S(1)} %pad_add_fusion.sc, f32[3,2,384,128]{3,2,1,0:T(8,128)S(1)} %get-tuple-element.26.st, f32[3,2,384,128]{3,2,1,0:T(8,128)S(1)} %collective-permute-done.stp, ...), custom_call_target="tpu_custom_call" | custom-call | tf_op jit(solution)/shard_map/pallas_call | solution.py:422
  79.3 7.1 %shard_map.105 = (f32[3,2,128,128]{3,2,1,0:T(8,128)S(1)}, f32[72,8,384]{2,1,0:T(8,128)S(1)}, f32[2,8,8,384]{3,2,1,0:T(8,128)S(1)}, f32[4,8,384]{2,1,0:T(8,128)}) custom-call(s32[3]{0:T(128)S(1)} %pad_add_fusion.sc, f32[3,2,384,128]{3,2,1,0:T(8,128)S(1)} %get-tuple-element.26.st, f32[3,2,384,128]{3,2,1,0:T(8,128)S(1)} %collective-permute-done.stp, ...), custom_call_target="tpu_custom_call" | custom-call | tf_op jit(solution)/shard_map/pallas_call | solution.py:422
  86.4 5.8 %shard_map.106 = (f32[3,2,64,128]{3,2,1,0:T(8,128)S(1)}, f32[72,8,384]{2,1,0:T(8,128)}, f32[2,8,8,384]{3,2,1,0:T(8,128)}, f32[4,8,384]{2,1,0:T(8,128)S(1)}) custom-call(s32[3]{0:T(128)S(1)} %pad_add_fusion.sc, f32[3,2,384,128]{3,2,1,0:T(8,128)S(1)} %get-tuple-element.26.st, f32[3,2,384,128]{3,2,1,0:T(8,128)S(1)} %collective-permute-done.stp, ...), custom_call_target="tpu_custom_call" | custom-call | tf_op jit(solution)/shard_map/pallas_call | solution.py:422
  92.2 1.7 %collective-permute-start.8 = (f32[4,8,384]{2,1,0:T(8,128)S(1)}, f32[4,8,384]{2,1,0:T(8,128)S(1)}, u32[]{:S(2)}, u32[]{:S(2)}) collective-permute-start(f32[4,8,384]{2,1,0:T(8,128)S(1)} %get-tuple-element.44.mine), channel_id=1, source_target_pairs={{0,16},{16,0},{32,48},{48,32},{64,80},{80,64},{96,112},{112,96},{1... | collective-permute-start | bytes 147464 | tf_op jit(solution)/shard_map/ppermute | solution.py:431
  94.0 0.9 collective-permute-done.8.pair
  94.9 2.9 %collective-permute-start.9 = (f32[2,4,8,384]{3,2,1,0:T(8,128)S(1)}, f32[2,4,8,384]{3,2,1,0:T(8,128)S(1)}, u32[]{:S(2)}, u32[]{:S(2)}) collective-permute-start(f32[2,4,8,384]{3,2,1,0:T(8,128)S(1)} %pad_maximum_fusion), channel_id=1, source_target_pairs={{16,32},{32,16},{48,64},{64,48},{80,96},{96,80},{112,128},{128,112... | collective-permute-start | bytes 294920 | tf_op jit(solution)/shard_map/ppermute | solution.py:432
  97.8 7.2 %collective-permute-done.9.remote = f32[2,4,8,384]{3,2,1,0:T(8,128)S(1)} collective-permute-done((f32[2,4,8,384]{3,2,1,0:T(8,128)S(1)}, f32[2,4,8,384]{3,2,1,0:T(8,128)S(1)}, u32[]{:S(2)}, u32[]{:S(2)}) %collective-permute-start.9) | collective-permute-done | bytes 98336 | tf_op jit(solution)/shard_map/ppermute | solution.py:432
  105.0 2.0 %collective-permute-start.10 = (f32[2,4,8,384]{3,2,1,0:T(8,128)S(1)}, f32[2,4,8,384]{3,2,1,0:T(8,128)S(1)}, u32[]{:S(2)}, u32[]{:S(2)}) collective-permute-start(f32[2,4,8,384]{3,2,1,0:T(8,128)S(1)} %collective-permute-done.9.remote), channel_id=1, source_target_pairs={{0,16},{16,0},{32,48},{48,32},{64,80},{80,64},{96,112},{112,96},{1... | collective-permute-start | bytes 294920 | tf_op jit(solution)/shard_map/ppermute | solution.py:433
  107.0 2.9 %collective-permute-start.11 = (f32[4,8,384]{2,1,0:T(8,128)S(1)}, f32[4,8,384]{2,1,0:T(8,128)S(1)}, u32[]{:S(2)}, u32[]{:S(2)}) collective-permute-start(f32[4,8,384]{2,1,0:T(8,128)S(1)} %get-tuple-element.44.mine), channel_id=1, source_target_pairs={{16,64},{64,16},{48,96},{96,48},{80,128},{128,80},{112,160},{160,1... | collective-permute-start | bytes 147464 | tf_op jit(solution)/shard_map/ppermute | solution.py:430
  109.9 2.5 %collective-permute-done.11.far = f32[4,8,384]{2,1,0:T(8,128)S(1)} collective-permute-done((f32[4,8,384]{2,1,0:T(8,128)S(1)}, f32[4,8,384]{2,1,0:T(8,128)S(1)}, u32[]{:S(2)}, u32[]{:S(2)}) %collective-permute-start.11) | collective-permute-done | bytes 49184 | tf_op jit(solution)/shard_map/ppermute | solution.py:430
  112.4 3.9 %shard_map.107 = (f32[48,8,256]{2,1,0:T(8,128)}, f32[48,8,256]{2,1,0:T(8,128)}, f32[48,8,256]{2,1,0:T(8,128)}, f32[8,256]{1,0:T(8,128)}) custom-call(s32[3]{0:T(128)S(1)} %pad_add_fusion.sc, f32[4,8,384]{2,1,0:T(8,128)S(1)} %get-tuple-element.44.mine, f32[4,8,384]{2,1,0:T(8,128)S(1)} %collective-permute-done.8.pair, ...), custom_call_target="tpu_custom_call" | custom-call | tf_op jit(solution)/shard_map/pallas_call | solution.py:434
  (8 shorter events, 0.0 us)
Async XLA Ops:
  3.2 67.4 %collective-permute-start = (f32[3,2,384,128]{3,2,1,0:T(8,128)S(1)}, f32[3,2,384,128]{3,2,1,0:T(8,128)S(1)}, u32[]{:S(2)}, u32[]{:S(2)}) collective-permute-start(f32[3,2,384,128]{3,2,1,0:T(8,128)S(1)} %get-tuple-element.26.st), channel_id=1, source_target_pairs={{0,16},{16,0},{32,48},{48,32},{64,80},{80,64},{96,112},{112,96},{1... | collective-permute-start | bytes 3538952 | tf_op jit(solution)/shard_map/ppermute | solution.py:408
  3.9 5.5 %collective-permute-start.1 = (f32[296,128]{1,0:T(8,128)S(1)}, f32[296,128]{1,0:T(8,128)S(1)}, u32[]{:S(2)}, u32[]{:S(2)}) collective-permute-start(f32[296,128]{1,0:T(8,128)S(1)} %get-tuple-element.27), channel_id=1, source_target_pairs={{0,1},{1,0},{2,3},{3,2},{4,5},{5,4},{6,7},{7,6},{8,9},{9,8},{10,11... | collective-permute-start | bytes 454664 | tf_op jit(solution)/shard_map/ppermute | solution.py:405
  3.9 12.4 %collective-permute-start.2 = (f32[296,128]{1,0:T(8,128)S(1)}, f32[296,128]{1,0:T(8,128)S(1)}, u32[]{:S(2)}, u32[]{:S(2)}) collective-permute-start(f32[296,128]{1,0:T(8,128)S(1)} %get-tuple-element.28), channel_id=1, source_target_pairs={{1,2},{2,1},{3,4},{4,3},{5,6},{6,5},{7,8},{8,7},{9,10},{10,9},{11,... | collective-permute-start | bytes 454664 | tf_op jit(solution)/shard_map/ppermute | solution.py:406
  17.4 53.2 %collective-permute-start.3 = (f32[1176,128]{1,0:T(8,128)S(1)}, f32[1176,128]{1,0:T(8,128)S(1)}, u32[]{:S(2)}, u32[]{:S(2)}) collective-permute-start(f32[1176,128]{1,0:T(8,128)S(1)} %get-tuple-element.34.own), channel_id=1, source_target_pairs={{0,16},{16,0},{32,48},{48,32},{64,80},{80,64},{96,112},{112,96},{1... | collective-permute-start | bytes 1806344 | tf_op jit(solution)/shard_map/ppermute | solution.py:416
  18.3 52.2 %collective-permute-start.7 = (f32[3,2,144,128]{3,2,1,0:T(8,128)S(1)}, f32[3,2,144,128]{3,2,1,0:T(8,128)S(1)}, u32[]{:S(2)}, u32[]{:S(2)}) collective-permute-start(f32[3,2,144,128]{3,2,1,0:T(8,128)S(1)} %get-tuple-element.39), channel_id=1, source_target_pairs={{16,32},{32,16},{48,64},{64,48},{80,96},{96,80},{112,128},{128,112... | collective-permute-start | bytes 1327112 | tf_op jit(solution)/shard_map/ppermute | solution.py:407
  25.0 39.3 %collective-permute-start.5 = (f32[456,128]{1,0:T(8,128)S(1)}, f32[456,128]{1,0:T(8,128)S(1)}, u32[]{:S(2)}, u32[]{:S(2)}) collective-permute-start(f32[456,128]{1,0:T(8,128)S(1)} %get-tuple-element.36), channel_id=1, source_target_pairs={{16,32},{32,16},{48,64},{64,48},{80,96},{96,80},{112,128},{128,112... | collective-permute-start | bytes 700424 | tf_op jit(solution)/shard_map/ppermute | solution.py:415
  27.8 51.5 %collective-permute-start.6 = (f32[3,2,96,128]{3,2,1,0:T(8,128)S(1)}, f32[3,2,96,128]{3,2,1,0:T(8,128)S(1)}, u32[]{:S(2)}, u32[]{:S(2)}) collective-permute-start(f32[3,2,96,128]{3,2,1,0:T(8,128)S(1)} %get-tuple-element.38), channel_id=1, source_target_pairs={{16,32},{32,16},{48,64},{64,48},{80,96},{96,80},{112,128},{128,112... | collective-permute-start | bytes 884744 | tf_op jit(solution)/shard_map/ppermute | solution.py:417
  64.3 22.1 %collective-permute-start.4 = (f32[3,2,48,128]{3,2,1,0:T(8,128)S(1)}, f32[3,2,48,128]{3,2,1,0:T(8,128)S(1)}, u32[]{:S(2)}, u32[]{:S(2)}) collective-permute-start(f32[3,2,48,128]{3,2,1,0:T(8,128)S(1)} %get-tuple-element.35), channel_id=1, source_target_pairs={{16,32},{32,16},{48,64},{64,48},{80,96},{96,80},{112,128},{128,112... | collective-permute-start | bytes 442376 | tf_op jit(solution)/shard_map/ppermute | solution.py:417
  92.2 2.6 %collective-permute-start.8 = (f32[4,8,384]{2,1,0:T(8,128)S(1)}, f32[4,8,384]{2,1,0:T(8,128)S(1)}, u32[]{:S(2)}, u32[]{:S(2)}) collective-permute-start(f32[4,8,384]{2,1,0:T(8,128)S(1)} %get-tuple-element.44.mine), channel_id=1, source_target_pairs={{0,16},{16,0},{32,48},{48,32},{64,80},{80,64},{96,112},{112,96},{1... | collective-permute-start | bytes 147464 | tf_op jit(solution)/shard_map/ppermute | solution.py:431
  94.9 10.1 %collective-permute-start.9 = (f32[2,4,8,384]{3,2,1,0:T(8,128)S(1)}, f32[2,4,8,384]{3,2,1,0:T(8,128)S(1)}, u32[]{:S(2)}, u32[]{:S(2)}) collective-permute-start(f32[2,4,8,384]{3,2,1,0:T(8,128)S(1)} %pad_maximum_fusion), channel_id=1, source_target_pairs={{16,32},{32,16},{48,64},{64,48},{80,96},{96,80},{112,128},{128,112... | collective-permute-start | bytes 294920 | tf_op jit(solution)/shard_map/ppermute | solution.py:432
  105.0 7.4 %collective-permute-start.10 = (f32[2,4,8,384]{3,2,1,0:T(8,128)S(1)}, f32[2,4,8,384]{3,2,1,0:T(8,128)S(1)}, u32[]{:S(2)}, u32[]{:S(2)}) collective-permute-start(f32[2,4,8,384]{3,2,1,0:T(8,128)S(1)} %collective-permute-done.9.remote), channel_id=1, source_target_pairs={{0,16},{16,0},{32,48},{48,32},{64,80},{80,64},{96,112},{112,96},{1... | collective-permute-start | bytes 294920 | tf_op jit(solution)/shard_map/ppermute | solution.py:433
  107.0 5.4 %collective-permute-start.11 = (f32[4,8,384]{2,1,0:T(8,128)S(1)}, f32[4,8,384]{2,1,0:T(8,128)S(1)}, u32[]{:S(2)}, u32[]{:S(2)}) collective-permute-start(f32[4,8,384]{2,1,0:T(8,128)S(1)} %get-tuple-element.44.mine), channel_id=1, source_target_pairs={{16,64},{64,16},{48,96},{96,48},{80,128},{128,80},{112,160},{160,1... | collective-permute-start | bytes 147464 | tf_op jit(solution)/shard_map/ppermute | solution.py:430

commit v3 on v2

v3 whole, which is shorter than its diff:
```python
import functools

import jax
import jax.numpy as jnp
from jax import lax
from jax.experimental import pallas as pl
from jax.experimental.pallas import tpu as pltpu
from jax.sharding import PartitionSpec as P

ITERS = 16
TIME_STEP = 0.2
CORIOLIS = 0.3
PRESS_COEF = 0.05
VISCOSITY = 0.1
DIFFUSIVITY = 0.1
SIGMA_SHIFT = 0.25
CHEB_CENTER = 3.625
CHEB_HALF = 3.375
DIVERGENCE_COEF = 8.0

LEV = 48
ROWS = 8
COLS = 256
EXT = 128
WIDE = COLS + EXT
HALO = 6
SIZES = (32, 16)
CHUNKS = len(SIZES)
STARTS = tuple(sum(SIZES[:c]) for c in range(CHUNKS))
SLOT = 25
SLOTS = 5
EDGE_TILES = -(-3 * ROWS // SLOTS)
CORNER_TILES = -(-3 * HALO // SLOTS)
F32 = jnp.float32


def cheb_table(count):
    first = CHEB_CENTER / CHEB_HALF
    ratio = 1.0 / first
    keeps = []
    gains = []
    for index in range(count):
        ratio_next = 1.0 / (2.0 * first - ratio)
        keeps.append(ratio_next * ratio)
        gains.append(2.0 * ratio_next / CHEB_HALF)
        ratio = ratio_next
    return (keeps, gains)


def lanes(shape):
    return lax.broadcasted_iota(jnp.int32, shape, len(shape) - 1)


def place(low, high, units, slot):
    left, right = units
    lane = lanes(low.shape)
    here = (lane >= SLOT * slot) & (lane < SLOT * slot + SLOT)
    low = low if slot == 0 else pltpu.roll(low, SLOT * slot, 1)
    high = pltpu.roll(high, SLOT * slot + SLOT, 1)
    return jnp.where(here, low, left), jnp.where(here, high, right)


def unpack(high, low, slot):
    lane = lanes(high.shape)
    high = high if slot == 0 else pltpu.roll(high, 128 - SLOT * slot, 1)
    low = pltpu.roll(low, 128 - SLOT - SLOT * slot, 1)
    return jnp.where(lane < SLOT, high, jnp.where(lane >= 128 - SLOT, low, 0.0))


def ordered(first, second, flag):
    odd = jnp.full(first.shape, flag, jnp.int32) == 1
    return jnp.where(odd, second, first), jnp.where(odd, first, second)


def pack_kernel(sc, u, v, s, wet, act, surf, depth, edge_a, edge_b, corner_a, corner_b, *rest):
    mains = rest[:CHUNKS]
    st, plane = rest[CHUNKS : CHUNKS + 2]
    buffers = rest[CHUNKS + 2 : CHUNKS + 9]
    sems = rest[CHUNKS + 9]
    core = sc[1]
    north_odd = sc[2]
    sources = (wet, act, surf, depth, u, v, s)
    copies = [pltpu.make_async_copy(a, b, sems.at[i]) for i, (a, b) in enumerate(zip(sources, buffers))]
    for copy in copies:
        copy.start()
    for copy in copies[:4]:
        copy.wait()
    wet, act, surf, depth, *cubes = buffers
    count = (act[...] * wet[...]).astype(F32)
    plane[0] = surf[...]
    plane[1] = count
    plane[2] = depth[...]
    for f in range(3):
        copies[4 + f].wait()
        for lev in range(LEV):
            tile = jnp.where(count > lev, cubes[f][lev], 0.0)
            for h in range(2):
                st[pl.ds((2 * f + h) * ROWS * LEV + lev, ROWS, stride=LEV), :] = tile[:, h * 128 : (h + 1) * 128]
    base = 2 * core
    for c in range(CHUNKS):
        levels = SIZES[c]
        for f in range(3):
            for j in range(HALO):
                for h in range(2):
                    start = pl.multiple_of(((2 * f + h) * ROWS + base + j) * LEV + STARTS[c], 8)
                    at = ((2 * f + h) * HALO + j) * levels
                    mains[c][at : at + levels, :] = st[pl.ds(start, levels), :]
    for h in range(2):
        at = 6 * HALO * SIZES[0] + 8 * h
        mains[0][at : at + 8, :] = count[:, 128 * h : 128 * h + 128]
        at = 6 * ROWS * LEV + 8 * h
        st[at : at + 8, :] = count[:, 128 * h : 128 * h + 128]
    blank = jnp.zeros((LEV, 128), F32)
    for tiles, rows, first, a, b in (
        (EDGE_TILES, ROWS, 0, edge_a, edge_b),
        (CORNER_TILES, HALO, base, corner_a, corner_b),
    ):
        for g in range(tiles):
            units = (blank, blank)
            for slot in range(min(SLOTS, 3 * rows - SLOTS * g)):
                f, r = divmod(SLOTS * g + slot, rows)
                low = pl.multiple_of((2 * f * ROWS + first + r) * LEV, 8)
                high = pl.multiple_of(((2 * f + 1) * ROWS + first + r) * LEV, 8)
                units = place(st[pl.ds(low, LEV), :], st[pl.ds(high, LEV), :], units, slot)
            b[g * LEV : g * LEV + LEV, :], a[g * LEV : g * LEV + LEV, :] = ordered(*units, north_odd)
    units = (blank[:ROWS], blank[:ROWS])
    for slot, field in enumerate((surf[...], count, depth[...])):
        units = place(field[:, :128], field[:, 128:], units, slot)
    left, right = ordered(*units, north_odd)
    for tiles, a, b in ((EDGE_TILES, edge_a, edge_b), (CORNER_TILES, corner_a, corner_b)):
        b[tiles * LEV :, :] = left
        a[tiles * LEV :, :] = right


def shifts(q):
    return (
        pltpu.roll(q, WIDE - 1, 1),
        pltpu.roll(q, 1, 1),
        pltpu.roll(q, WIDE - 2, 1),
        pltpu.roll(q, 2, 1),
    )


def slope(ahead, behind, ahead2, behind2):
    return (8.0 / 12.0) * (ahead - behind) - (1.0 / 12.0) * (ahead2 - behind2)


def running(x, sub):
    for step in (1, 2, 4):
        x = x + jnp.where(sub >= step, pltpu.roll(x, step, 0), 0.0)
    return x


def rk_kernel(chunk, sc, st, stp, edge_a, edge_b, edgep_a, edgep_b, main, main0, corner_a, corner_b, plane, *rest):
    levels = SIZES[chunk]
    if chunk:
        carry_in, sums_in = rest[:2]
        rest = rest[2:]
    if chunk == CHUNKS - 1:
        flows, rest = rest[0], rest[1:]
    out, carry, sums, ext, one, two, counts, flat, remote = rest
    core = sc[1]
    north_odd = sc[2]
    lev0 = STARTS[chunk]
    beside = 16 * (1 - core)
    beyond = 2 + 14 * core
    for source, first in ((st, ROWS), (stp, beside)):
        for f in range(3):
            for r in range(ROWS):
                for h in range(2):
                    at = ((2 * f + h) * ROWS + r) * LEV + lev0
                    ext[f, first + r, :, h * 128 : (h + 1) * 128] = source[at : at + levels, :]
    for f in range(3):
        for j in range(HALO):
            for h in range(2):
                at = ((2 * f + h) * HALO + j) * levels
                ext[f, beyond + j, :, h * 128 : (h + 1) * 128] = main[at : at + levels, :]
    for tiles, rows, first, a, b in (
        (EDGE_TILES, ROWS, ROWS, edge_a, edge_b),
        (EDGE_TILES, ROWS, beside, edgep_a, edgep_b),
        (CORNER_TILES, HALO, beyond, corner_a, corner_b),
    ):
        for g in range(tiles):
            here = slice(g * LEV + lev0, g * LEV + lev0 + levels)
            high, low = ordered(a[here, :], b[here, :], north_odd)
            for slot in range(min(SLOTS, 3 * rows - SLOTS * g)):
                f, r = divmod(SLOTS * g + slot, rows)
                ext[f, first + r, :, COLS:] = unpack(high, low, slot)

    def beyond_plane(tiles, a, b, slot):
        high, low = ordered(a[tiles * LEV :, :], b[tiles * LEV :, :], north_odd)
        return unpack(high, low, slot)

    for f in range(3):
        flat[f, :, :COLS] = plane[f]
        flat[f, :, COLS:] = beyond_plane(EDGE_TILES, edge_a, edge_b, f)
    remote[0, :, COLS:] = beyond_plane(EDGE_TILES, edgep_a, edgep_b, 1)
    remote[1, :, COLS:] = beyond_plane(CORNER_TILES, corner_a, corner_b, 1)
    for h in range(2):
        at = 6 * ROWS * LEV + 8 * h
        remote[0, :, h * 128 : (h + 1) * 128] = stp[at : at + 8, :]
        at = 6 * HALO * SIZES[0] + 8 * h
        remote[1, :, h * 128 : (h + 1) * 128] = main0[at : at + 8, :]
    for r in range(ROWS):
        counts[ROWS + r] = jnp.broadcast_to(flat[1, r : r + 1, :], (8, WIDE))
        counts[beside + r] = jnp.broadcast_to(remote[0, r : r + 1, :], (8, WIDE))
    for j in range(HALO):
        counts[beyond + j] = jnp.broadcast_to(remote[1, pl.ds(2 * (1 - core) + j, 1), :], (8, WIDE))

    sub = lax.broadcasted_iota(jnp.int32, (8, WIDE), 0)

    def stage(source, lead, rows, inset, write, slot):
        def row(o, _):
            count = counts[o + inset]
            if chunk:
                sum_x = jnp.broadcast_to(carry_in[pl.ds(slot + 2 * o, 1), :], (8, WIDE))
                sum_y = jnp.broadcast_to(carry_in[pl.ds(slot + 2 * o + 1, 1), :], (8, WIDE))
            else:
                sum_x = jnp.zeros((8, WIDE), F32)
                sum_y = jnp.zeros((8, WIDE), F32)
            for t in range(levels // 8):
                here = slice(8 * t, 8 * t + 8)
                mid = []
                dxs = []
                dys = []
                laps = []
                for f in range(3):
                    q = source[f, o + lead + 2, here, :]
                    back2, back = source[f, o + lead, here, :], source[f, o + lead + 1, here, :]
                    fore, fore2 = source[f, o + lead + 3, here, :], source[f, o + lead + 4, here, :]
                    right, left, right2, left2 = shifts(q)
                    mid.append(q)
                    dxs.append(slope(fore, back, fore2, back2))
                    dys.append(slope(right, left, right2, left2))
                    laps.append((fore + back) + (right + left) - 4.0 * q)
                press_x = running(dxs[2], sub) + sum_x
                press_y = running(dys[2], sub) + sum_y
                sum_x = jnp.broadcast_to(press_x[7:8, :], (8, WIDE))
                sum_y = jnp.broadcast_to(press_y[7:8, :], (8, WIDE))
                u, v, _s = mid
                rates = [VISCOSITY * laps[f] - (u * dxs[f] + v * dys[f]) for f in range(3)]
                rates[0] = rates[0] + (CORIOLIS * v - PRESS_COEF * press_x)
                rates[1] = rates[1] - (CORIOLIS * u + PRESS_COEF * press_y)
                keep = count > (sub + (lev0 + 8 * t)).astype(F32)
                write(o, here, t, mid, [jnp.where(keep, r, 0.0) for r in rates])
            carry[pl.ds(slot + 2 * o, 1), :] = sum_x[:1, :]
            carry[pl.ds(slot + 2 * o + 1, 1), :] = sum_y[:1, :]
            return 0

        lax.fori_loop(0, rows, row, 0, unroll=max(1, min(4, 32 // levels)))

    def write1(o, here, t, mid, rates):
        for f in range(3):
            one[f, o, here, :] = mid[f] + TIME_STEP * rates[f]

    def write2(o, here, t, mid, rates):
        for f in range(3):
            first = ext[f, o + 6, here, :]
            two[f, o, here, :] = 0.75 * first + (0.25 * mid[f] + (0.25 * TIME_STEP) * rates[f])

    def write3(o, here, t, mid, rates):
        for f in range(3):
            first = ext[f, o + 8, here, :]
            value = (1.0 / 3.0) * first + ((2.0 / 3.0) * mid[f] + (2.0 / 3.0 * TIME_STEP) * rates[f])
            at = pl.multiple_of(o * levels + 8 * t, 8)
            for h in range(2):
                out[f, h, pl.ds(at, 8), :] = value[:, h * 128 : (h + 1) * 128]
            if f < 2:
                if t == 0:
                    sums[f, o] = value + sums_in[f, o] if chunk else value
                else:
                    sums[f, o] = sums[f, o] + value

    stage(ext, 2, 16, 4, write1, 0)
    stage(one, 0, 12, 6, write2, 32)
    stage(two, 0, 8, 8, write3, 56)
    if chunk == CHUNKS - 1:
        for f in range(2):
            for o in range(ROWS):
                flows[f, o : o + 1, :] = jnp.sum(sums[f, o], axis=0, keepdims=True)
            flows[f] = flat[2] * (flows[f] * (1.0 / LEV))
            flows[2 + f] = flat[f]


def solve_kernel(sc, mine, pair, remote, remote_pair, far, *rest):
    states = rest[:CHUNKS]
    east, north, salt, level = rest[CHUNKS : CHUNKS + 4]
    wide = rest[CHUNKS + 4]
    core = sc[1]
    wide[:, 24:32, :] = mine[...]
    for slot, block in (
        (4 - 2 * core, pair[...]),
        (2 + 2 * core, remote[0]),
        (1 + 4 * core, remote[1]),
        (5 - 4 * core, remote_pair[0]),
        (6 - 6 * core, remote_pair[1]),
        (6 * core, far[...]),
    ):
        wide[:, pl.ds(pl.multiple_of(8 * slot, 8), 8), :] = block
    high = 56

    def up(x):
        return pltpu.roll(x, high - 1, 0)

    def down(x):
        return pltpu.roll(x, 1, 0)

    def right(x):
        return pltpu.roll(x, WIDE - 1, 1)

    def left(x):
        return pltpu.roll(x, 1, 1)

    wet = jnp.where(wide[3] > 0.0, 1.0, 0.0)
    dry = 1.0 - wet

    def apply(e):
        w = wet * e
        rows = up(w) + down(w)
        mix = 4.0 * w + rows
        sides = right(mix) + left(mix)
        stencil = (20.0 / 6.0) * w - (4.0 / 6.0) * rows - (1.0 / 6.0) * sides
        return wet * (SIGMA_SHIFT * e + stencil) + dry * e

    flow_east = wide[0]
    flow_north = wide[1]
    x = wide[2]
    div = 0.5 * (up(flow_east) - down(flow_east)) + 0.5 * (right(flow_north) - left(flow_north))
    res = wet * (SIGMA_SHIFT * x - DIVERGENCE_COEF * div) - apply(x)
    step = res * (1.0 / CHEB_CENTER)
    keeps, gains = cheb_table(ITERS)
    for index in range(ITERS):
        x = x + step
        if index < ITERS - 1:
            res = res - apply(step)
            step = keeps[index] * step + gains[index] * res
    slope_east = (0.5 * (up(x) - down(x)))[24:32, :COLS]
    slope_north = (0.5 * (right(x) - left(x)))[24:32, :COLS]
    level[...] = x[24:32, :COLS]
    count = mine[3][:, :COLS]
    for lev in range(LEV):
        c = max(i for i in range(CHUNKS) if STARTS[i] <= lev)
        levels = SIZES[c]
        at = lev - STARTS[c]
        keep = count > lev
        for h in range(2):
            cols = slice(h * 128, (h + 1) * 128)
            parts = [states[c][f, h, pl.ds(at, ROWS, stride=levels), :] for f in range(3)]
            east[lev, :, cols] = jnp.where(keep[:, cols], parts[0] - slope_east[:, cols], 0.0)
            north[lev, :, cols] = jnp.where(keep[:, cols], parts[1] - slope_north[:, cols], 0.0)
            salt[lev, :, cols] = parts[2]


def swap(pairs):
    return [p for a, b in pairs for p in ((a, b), (b, a))]


def call(body, outs, scratch=(), ins=0, space=pltpu.VMEM, cost=None):
    vmem = pl.BlockSpec(memory_space=pltpu.VMEM)
    smem = pl.BlockSpec(memory_space=pltpu.SMEM)
    return pl.pallas_call(
        body,
        out_shape=[jax.ShapeDtypeStruct(s, F32) for s in outs],
        in_specs=[smem] + [pl.BlockSpec(memory_space=space)] * ins,
        out_specs=[vmem] * len(outs),
        scratch_shapes=[pltpu.VMEM(s, F32) if isinstance(s, tuple) else s for s in scratch],
        cost_estimate=cost and pl.CostEstimate(flops=cost, transcendentals=0, bytes_accessed=0),
        compiler_params=pltpu.CompilerParams(vmem_limit_bytes=16 * 1024 * 1024),
    )


def local(u, v, s, surface, depth, wet, active):
    gx = lax.axis_size("gx")
    gy = lax.axis_size("gy")
    me = lax.axis_index("gx")
    scalars = jnp.stack([me, me % 2, lax.axis_index("gy") % 2]).astype(jnp.int32)
    on_chip = swap([(i, i + 1) for i in range(0, gx, 2)])
    next_chip = swap([(i, i + 1) for i in range(1, gx - 1, 2)])
    far_chip = swap([(i, i + 3) for i in range(1, gx - 3, 2)])
    even = swap([(i, i + 1) for i in range(0, gy, 2)])
    odd = swap([(i, i + 1) for i in range(1, gy - 1, 2)])

    def both(first, second):
        return [(i * gy + j, k * gy + l) for i, k in first for j, l in second]

    edge_a, edge_b, corner_a, corner_b, *packed = call(
        pack_kernel,
        [(EDGE_TILES * LEV + 8, 128)] * 2
        + [(CORNER_TILES * LEV + 8, 128)] * 2
        + [(6 * HALO * levels + (0 if c else 16), 128) for c, levels in enumerate(SIZES)]
        + [(6 * ROWS * LEV + 16, 128), (3, ROWS, COLS)],
        [pltpu.VMEM((ROWS, COLS), jnp.int32)] * 2
        + [(ROWS, COLS)] * 2
        + [(LEV, ROWS, COLS)] * 3
        + [pltpu.SemaphoreType.DMA((7,))],
        ins=7,
        space=pltpu.HBM,
    )(scalars, *(pltpu.with_memory_space_constraint(x, pltpu.HBM) for x in (u, v, s, wet, active, surface, depth)))
    mains = packed[:CHUNKS]
    st, plane = packed[CHUNKS:]
    stp = lax.ppermute(st, "gx", on_chip)
    main = [lax.ppermute(mains[0], "gx", next_chip)]
    stp, corner_a, corner_b = lax.optimization_barrier((stp, corner_a, corner_b))
    edge_a = lax.ppermute(edge_a, "gy", even)
    edge_b = lax.ppermute(edge_b, "gy", odd)
    corner_a = lax.ppermute(corner_a, ("gx", "gy"), both(next_chip, even))
    corner_b = lax.ppermute(corner_b, ("gx", "gy"), both(next_chip, odd))
    corner_a, corner_b, edge_a, edge_b, *later = lax.optimization_barrier((corner_a, corner_b, edge_a, edge_b, *mains[1:]))
    main += [lax.ppermute(m, "gx", next_chip) for m in later]
    edgep_a = lax.ppermute(edge_a, "gx", on_chip)
    edgep_b = lax.ppermute(edge_b, "gx", on_chip)

    states = []
    tail = []
    for c, levels in enumerate(SIZES):
        *flows, out, carry, sums = call(
            functools.partial(rk_kernel, c),
            [(4, ROWS, WIDE)] * (c == CHUNKS - 1)
            + [(3, 2, ROWS * levels, 128), (72, WIDE), (2, ROWS, 8, WIDE)],
            [(3, 24, levels, WIDE), (3, 16, levels, WIDE), (3, 12, levels, WIDE)]
            + [(24, 8, WIDE), (3, ROWS, WIDE), (2, ROWS, WIDE)],
            ins=11 + len(tail),
        )(scalars, st, stp, edge_a, edge_b, edgep_a, edgep_b, main[c], main[0], corner_a, corner_b, plane, *tail)
        tail = [carry, sums]
        states.append(out)
    flows = flows[0]
    far = lax.ppermute(flows, "gx", far_chip)
    pair = lax.ppermute(flows, "gx", on_chip)
    remote = lax.ppermute(jnp.stack([flows, pair]), "gx", next_chip)
    remote, far = lax.optimization_barrier((remote, far))
    remote_pair = lax.ppermute(remote, "gx", on_chip)
    east, north, salt, level = call(
        solve_kernel,
        [(LEV, ROWS, COLS)] * 3 + [(ROWS, COLS)],
        [(4, 56, WIDE)],
        ins=5 + CHUNKS,
    )(scalars, flows, pair, remote, remote_pair, far, *states)
    return east, north, salt, level


def solution(mesh):
    cube = P(None, "gx", "gy")
    flat = P("gx", "gy")
    return jax.shard_map(
        local,
        mesh=mesh,
        in_specs=(cube, cube, cube, flat, flat, flat, flat),
        out_specs=(cube, cube, cube, flat),
        check_vma=False,
    )
```

time: 117 us -> 95.3 us (0.81)
  the two profiles are of different devices: /device:TPU:53 before, /device:TPU:31 now
where the time goes in v3:
time: 95.3 us; the launch traced here: 94.6 us
  waiting for transfers between devices  35.6 us (37%)
  starting transfers between devices  35.4 us (37%)
  Pallas kernels  22.8 us (24%)
    ppermute x1, waiting for transfers between devices, local(): edge_a = lax.ppermute(edge_a, 'gy', even)  20.3 us
    pallas_call x2, Pallas kernels, local(): call(functools.partial(rk_kernel, c), [(4, ROWS, WIDE)] * (c == CHUNKS -...  16 us
    ppermute x1, starting transfers between devices, local(): main = [lax.ppermute(mains[0], 'gx', next_chip)]  8.72 us
    ppermute x1, waiting for transfers between devices, local(): remote = lax.ppermute(jnp.stack([flows, pair]), 'gx', next_chip)  8.59 us
    ppermute x1, starting transfers between devices, local(): main += [lax.ppermute(m, 'gx', next_chip) for m in later]  4.92 us
    ppermute x1, starting transfers between devices, local(): corner_b = lax.ppermute(corner_b, ('gx', 'gy'), both(next_chip, odd))  4.29 us
    pallas_call x1, Pallas kernels, local(): call(solve_kernel, [(LEV, ROWS, COLS)] * 3 + [(ROWS, COLS)], [(4, 56, WID...  4.14 us
    ppermute x1, starting transfers between devices, local(): edge_b = lax.ppermute(edge_b, 'gy', odd)  3.71 us
  transfers between devices with their start and end apart: 13, of which 7 were waited for; matrix products, arithmetic and copies ran while one was open for 0% of the time, Pallas kernels for 11%

profile of v3, /device:TPU:31, one launch (start us, length us, event | category | flops | bytes accessed | tf_op | source)
XLA Modules:
  0.0 94.6 jit_solution(2382552925840761986)
XLA Ops:
  0.7 2.6 %shard_map.102 = (f32[248,128]{1,0:T(8,128)S(1)}, f32[248,128]{1,0:T(8,128)S(1)}, f32[200,128]{1,0:T(8,128)S(1)}, f32[200,128]{1,0:T(8,128)S(1)}, f32[1168,128]{...) custom-call(s32[3]{0:T(128)S(1)} %pad_add_fusion.sc, ...), custom_call_target="tpu_custom_call" | custom-call | tf_op jit(solution)/shard_map/pallas_call | solution.py:386
  3.4 0.8 collective-permute-start
  4.1 8.7 %collective-permute-start.8 = (f32[1168,128]{1,0:T(8,128)S(1)}, f32[1168,128]{1,0:T(8,128)S(1)}, u32[]{:S(2)}, u32[]{:S(2)}) collective-permute-start(f32[1168,128]{1,0:T(8,128)S(1)} %get-tuple-element.39), channel_id=1, source_target_pairs={{16,32},{32,16},{48,64},{64,48},{80,96},{96,80},{112,128},{128,112... | collective-permute-start | bytes 1794056 | tf_op jit(solution)/shard_map/ppermute | solution.py:402
  12.8 0.8 collective-permute-start.3
  13.7 3.7 %collective-permute-start.4 = (f32[248,128]{1,0:T(8,128)S(1)}, f32[248,128]{1,0:T(8,128)S(1)}, u32[]{:S(2)}, u32[]{:S(2)}) collective-permute-start(f32[248,128]{1,0:T(8,128)S(1)} %get-tuple-element.34), channel_id=1, source_target_pairs={{1,2},{2,1},{3,4},{4,3},{5,6},{6,5},{7,8},{8,7},{9,10},{10,9},{11,... | collective-permute-start | bytes 380936 | tf_op jit(solution)/shard_map/ppermute | solution.py:405
  17.4 2.5 %collective-permute-start.1 = (f32[200,128]{1,0:T(8,128)S(1)}, f32[200,128]{1,0:T(8,128)S(1)}, u32[]{:S(2)}, u32[]{:S(2)}) collective-permute-start(f32[200,128]{1,0:T(8,128)S(1)} %get-tuple-element.31), channel_id=1, source_target_pairs={{16,33},{17,32},{18,35},{19,34},{20,37},{21,36},{22,39},{23,38},{2... | collective-permute-start | bytes 307208 | tf_op jit(solution)/shard_map/ppermute | solution.py:406
  19.9 4.3 %collective-permute-start.2 = (f32[200,128]{1,0:T(8,128)S(1)}, f32[200,128]{1,0:T(8,128)S(1)}, u32[]{:S(2)}, u32[]{:S(2)}) collective-permute-start(f32[200,128]{1,0:T(8,128)S(1)} %get-tuple-element.32), channel_id=1, source_target_pairs={{17,34},{18,33},{19,36},{20,35},{21,38},{22,37},{23,40},{24,39},{2... | collective-permute-start | bytes 307208 | tf_op jit(solution)/shard_map/ppermute | solution.py:407
  24.2 20.3 %collective-permute-done.3.edge_a = f32[248,128]{1,0:T(8,128)S(1)} collective-permute-done((f32[248,128]{1,0:T(8,128)S(1)}, f32[248,128]{1,0:T(8,128)S(1)}, u32[]{:S(2)}, u32[]{:S(2)}) %collective-permute-start.3) | collective-permute-done | bytes 127008 | tf_op jit(solution)/shard_map/ppermute | solution.py:404
  44.5 3.6 %collective-permute-done.2.corner_b = f32[200,128]{1,0:T(8,128)S(1)} collective-permute-done((f32[200,128]{1,0:T(8,128)S(1)}, f32[200,128]{1,0:T(8,128)S(1)}, u32[]{:S(2)}, u32[]{:S(2)}) %collective-permute-start.2) | collective-permute-done | bytes 102432 | tf_op jit(solution)/shard_map/ppermute | solution.py:407
  48.1 4.9 %collective-permute-start.7 = (f32[576,128]{1,0:T(8,128)S(1)}, f32[576,128]{1,0:T(8,128)S(1)}, u32[]{:S(2)}, u32[]{:S(2)}) collective-permute-start(f32[576,128]{1,0:T(8,128)S(1)} %get-tuple-element.38), channel_id=1, source_target_pairs={{16,32},{32,16},{48,64},{64,48},{80,96},{96,80},{112,128},{128,112... | collective-permute-start | bytes 884744 | tf_op jit(solution)/shard_map/ppermute | solution.py:409
  53.0 3.4 %collective-permute-start.5 = (f32[248,128]{1,0:T(8,128)S(1)}, f32[248,128]{1,0:T(8,128)S(1)}, u32[]{:S(2)}, u32[]{:S(2)}) collective-permute-start(f32[248,128]{1,0:T(8,128)S(1)} %collective-permute-done.3.edge_a), channel_id=1, source_target_pairs={{0,16},{16,0},{32,48},{48,32},{64,80},{80,64},{96,112},{112,96},{1... | collective-permute-start | bytes 380936 | tf_op jit(solution)/shard_map/ppermute | solution.py:410
  56.4 0.1 collective-permute-start.6
  56.5 0.9 collective-permute-done.5.edgep_a
  57.4 0.4 collective-permute-done.6.edgep_b
  57.8 10.0 %shard_map.103 = (f32[3,2,256,128]{3,2,1,0:T(8,128)S(1)}, f32[72,384]{1,0:T(8,128)S(1)}, f32[2,8,8,384]{3,2,1,0:T(8,128)S(1)}) custom-call(s32[3]{0:T(128)S(1)} %pad_add_fusion.sc, f32[2320,128]{1,0:T(8,128)S(1)} %get-tuple-element.27.st, f32[2320,128]{1,0:T(8,128)S(1)} %collective-permute-done.stp, f32[248,128]{1,0:T(8,128)S(1)} %collective-permute-done.3.edge_a, ...), custom_call_target="tpu_custom_call" | custom-call | tf_op jit(solution)/shard_map/pallas_call | solution.py:416
  67.8 6.0 %shard_map.104 = (f32[4,8,384]{2,1,0:T(8,128)S(1)}, f32[3,2,128,128]{3,2,1,0:T(8,128)S(1)}, f32[72,384]{1,0:T(8,128)}, f32[2,8,8,384]{3,2,1,0:T(8,128)}) custom-call(s32[3]{0:T(128)S(1)} %pad_add_fusion.sc, f32[2320,128]{1,0:T(8,128)S(1)} %get-tuple-element.27.st, f32[2320,128]{1,0:T(8,128)S(1)} %collective-permute-done.stp, ...), custom_call_target="tpu_custom_call" | custom-call | tf_op jit(solution)/shard_map/pallas_call | solution.py:416
  73.8 2.2 %collective-permute-start.9 = (f32[4,8,384]{2,1,0:T(8,128)S(1)}, f32[4,8,384]{2,1,0:T(8,128)S(1)}, u32[]{:S(2)}, u32[]{:S(2)}) collective-permute-start(f32[4,8,384]{2,1,0:T(8,128)S(1)} %get-tuple-element.45.mine), channel_id=1, source_target_pairs={{0,16},{16,0},{32,48},{48,32},{64,80},{80,64},{96,112},{112,96},{1... | collective-permute-start | bytes 147464 | tf_op jit(solution)/shard_map/ppermute | solution.py:428
  76.0 0.9 collective-permute-done.9.pair
  76.9 1.9 %collective-permute-start.10 = (f32[2,4,8,384]{3,2,1,0:T(8,128)S(1)}, f32[2,4,8,384]{3,2,1,0:T(8,128)S(1)}, u32[]{:S(2)}, u32[]{:S(2)}) collective-permute-start(f32[2,4,8,384]{3,2,1,0:T(8,128)S(1)} %pad_maximum_fusion), channel_id=1, source_target_pairs={{16,32},{32,16},{48,64},{64,48},{80,96},{96,80},{112,128},{128,112... | collective-permute-start | bytes 294920 | tf_op jit(solution)/shard_map/ppermute | solution.py:429
  78.9 0.7 collective-permute-start.11
  79.5 8.6 %collective-permute-done.10.remote = f32[2,4,8,384]{3,2,1,0:T(8,128)S(1)} collective-permute-done((f32[2,4,8,384]{3,2,1,0:T(8,128)S(1)}, f32[2,4,8,384]{3,2,1,0:T(8,128)S(1)}, u32[]{:S(2)}, u32[]{:S(2)}) %collective-permute-start.10) | collective-permute-done | bytes 98336 | tf_op jit(solution)/shard_map/ppermute | solution.py:429
  88.1 1.4 %collective-permute-start.12 = (f32[2,4,8,384]{3,2,1,0:T(8,128)S(1)}, f32[2,4,8,384]{3,2,1,0:T(8,128)S(1)}, u32[]{:S(2)}, u32[]{:S(2)}) collective-permute-start(f32[2,4,8,384]{3,2,1,0:T(8,128)S(1)} %collective-permute-done.10.remote), channel_id=1, source_target_pairs={{0,16},{16,0},{32,48},{48,32},{64,80},{80,64},{96,112},{112,96},{1... | collective-permute-start | bytes 294920 | tf_op jit(solution)/shard_map/ppermute | solution.py:431
  89.5 0.9 collective-permute-done.12.remote_pair
  90.5 4.1 %shard_map.105 = (f32[48,8,256]{2,1,0:T(8,128)}, f32[48,8,256]{2,1,0:T(8,128)}, f32[48,8,256]{2,1,0:T(8,128)}, f32[8,256]{1,0:T(8,128)}) custom-call(s32[3]{0:T(128)S(1)} %pad_add_fusion.sc, f32[4,8,384]{2,1,0:T(8,128)S(1)} %get-tuple-element.45.mine, f32[4,8,384]{2,1,0:T(8,128)S(1)} %collective-permute-done.9.pair, ...), custom_call_target="tpu_custom_call" | custom-call | tf_op jit(solution)/shard_map/pallas_call | solution.py:432
  (8 shorter events, 0.1 us)
Async XLA Ops:
  3.4 14.0 %collective-permute-start = (f32[2320,128]{1,0:T(8,128)S(1)}, f32[2320,128]{1,0:T(8,128)S(1)}, u32[]{:S(2)}, u32[]{:S(2)}) collective-permute-start(f32[2320,128]{1,0:T(8,128)S(1)} %get-tuple-element.27.st), channel_id=1, source_target_pairs={{0,16},{16,0},{32,48},{48,32},{64,80},{80,64},{96,112},{112,96},{1... | collective-permute-start | bytes 3563528 | tf_op jit(solution)/shard_map/ppermute | solution.py:401
  4.1 52.4 %collective-permute-start.8 = (f32[1168,128]{1,0:T(8,128)S(1)}, f32[1168,128]{1,0:T(8,128)S(1)}, u32[]{:S(2)}, u32[]{:S(2)}) collective-permute-start(f32[1168,128]{1,0:T(8,128)S(1)} %get-tuple-element.39), channel_id=1, source_target_pairs={{16,32},{32,16},{48,64},{64,48},{80,96},{96,80},{112,128},{128,112... | collective-permute-start | bytes 1794056 | tf_op jit(solution)/shard_map/ppermute | solution.py:402
  12.8 31.6 %collective-permute-start.3 = (f32[248,128]{1,0:T(8,128)S(1)}, f32[248,128]{1,0:T(8,128)S(1)}, u32[]{:S(2)}, u32[]{:S(2)}) collective-permute-start(f32[248,128]{1,0:T(8,128)S(1)} %get-tuple-element.33), channel_id=1, source_target_pairs={{0,1},{1,0},{2,3},{3,2},{4,5},{5,4},{6,7},{7,6},{8,9},{9,8},{10,11... | collective-permute-start | bytes 380936 | tf_op jit(solution)/shard_map/ppermute | solution.py:404
  13.7 30.8 %collective-permute-start.4 = (f32[248,128]{1,0:T(8,128)S(1)}, f32[248,128]{1,0:T(8,128)S(1)}, u32[]{:S(2)}, u32[]{:S(2)}) collective-permute-start(f32[248,128]{1,0:T(8,128)S(1)} %get-tuple-element.34), channel_id=1, source_target_pairs={{1,2},{2,1},{3,4},{4,3},{5,6},{6,5},{7,8},{8,7},{9,10},{10,9},{11,... | collective-permute-start | bytes 380936 | tf_op jit(solution)/shard_map/ppermute | solution.py:405
  17.4 27.1 %collective-permute-start.1 = (f32[200,128]{1,0:T(8,128)S(1)}, f32[200,128]{1,0:T(8,128)S(1)}, u32[]{:S(2)}, u32[]{:S(2)}) collective-permute-start(f32[200,128]{1,0:T(8,128)S(1)} %get-tuple-element.31), channel_id=1, source_target_pairs={{16,33},{17,32},{18,35},{19,34},{20,37},{21,36},{22,39},{23,38},{2... | collective-permute-start | bytes 307208 | tf_op jit(solution)/shard_map/ppermute | solution.py:406
  19.9 28.2 %collective-permute-start.2 = (f32[200,128]{1,0:T(8,128)S(1)}, f32[200,128]{1,0:T(8,128)S(1)}, u32[]{:S(2)}, u32[]{:S(2)}) collective-permute-start(f32[200,128]{1,0:T(8,128)S(1)} %get-tuple-element.32), channel_id=1, source_target_pairs={{17,34},{18,33},{19,36},{20,35},{21,38},{22,37},{23,40},{24,39},{2... | collective-permute-start | bytes 307208 | tf_op jit(solution)/shard_map/ppermute | solution.py:407
  48.1 19.7 %collective-permute-start.7 = (f32[576,128]{1,0:T(8,128)S(1)}, f32[576,128]{1,0:T(8,128)S(1)}, u32[]{:S(2)}, u32[]{:S(2)}) collective-permute-start(f32[576,128]{1,0:T(8,128)S(1)} %get-tuple-element.38), channel_id=1, source_target_pairs={{16,32},{32,16},{48,64},{64,48},{80,96},{96,80},{112,128},{128,112... | collective-permute-start | bytes 884744 | tf_op jit(solution)/shard_map/ppermute | solution.py:409
  53.0 4.4 %collective-permute-start.5 = (f32[248,128]{1,0:T(8,128)S(1)}, f32[248,128]{1,0:T(8,128)S(1)}, u32[]{:S(2)}, u32[]{:S(2)}) collective-permute-start(f32[248,128]{1,0:T(8,128)S(1)} %collective-permute-done.3.edge_a), channel_id=1, source_target_pairs={{0,16},{16,0},{32,48},{48,32},{64,80},{80,64},{96,112},{112,96},{1... | collective-permute-start | bytes 380936 | tf_op jit(solution)/shard_map/ppermute | solution.py:410
  56.4 1.3 %collective-permute-start.6 = (f32[248,128]{1,0:T(8,128)S(1)}, f32[248,128]{1,0:T(8,128)S(1)}, u32[]{:S(2)}, u32[]{:S(2)}) collective-permute-start(f32[248,128]{1,0:T(8,128)S(1)} %collective-permute-done.4.edge_b), channel_id=1, source_target_pairs={{0,16},{16,0},{32,48},{48,32},{64,80},{80,64},{96,112},{112,96},{1... | collective-permute-start | bytes 380936 | tf_op jit(solution)/shard_map/ppermute | solution.py:411
  73.8 3.1 %collective-permute-start.9 = (f32[4,8,384]{2,1,0:T(8,128)S(1)}, f32[4,8,384]{2,1,0:T(8,128)S(1)}, u32[]{:S(2)}, u32[]{:S(2)}) collective-permute-start(f32[4,8,384]{2,1,0:T(8,128)S(1)} %get-tuple-element.45.mine), channel_id=1, source_target_pairs={{0,16},{16,0},{32,48},{48,32},{64,80},{80,64},{96,112},{112,96},{1... | collective-permute-start | bytes 147464 | tf_op jit(solution)/shard_map/ppermute | solution.py:428
  76.9 11.2 %collective-permute-start.10 = (f32[2,4,8,384]{3,2,1,0:T(8,128)S(1)}, f32[2,4,8,384]{3,2,1,0:T(8,128)S(1)}, u32[]{:S(2)}, u32[]{:S(2)}) collective-permute-start(f32[2,4,8,384]{3,2,1,0:T(8,128)S(1)} %pad_maximum_fusion), channel_id=1, source_target_pairs={{16,32},{32,16},{48,64},{64,48},{80,96},{96,80},{112,128},{128,112... | collective-permute-start | bytes 294920 | tf_op jit(solution)/shard_map/ppermute | solution.py:429
  78.9 0.7 collective-permute-start.11
  88.1 2.3 %collective-permute-start.12 = (f32[2,4,8,384]{3,2,1,0:T(8,128)S(1)}, f32[2,4,8,384]{3,2,1,0:T(8,128)S(1)}, u32[]{:S(2)}, u32[]{:S(2)}) collective-permute-start(f32[2,4,8,384]{3,2,1,0:T(8,128)S(1)} %collective-permute-done.10.remote), channel_id=1, source_target_pairs={{0,16},{16,0},{32,48},{48,32},{64,80},{80,64},{96,112},{112,96},{1... | collective-permute-start | bytes 294920 | tf_op jit(solution)/shard_map/ppermute | solution.py:431

commit v4 on v3

--- a/solution.py
+++ b/solution.py
@@ -399,14 +399,12 @@
     mains = packed[:CHUNKS]
     st, plane = packed[CHUNKS:]
     stp = lax.ppermute(st, "gx", on_chip)
-    main = [lax.ppermute(mains[0], "gx", next_chip)]
-    stp, corner_a, corner_b = lax.optimization_barrier((stp, corner_a, corner_b))
     edge_a = lax.ppermute(edge_a, "gy", even)
     edge_b = lax.ppermute(edge_b, "gy", odd)
     corner_a = lax.ppermute(corner_a, ("gx", "gy"), both(next_chip, even))
     corner_b = lax.ppermute(corner_b, ("gx", "gy"), both(next_chip, odd))
-    corner_a, corner_b, edge_a, edge_b, *later = lax.optimization_barrier((corner_a, corner_b, edge_a, edge_b, *mains[1:]))
-    main += [lax.ppermute(m, "gx", next_chip) for m in later]
+    edge_a, edge_b, corner_a, corner_b, stp, *mains = lax.optimization_barrier((edge_a, edge_b, corner_a, corner_b, stp, *mains))
+    main = [lax.ppermute(m, "gx", next_chip) for m in mains]
     edgep_a = lax.ppermute(edge_a, "gx", on_chip)
     edgep_b = lax.ppermute(edge_b, "gx", on_chip)
 

time: 95.3 us -> 103 us (1.081)
  starting transfers between devices: 35.4 us -> 52.2 us
  waiting for transfers between devices: 35.6 us -> 25.9 us
    ppermute x1, waiting for transfers between devices: 20.3 us -> 0.01 us  [local(): edge_a = lax.ppermute(edge_a, 'gy', even)]
    ppermute x1, starting transfers between devices: 2.24 us -> 16.4 us  [local(): pair = lax.ppermute(flows, 'gx', on_chip)]
    ppermute x2, waiting for transfers between devices: 0.01 us -> 9.76 us  [local(): main = [lax.ppermute(m, 'gx', next_chip) for m in mains]]
    ppermute x1, waiting for transfers between devices: 0.01 us -> 4.59 us  [local(): corner_a = lax.ppermute(corner_a, ('gx', 'gy'), both(next_chip, even))]
    ppermute x2, starting transfers between devices: 13.6 us -> 9.58 us  [local(): main = [lax.ppermute(m, 'gx', next_chip) for m in mains]]
    ppermute x1, starting transfers between devices: 2.48 us -> 5.87 us  [local(): corner_a = lax.ppermute(corner_a, ('gx', 'gy'), both(next_chip, even))]
    ppermute x1, starting transfers between devices: 3.4 us -> 6.19 us  [local(): edgep_a = lax.ppermute(edge_a, 'gx', on_chip)]
    ppermute x1, waiting for transfers between devices: 3.62 us -> 0.98 us  [local(): corner_b = lax.ppermute(corner_b, ('gx', 'gy'), both(next_chip, odd))]
  transfers between devices with their start and end apart: 13 -> 13, of which waited for: 7 -> 8; matrix products, arithmetic and copies ran while one was open for 0% -> 0% of each run, Pallas kernels for 11% -> 10%
where the time goes in v4:
time: 103 us; the launch traced here: 102 us
  starting transfers between devices  52.2 us (51%)
  waiting for transfers between devices  25.9 us (25%)
  Pallas kernels  22.8 us (22%)
    ppermute x1, starting transfers between devices, local(): pair = lax.ppermute(flows, 'gx', on_chip)  16.4 us
    pallas_call x2, Pallas kernels, local(): call(functools.partial(rk_kernel, c), [(4, ROWS, WIDE)] * (c == CHUNKS -...  16 us
    ppermute x2, waiting for transfers between devices, local(): main = [lax.ppermute(m, 'gx', next_chip) for m in mains]  9.76 us
    ppermute x2, starting transfers between devices, local(): main = [lax.ppermute(m, 'gx', next_chip) for m in mains]  9.58 us
    ppermute x1, waiting for transfers between devices, local(): remote = lax.ppermute(jnp.stack([flows, pair]), 'gx', next_chip)  7.53 us
    ppermute x1, starting transfers between devices, local(): edgep_a = lax.ppermute(edge_a, 'gx', on_chip)  6.19 us
    ppermute x1, starting transfers between devices, local(): corner_a = lax.ppermute(corner_a, ('gx', 'gy'), both(next_chip, even))  5.87 us
    ppermute x1, starting transfers between devices, local(): edge_b = lax.ppermute(edge_b, 'gy', odd)  4.77 us
  transfers between devices with their start and end apart: 13, of which 8 were waited for; matrix products, arithmetic and copies ran while one was open for 0% of the time, Pallas kernels for 10%

profile of v4, /device:TPU:31, one launch (start us, length us, event | category | flops | bytes accessed | tf_op | source)
XLA Modules:
  0.0 101.7 jit_solution(13926794615500277124)
XLA Ops:
  0.7 2.6 %shard_map.102 = (f32[248,128]{1,0:T(8,128)S(1)}, f32[248,128]{1,0:T(8,128)S(1)}, f32[200,128]{1,0:T(8,128)S(1)}, f32[200,128]{1,0:T(8,128)S(1)}, f32[1168,128]{...) custom-call(s32[3]{0:T(128)S(1)} %pad_add_fusion.sc, ...), custom_call_target="tpu_custom_call" | custom-call | tf_op jit(solution)/shard_map/pallas_call | solution.py:386
  3.4 0.8 collective-permute-start.4
  4.1 1.7 %collective-permute-start = (f32[248,128]{1,0:T(8,128)S(1)}, f32[248,128]{1,0:T(8,128)S(1)}, u32[]{:S(2)}, u32[]{:S(2)}) collective-permute-start(f32[248,128]{1,0:T(8,128)S(1)} %get-tuple-element.27), channel_id=1, source_target_pairs={{0,1},{1,0},{2,3},{3,2},{4,5},{5,4},{6,7},{7,6},{8,9},{9,8},{10,11... | collective-permute-start | bytes 380936 | tf_op jit(solution)/shard_map/ppermute | solution.py:402
  5.8 4.8 %collective-permute-start.1 = (f32[248,128]{1,0:T(8,128)S(1)}, f32[248,128]{1,0:T(8,128)S(1)}, u32[]{:S(2)}, u32[]{:S(2)}) collective-permute-start(f32[248,128]{1,0:T(8,128)S(1)} %get-tuple-element.28), channel_id=1, source_target_pairs={{1,2},{2,1},{3,4},{4,3},{5,6},{6,5},{7,8},{8,7},{9,10},{10,9},{11,... | collective-permute-start | bytes 380936 | tf_op jit(solution)/shard_map/ppermute | solution.py:403
  10.5 5.9 %collective-permute-start.2 = (f32[200,128]{1,0:T(8,128)S(1)}, f32[200,128]{1,0:T(8,128)S(1)}, u32[]{:S(2)}, u32[]{:S(2)}) collective-permute-start(f32[200,128]{1,0:T(8,128)S(1)} %get-tuple-element.29), channel_id=1, source_target_pairs={{16,33},{17,32},{18,35},{19,34},{20,37},{21,36},{22,39},{23,38},{2... | collective-permute-start | bytes 307208 | tf_op jit(solution)/shard_map/ppermute | solution.py:404
  16.4 2.8 %collective-permute-start.3 = (f32[200,128]{1,0:T(8,128)S(1)}, f32[200,128]{1,0:T(8,128)S(1)}, u32[]{:S(2)}, u32[]{:S(2)}) collective-permute-start(f32[200,128]{1,0:T(8,128)S(1)} %get-tuple-element.30), channel_id=1, source_target_pairs={{17,34},{18,33},{19,36},{20,35},{21,38},{22,37},{23,40},{24,39},{2... | collective-permute-start | bytes 307208 | tf_op jit(solution)/shard_map/ppermute | solution.py:405
  19.2 4.6 %collective-permute-done.2.corner_a = f32[200,128]{1,0:T(8,128)S(1)} collective-permute-done((f32[200,128]{1,0:T(8,128)S(1)}, f32[200,128]{1,0:T(8,128)S(1)}, u32[]{:S(2)}, u32[]{:S(2)}) %collective-permute-start.2) | collective-permute-done | bytes 102432 | tf_op jit(solution)/shard_map/ppermute | solution.py:404
  23.8 1.0 collective-permute-done.3.corner_b
  24.8 7.7 %collective-permute-start.8 = (f32[1168,128]{1,0:T(8,128)S(1)}, f32[1168,128]{1,0:T(8,128)S(1)}, u32[]{:S(2)}, u32[]{:S(2)}) collective-permute-start(f32[1168,128]{1,0:T(8,128)S(1)} %get-tuple-element.37), channel_id=1, source_target_pairs={{16,32},{32,16},{48,64},{64,48},{80,96},{96,80},{112,128},{128,112... | collective-permute-start | bytes 1794056 | tf_op jit(solution)/shard_map/ppermute | solution.py:407
  32.5 1.9 %collective-permute-start.7 = (f32[576,128]{1,0:T(8,128)S(1)}, f32[576,128]{1,0:T(8,128)S(1)}, u32[]{:S(2)}, u32[]{:S(2)}) collective-permute-start(f32[576,128]{1,0:T(8,128)S(1)} %get-tuple-element.36), channel_id=1, source_target_pairs={{16,32},{32,16},{48,64},{64,48},{80,96},{96,80},{112,128},{128,112... | collective-permute-start | bytes 884744 | tf_op jit(solution)/shard_map/ppermute | solution.py:407
  34.4 6.2 %collective-permute-start.5 = (f32[248,128]{1,0:T(8,128)S(1)}, f32[248,128]{1,0:T(8,128)S(1)}, u32[]{:S(2)}, u32[]{:S(2)}) collective-permute-start(f32[248,128]{1,0:T(8,128)S(1)} %collective-permute-done.edge_a), channel_id=1, source_target_pairs={{0,16},{16,0},{32,48},{48,32},{64,80},{80,64},{96,112},{112,96},{1... | collective-permute-start | bytes 380936 | tf_op jit(solution)/shard_map/ppermute | solution.py:408
  40.7 0.9 collective-permute-done.5.edgep_a
  41.6 0.4 collective-permute-done.6.edgep_b
  42.0 9.8 %collective-permute-done.8.main.main0 = f32[1168,128]{1,0:T(8,128)S(1)} collective-permute-done((f32[1168,128]{1,0:T(8,128)S(1)}, f32[1168,128]{1,0:T(8,128)S(1)}, u32[]{:S(2)}, u32[]{:S(2)}) %collective-permute-start.8) | collective-permute-done | bytes 598048 | tf_op jit(solution)/shard_map/ppermute | solution.py:407
  51.7 10.0 %shard_map.103 = (f32[3,2,256,128]{3,2,1,0:T(8,128)S(1)}, f32[72,384]{1,0:T(8,128)S(1)}, f32[2,8,8,384]{3,2,1,0:T(8,128)S(1)}) custom-call(s32[3]{0:T(128)S(1)} %pad_add_fusion.sc, f32[2320,128]{1,0:T(8,128)S(1)} %get-tuple-element.26.st, f32[2320,128]{1,0:T(8,128)S(1)} %collective-permute-done.4.stp, f32[248,128]{1,0:T(8,128)S(1)} %collective-permute-done.edge_a, ...), custom_call_target="tpu_custom_call" | custom-call | tf_op jit(solution)/shard_map/pallas_call | solution.py:414
  61.7 6.0 %shard_map.104 = (f32[4,8,384]{2,1,0:T(8,128)S(1)}, f32[3,2,128,128]{3,2,1,0:T(8,128)S(1)}, f32[72,384]{1,0:T(8,128)}, f32[2,8,8,384]{3,2,1,0:T(8,128)}) custom-call(s32[3]{0:T(128)S(1)} %pad_add_fusion.sc, f32[2320,128]{1,0:T(8,128)S(1)} %get-tuple-element.26.st, f32[2320,128]{1,0:T(8,128)S(1)} %collective-permute-done.4.stp, ...), custom_call_target="tpu_custom_call" | custom-call | tf_op jit(solution)/shard_map/pallas_call | solution.py:414
  67.7 16.4 %collective-permute-start.9 = (f32[4,8,384]{2,1,0:T(8,128)S(1)}, f32[4,8,384]{2,1,0:T(8,128)S(1)}, u32[]{:S(2)}, u32[]{:S(2)}) collective-permute-start(f32[4,8,384]{2,1,0:T(8,128)S(1)} %get-tuple-element.43.mine), channel_id=1, source_target_pairs={{0,16},{16,0},{32,48},{48,32},{64,80},{80,64},{96,112},{112,96},{1... | collective-permute-start | bytes 147464 | tf_op jit(solution)/shard_map/ppermute | solution.py:426
  84.2 0.9 collective-permute-done.9.pair
  85.1 1.9 %collective-permute-start.10 = (f32[2,4,8,384]{3,2,1,0:T(8,128)S(1)}, f32[2,4,8,384]{3,2,1,0:T(8,128)S(1)}, u32[]{:S(2)}, u32[]{:S(2)}) collective-permute-start(f32[2,4,8,384]{3,2,1,0:T(8,128)S(1)} %pad_maximum_fusion), channel_id=1, source_target_pairs={{16,32},{32,16},{48,64},{64,48},{80,96},{96,80},{112,128},{128,112... | collective-permute-start | bytes 294920 | tf_op jit(solution)/shard_map/ppermute | solution.py:427
  87.0 0.7 collective-permute-start.11
  87.7 7.5 %collective-permute-done.10.remote = f32[2,4,8,384]{3,2,1,0:T(8,128)S(1)} collective-permute-done((f32[2,4,8,384]{3,2,1,0:T(8,128)S(1)}, f32[2,4,8,384]{3,2,1,0:T(8,128)S(1)}, u32[]{:S(2)}, u32[]{:S(2)}) %collective-permute-start.10) | collective-permute-done | bytes 98336 | tf_op jit(solution)/shard_map/ppermute | solution.py:427
  95.2 1.5 %collective-permute-start.12 = (f32[2,4,8,384]{3,2,1,0:T(8,128)S(1)}, f32[2,4,8,384]{3,2,1,0:T(8,128)S(1)}, u32[]{:S(2)}, u32[]{:S(2)}) collective-permute-start(f32[2,4,8,384]{3,2,1,0:T(8,128)S(1)} %collective-permute-done.10.remote), channel_id=1, source_target_pairs={{0,16},{16,0},{32,48},{48,32},{64,80},{80,64},{96,112},{112,96},{1... | collective-permute-start | bytes 294920 | tf_op jit(solution)/shard_map/ppermute | solution.py:429
  96.6 0.9 collective-permute-done.12.remote_pair
  97.6 4.1 %shard_map.105 = (f32[48,8,256]{2,1,0:T(8,128)}, f32[48,8,256]{2,1,0:T(8,128)}, f32[48,8,256]{2,1,0:T(8,128)}, f32[8,256]{1,0:T(8,128)}) custom-call(s32[3]{0:T(128)S(1)} %pad_add_fusion.sc, f32[4,8,384]{2,1,0:T(8,128)S(1)} %get-tuple-element.43.mine, f32[4,8,384]{2,1,0:T(8,128)S(1)} %collective-permute-done.9.pair, ...), custom_call_target="tpu_custom_call" | custom-call | tf_op jit(solution)/shard_map/pallas_call | solution.py:430
  (8 shorter events, 0.2 us)
Async XLA Ops:
  3.4 21.5 %collective-permute-start.4 = (f32[2320,128]{1,0:T(8,128)S(1)}, f32[2320,128]{1,0:T(8,128)S(1)}, u32[]{:S(2)}, u32[]{:S(2)}) collective-permute-start(f32[2320,128]{1,0:T(8,128)S(1)} %get-tuple-element.26.st), channel_id=1, source_target_pairs={{0,16},{16,0},{32,48},{48,32},{64,80},{80,64},{96,112},{112,96},{1... | collective-permute-start | bytes 3563528 | tf_op jit(solution)/shard_map/ppermute | solution.py:401
  4.1 20.7 %collective-permute-start = (f32[248,128]{1,0:T(8,128)S(1)}, f32[248,128]{1,0:T(8,128)S(1)}, u32[]{:S(2)}, u32[]{:S(2)}) collective-permute-start(f32[248,128]{1,0:T(8,128)S(1)} %get-tuple-element.27), channel_id=1, source_target_pairs={{0,1},{1,0},{2,3},{3,2},{4,5},{5,4},{6,7},{7,6},{8,9},{9,8},{10,11... | collective-permute-start | bytes 380936 | tf_op jit(solution)/shard_map/ppermute | solution.py:402
  5.8 19.0 %collective-permute-start.1 = (f32[248,128]{1,0:T(8,128)S(1)}, f32[248,128]{1,0:T(8,128)S(1)}, u32[]{:S(2)}, u32[]{:S(2)}) collective-permute-start(f32[248,128]{1,0:T(8,128)S(1)} %get-tuple-element.28), channel_id=1, source_target_pairs={{1,2},{2,1},{3,4},{4,3},{5,6},{6,5},{7,8},{8,7},{9,10},{10,9},{11,... | collective-permute-start | bytes 380936 | tf_op jit(solution)/shard_map/ppermute | solution.py:403
  10.5 13.3 %collective-permute-start.2 = (f32[200,128]{1,0:T(8,128)S(1)}, f32[200,128]{1,0:T(8,128)S(1)}, u32[]{:S(2)}, u32[]{:S(2)}) collective-permute-start(f32[200,128]{1,0:T(8,128)S(1)} %get-tuple-element.29), channel_id=1, source_target_pairs={{16,33},{17,32},{18,35},{19,34},{20,37},{21,36},{22,39},{23,38},{2... | collective-permute-start | bytes 307208 | tf_op jit(solution)/shard_map/ppermute | solution.py:404
  16.4 8.4 %collective-permute-start.3 = (f32[200,128]{1,0:T(8,128)S(1)}, f32[200,128]{1,0:T(8,128)S(1)}, u32[]{:S(2)}, u32[]{:S(2)}) collective-permute-start(f32[200,128]{1,0:T(8,128)S(1)} %get-tuple-element.30), channel_id=1, source_target_pairs={{17,34},{18,33},{19,36},{20,35},{21,38},{22,37},{23,40},{24,39},{2... | collective-permute-start | bytes 307208 | tf_op jit(solution)/shard_map/ppermute | solution.py:405
  24.8 26.9 %collective-permute-start.8 = (f32[1168,128]{1,0:T(8,128)S(1)}, f32[1168,128]{1,0:T(8,128)S(1)}, u32[]{:S(2)}, u32[]{:S(2)}) collective-permute-start(f32[1168,128]{1,0:T(8,128)S(1)} %get-tuple-element.37), channel_id=1, source_target_pairs={{16,32},{32,16},{48,64},{64,48},{80,96},{96,80},{112,128},{128,112... | collective-permute-start | bytes 1794056 | tf_op jit(solution)/shard_map/ppermute | solution.py:407
  32.5 29.2 %collective-permute-start.7 = (f32[576,128]{1,0:T(8,128)S(1)}, f32[576,128]{1,0:T(8,128)S(1)}, u32[]{:S(2)}, u32[]{:S(2)}) collective-permute-start(f32[576,128]{1,0:T(8,128)S(1)} %get-tuple-element.36), channel_id=1, source_target_pairs={{16,32},{32,16},{48,64},{64,48},{80,96},{96,80},{112,128},{128,112... | collective-permute-start | bytes 884744 | tf_op jit(solution)/shard_map/ppermute | solution.py:407
  34.4 7.2 %collective-permute-start.5 = (f32[248,128]{1,0:T(8,128)S(1)}, f32[248,128]{1,0:T(8,128)S(1)}, u32[]{:S(2)}, u32[]{:S(2)}) collective-permute-start(f32[248,128]{1,0:T(8,128)S(1)} %collective-permute-done.edge_a), channel_id=1, source_target_pairs={{0,16},{16,0},{32,48},{48,32},{64,80},{80,64},{96,112},{112,96},{1... | collective-permute-start | bytes 380936 | tf_op jit(solution)/shard_map/ppermute | solution.py:408
  40.6 1.3 %collective-permute-start.6 = (f32[248,128]{1,0:T(8,128)S(1)}, f32[248,128]{1,0:T(8,128)S(1)}, u32[]{:S(2)}, u32[]{:S(2)}) collective-permute-start(f32[248,128]{1,0:T(8,128)S(1)} %collective-permute-done.1.edge_b), channel_id=1, source_target_pairs={{0,16},{16,0},{32,48},{48,32},{64,80},{80,64},{96,112},{112,96},{1... | collective-permute-start | bytes 380936 | tf_op jit(solution)/shard_map/ppermute | solution.py:409
  67.7 17.3 %collective-permute-start.9 = (f32[4,8,384]{2,1,0:T(8,128)S(1)}, f32[4,8,384]{2,1,0:T(8,128)S(1)}, u32[]{:S(2)}, u32[]{:S(2)}) collective-permute-start(f32[4,8,384]{2,1,0:T(8,128)S(1)} %get-tuple-element.43.mine), channel_id=1, source_target_pairs={{0,16},{16,0},{32,48},{48,32},{64,80},{80,64},{96,112},{112,96},{1... | collective-permute-start | bytes 147464 | tf_op jit(solution)/shard_map/ppermute | solution.py:426
  85.1 10.1 %collective-permute-start.10 = (f32[2,4,8,384]{3,2,1,0:T(8,128)S(1)}, f32[2,4,8,384]{3,2,1,0:T(8,128)S(1)}, u32[]{:S(2)}, u32[]{:S(2)}) collective-permute-start(f32[2,4,8,384]{3,2,1,0:T(8,128)S(1)} %pad_maximum_fusion), channel_id=1, source_target_pairs={{16,32},{32,16},{48,64},{64,48},{80,96},{96,80},{112,128},{128,112... | collective-permute-start | bytes 294920 | tf_op jit(solution)/shard_map/ppermute | solution.py:427
  87.0 0.7 collective-permute-start.11
  95.2 2.4 %collective-permute-start.12 = (f32[2,4,8,384]{3,2,1,0:T(8,128)S(1)}, f32[2,4,8,384]{3,2,1,0:T(8,128)S(1)}, u32[]{:S(2)}, u32[]{:S(2)}) collective-permute-start(f32[2,4,8,384]{3,2,1,0:T(8,128)S(1)} %collective-permute-done.10.remote), channel_id=1, source_target_pairs={{0,16},{16,0},{32,48},{48,32},{64,80},{80,64},{96,112},{112,96},{1... | collective-permute-start | bytes 294920 | tf_op jit(solution)/shard_map/ppermute | solution.py:429

commit v5 on v3

v5 whole, which is shorter than its diff:
```python
import jax
import jax.numpy as jnp
from jax import lax
from jax.experimental import pallas as pl
from jax.experimental.pallas import tpu as pltpu
from jax.sharding import PartitionSpec as P

ITERS = 16
TIME_STEP = 0.2
CORIOLIS = 0.3
PRESS_COEF = 0.05
VISCOSITY = 0.1
DIFFUSIVITY = 0.1
SIGMA_SHIFT = 0.25
CHEB_CENTER = 3.625
CHEB_HALF = 3.375
DIVERGENCE_COEF = 8.0

LEV = 48
ROWS = 8
COLS = 256
EXT = 128
WIDE = COLS + EXT
HALO = 6
SIZES = (48,)
CHUNKS = len(SIZES)
STARTS = tuple(sum(SIZES[:c]) for c in range(CHUNKS))
TILES = LEV // 8
SLOT = 25
SLOTS = 5
EDGE_TILES = -(-3 * ROWS // SLOTS)
CORNER_TILES = -(-3 * HALO // SLOTS)
F32 = jnp.float32


def cheb_table(count):
    first = CHEB_CENTER / CHEB_HALF
    ratio = 1.0 / first
    keeps = []
    gains = []
    for index in range(count):
        ratio_next = 1.0 / (2.0 * first - ratio)
        keeps.append(ratio_next * ratio)
        gains.append(2.0 * ratio_next / CHEB_HALF)
        ratio = ratio_next
    return (keeps, gains)


def lanes(shape):
    return lax.broadcasted_iota(jnp.int32, shape, len(shape) - 1)


def place(low, high, units, slot):
    left, right = units
    lane = lanes(low.shape)
    here = (lane >= SLOT * slot) & (lane < SLOT * slot + SLOT)
    low = low if slot == 0 else pltpu.roll(low, SLOT * slot, 1)
    high = pltpu.roll(high, SLOT * slot + SLOT, 1)
    return jnp.where(here, low, left), jnp.where(here, high, right)


def unpack(high, low, slot):
    lane = lanes(high.shape)
    high = high if slot == 0 else pltpu.roll(high, 128 - SLOT * slot, 1)
    low = pltpu.roll(low, 128 - SLOT - SLOT * slot, 1)
    return jnp.where(lane < SLOT, high, jnp.where(lane >= 128 - SLOT, low, 0.0))


def ordered(first, second, flag):
    odd = jnp.full(first.shape, flag, jnp.int32) == 1
    return jnp.where(odd, second, first), jnp.where(odd, first, second)


def pack_kernel(sc, u, v, s, wet, act, surf, depth, edge_a, edge_b, corner_a, corner_b, *rest):
    mains = rest[:CHUNKS]
    st, plane = rest[CHUNKS : CHUNKS + 2]
    buffers = rest[CHUNKS + 2 : CHUNKS + 9]
    sems = rest[CHUNKS + 9]
    core = sc[1]
    north_odd = sc[2]
    sources = (wet, act, surf, depth, u, v, s)
    copies = [pltpu.make_async_copy(a, b, sems.at[i]) for i, (a, b) in enumerate(zip(sources, buffers))]
    for copy in copies:
        copy.start()
    for copy in copies[:4]:
        copy.wait()
    wet, act, surf, depth, *cubes = buffers
    count = (act[...] * wet[...]).astype(F32)
    plane[0] = surf[...]
    plane[1] = count
    plane[2] = depth[...]
    for f in range(3):
        copies[4 + f].wait()
        for lev in range(LEV):
            tile = jnp.where(count > lev, cubes[f][lev], 0.0)
            spot = 8 * (lev % TILES) + lev // TILES
            for h in range(2):
                st[pl.ds((2 * f + h) * ROWS * LEV + spot, ROWS, stride=LEV), :] = tile[:, h * 128 : (h + 1) * 128]
    base = 2 * core
    for c in range(CHUNKS):
        levels = SIZES[c]
        for f in range(3):
            for j in range(HALO):
                for h in range(2):
                    start = pl.multiple_of(((2 * f + h) * ROWS + base + j) * LEV + STARTS[c], 8)
                    at = ((2 * f + h) * HALO + j) * levels
                    mains[c][at : at + levels, :] = st[pl.ds(start, levels), :]
    for h in range(2):
        at = 6 * HALO * SIZES[0] + 8 * h
        mains[0][at : at + 8, :] = count[:, 128 * h : 128 * h + 128]
        at = 6 * ROWS * LEV + 8 * h
        st[at : at + 8, :] = count[:, 128 * h : 128 * h + 128]
    blank = jnp.zeros((LEV, 128), F32)
    for tiles, rows, first, a, b in (
        (EDGE_TILES, ROWS, 0, edge_a, edge_b),
        (CORNER_TILES, HALO, base, corner_a, corner_b),
    ):
        for g in range(tiles):
            units = (blank, blank)
            for slot in range(min(SLOTS, 3 * rows - SLOTS * g)):
                f, r = divmod(SLOTS * g + slot, rows)
                low = pl.multiple_of((2 * f * ROWS + first + r) * LEV, 8)
                high = pl.multiple_of(((2 * f + 1) * ROWS + first + r) * LEV, 8)
                units = place(st[pl.ds(low, LEV), :], st[pl.ds(high, LEV), :], units, slot)
            b[g * LEV : g * LEV + LEV, :], a[g * LEV : g * LEV + LEV, :] = ordered(*units, north_odd)
    units = (blank[:ROWS], blank[:ROWS])
    for slot, field in enumerate((surf[...], count, depth[...])):
        units = place(field[:, :128], field[:, 128:], units, slot)
    left, right = ordered(*units, north_odd)
    for tiles, a, b in ((EDGE_TILES, edge_a, edge_b), (CORNER_TILES, corner_a, corner_b)):
        b[tiles * LEV :, :] = left
        a[tiles * LEV :, :] = right


def shifts(q):
    return (
        pltpu.roll(q, WIDE - 1, 1),
        pltpu.roll(q, 1, 1),
        pltpu.roll(q, WIDE - 2, 1),
        pltpu.roll(q, 2, 1),
    )


def before(x, sub):
    total = x
    for step in (1, 2, 4):
        total = total + jnp.where(sub >= step, pltpu.roll(total, step, 0), 0.0)
    return total - x


def rk_kernel(sc, st, stp, edge_a, edge_b, edgep_a, edgep_b, *rest):
    mains = rest[:CHUNKS]
    corner_a, corner_b, plane, flows, east, north, salt, ext, one, two, counts, flat, remote, runs = rest[CHUNKS:]
    core = sc[1]
    north_odd = sc[2]
    beside = 16 * (1 - core)
    beyond = 2 + 14 * core
    for source, first in ((st, ROWS), (stp, beside)):
        for f in range(3):
            for r in range(ROWS):
                for h in range(2):
                    at = ((2 * f + h) * ROWS + r) * LEV
                    ext[f, first + r, :, h * 128 : (h + 1) * 128] = source[at : at + LEV, :]
    for f in range(3):
        for j in range(HALO):
            for h in range(2):
                for main, levels, lev0 in zip(mains, SIZES, STARTS):
                    at = ((2 * f + h) * HALO + j) * levels
                    ext[f, beyond + j, lev0 : lev0 + levels, h * 128 : (h + 1) * 128] = main[at : at + levels, :]
    for tiles, rows, first, a, b in (
        (EDGE_TILES, ROWS, ROWS, edge_a, edge_b),
        (EDGE_TILES, ROWS, beside, edgep_a, edgep_b),
        (CORNER_TILES, HALO, beyond, corner_a, corner_b),
    ):
        for g in range(tiles):
            here = slice(g * LEV, g * LEV + LEV)
            high, low = ordered(a[here, :], b[here, :], north_odd)
            for slot in range(min(SLOTS, 3 * rows - SLOTS * g)):
                f, r = divmod(SLOTS * g + slot, rows)
                ext[f, first + r, :, COLS:] = unpack(high, low, slot)

    def beyond_plane(tiles, a, b, slot):
        high, low = ordered(a[tiles * LEV :, :], b[tiles * LEV :, :], north_odd)
        return unpack(high, low, slot)

    for f in range(3):
        flat[f, :, :COLS] = plane[f]
        flat[f, :, COLS:] = beyond_plane(EDGE_TILES, edge_a, edge_b, f)
    remote[0, :, COLS:] = beyond_plane(EDGE_TILES, edgep_a, edgep_b, 1)
    remote[1, :, COLS:] = beyond_plane(CORNER_TILES, corner_a, corner_b, 1)
    for h in range(2):
        at = 6 * ROWS * LEV + 8 * h
        remote[0, :, h * 128 : (h + 1) * 128] = stp[at : at + 8, :]
        at = 6 * HALO * SIZES[0] + 8 * h
        remote[1, :, h * 128 : (h + 1) * 128] = mains[0][at : at + 8, :]
    for r in range(ROWS):
        counts[ROWS + r] = jnp.broadcast_to(flat[1, r : r + 1, :], (8, WIDE))
        counts[beside + r] = jnp.broadcast_to(remote[0, r : r + 1, :], (8, WIDE))
    for j in range(HALO):
        counts[beyond + j] = jnp.broadcast_to(remote[1, pl.ds(2 * (1 - core) + j, 1), :], (8, WIDE))

    sub = lax.broadcasted_iota(jnp.int32, (8, WIDE), 0)

    def stage(source, lead, rows, inset, weight, scale, write, base=None):
        press = PRESS_COEF * scale / 12.0

        def twelve(ahead, behind, ahead2, behind2):
            return 8.0 * (ahead - behind) - (ahead2 - behind2)

        def row(o, _):
            count = counts[o + inset]
            total_x = jnp.zeros((8, WIDE), F32)
            total_y = jnp.zeros((8, WIDE), F32)
            for t in range(TILES):
                here = slice(8 * t, 8 * t + 8)
                back2, back, q, fore, fore2 = [source[2, o + lead + k, here, :] for k in range(5)]
                right, left, right2, left2 = shifts(q)
                grad_x = twelve(fore, back, fore2, back2)
                grad_y = twelve(right, left, right2, left2)
                around = (fore + back) + (right + left)
                total_x = total_x + grad_x
                total_y = total_y + grad_y
                runs[0, here, :] = total_x
                runs[1, here, :] = total_y
                advect = (scale / 12.0) * (
                    source[0, o + lead + 2, here, :] * grad_x + source[1, o + lead + 2, here, :] * grad_y
                )
                value = (weight - 4.0 * VISCOSITY * scale) * q + (VISCOSITY * scale * around - advect)
                if base:
                    value = value + base * ext[2, o + inset, here, :]
                keep = count > (TILES * sub + t).astype(F32)
                write(o, t, 2, jnp.where(keep, value, 0.0))
            above_x = before(total_x, sub)
            above_y = before(total_y, sub)
            for t in range(TILES):
                here = slice(8 * t, 8 * t + 8)
                u = source[0, o + lead + 2, here, :]
                v = source[1, o + lead + 2, here, :]
                us = (scale / 12.0) * u
                vs = (scale / 12.0) * v
                keep = count > (TILES * sub + t).astype(F32)
                for f in range(2):
                    q = source[f, o + lead + 2, here, :]
                    back2, back = source[f, o + lead, here, :], source[f, o + lead + 1, here, :]
                    fore, fore2 = source[f, o + lead + 3, here, :], source[f, o + lead + 4, here, :]
                    right, left, right2, left2 = shifts(q)
                    advect = us * twelve(fore, back, fore2, back2) + vs * twelve(right, left, right2, left2)
                    around = (fore + back) + (right + left)
                    value = (weight - 4.0 * VISCOSITY * scale) * q + (VISCOSITY * scale * around - advect)
                    if f == 0:
                        value = value + (CORIOLIS * scale * v - press * (runs[0, here, :] + above_x))
                    if f == 1:
                        value = value - (CORIOLIS * scale * u + press * (runs[1, here, :] + above_y))
                    if base:
                        value = value + base * ext[f, o + inset, here, :]
                    write(o, t, f, jnp.where(keep, value, 0.0))
            return 0

        lax.fori_loop(0, rows, row, 0, unroll=4)

    def write1(o, t, f, value):
        one[f, o, 8 * t : 8 * t + 8, :] = value

    def write2(o, t, f, value):
        two[f, o, 8 * t : 8 * t + 8, :] = value

    partial = {}

    def write3(o, t, f, value):
        out = (east, north, salt)[f]
        for h in range(2):
            out[h, pl.ds(ROWS * t + o, 8, stride=ROWS * TILES), :] = value[:, h * 128 : (h + 1) * 128]
        if f < 2:
            partial[f] = partial[f] + value if t else value
            if t == TILES - 1:
                flows[f, pl.ds(o, 1), :] = jnp.sum(partial[f], axis=0, keepdims=True)

    stage(ext, 2, 16, 4, 1.0, TIME_STEP, write1)
    stage(one, 0, 12, 6, 0.25, 0.25 * TIME_STEP, write2, 0.75)
    stage(two, 0, 8, 8, 2.0 / 3.0, 2.0 / 3.0 * TIME_STEP, write3, 1.0 / 3.0)
    for f in range(2):
        flows[f] = flat[2] * (flows[f] * (1.0 / LEV))
        flows[2 + f] = flat[f]


def solve_kernel(sc, mine, pair, remote, remote_pair, far, u, v, s, east, north, salt, level, wide, out_u, out_v, sems):
    core = sc[1]
    halves = [slice(128 * h, 128 * h + 128) for h in range(2)]
    copies = [pltpu.make_async_copy(s.at[h], salt.at[:, :, halves[h]], sems.at[h]) for h in range(2)]
    for copy in copies:
        copy.start()
    wide[:, 24:32, :] = mine[...]
    for slot, block in (
        (4 - 2 * core, pair[...]),
        (2 + 2 * core, remote[0]),
        (1 + 4 * core, remote[1]),
        (5 - 4 * core, remote_pair[0]),
        (6 - 6 * core, remote_pair[1]),
        (6 * core, far[...]),
    ):
        wide[:, pl.ds(pl.multiple_of(8 * slot, 8), 8), :] = block
    high = 48
    near = slice(4, 52)
    own = slice(20, 28)

    def up(x):
        return pltpu.roll(x, high - 1, 0)

    def down(x):
        return pltpu.roll(x, 1, 0)

    def right(x):
        return pltpu.roll(x, WIDE - 1, 1)

    def left(x):
        return pltpu.roll(x, 1, 1)

    wet = jnp.where(wide[3, near, :] > 0.0, 1.0, 0.0)
    sixth = wet * (1.0 / 6.0)
    middle = wet * (SIGMA_SHIFT + 20.0 / 6.0) + (1.0 - wet)

    def less(res, e):
        w = wet * e
        rows = up(w) + down(w)
        mix = 4.0 * w + rows
        return (res - middle * e) + sixth * (4.0 * rows + (right(mix) + left(mix)))

    flow_east = wide[0, near, :]
    flow_north = wide[1, near, :]
    x = wide[2, near, :]
    div = 0.5 * (up(flow_east) - down(flow_east)) + 0.5 * (right(flow_north) - left(flow_north))
    res = less(wet * (SIGMA_SHIFT * x - DIVERGENCE_COEF * div), x)
    step = res * (1.0 / CHEB_CENTER)
    keeps, gains = cheb_table(ITERS)
    for index in range(ITERS):
        x = x + step
        if index < ITERS - 1:
            res = less(res, step)
            step = keeps[index] * step + gains[index] * res
    slope_east = (0.5 * (up(x) - down(x)))[own, :COLS]
    slope_north = (0.5 * (right(x) - left(x)))[own, :COLS]
    level[...] = x[own, :COLS]
    count = mine[3][:, :COLS]
    part = LEV // 4
    for first in range(0, LEV, part):
        for lev in range(first, first + part):
            keep = count > lev
            for h, cols in enumerate(halves):
                out_u[h, lev] = jnp.where(keep[:, cols], u[h, lev] - slope_east[:, cols], 0.0)
                out_v[h, lev] = jnp.where(keep[:, cols], v[h, lev] - slope_north[:, cols], 0.0)
        some = slice(first, first + part)
        for source, target in ((out_u, east), (out_v, north)):
            for h, cols in enumerate(halves):
                copy = pltpu.make_async_copy(source.at[h, some], target.at[some, :, cols], sems.at[len(copies)])
                copy.start()
                copies.append(copy)
    for copy in copies:
        copy.wait()


def swap(pairs):
    return [p for a, b in pairs for p in ((a, b), (b, a))]


def call(body, outs, scratch=(), ins=0, space=pltpu.VMEM, away=0):
    vmem = pl.BlockSpec(memory_space=pltpu.VMEM)
    smem = pl.BlockSpec(memory_space=pltpu.SMEM)
    return pl.pallas_call(
        body,
        out_shape=[jax.ShapeDtypeStruct(s, F32) for s in outs],
        in_specs=[smem] + [pl.BlockSpec(memory_space=space)] * ins,
        out_specs=[pl.BlockSpec(memory_space=pltpu.HBM)] * away + [vmem] * (len(outs) - away),
        scratch_shapes=[pltpu.VMEM(s, F32) if isinstance(s, tuple) else s for s in scratch],
        compiler_params=pltpu.CompilerParams(vmem_limit_bytes=16 * 1024 * 1024),
    )


def local(u, v, s, surface, depth, wet, active):
    gx = lax.axis_size("gx")
    gy = lax.axis_size("gy")
    me = lax.axis_index("gx")
    scalars = jnp.stack([me, me % 2, lax.axis_index("gy") % 2]).astype(jnp.int32)
    on_chip = swap([(i, i + 1) for i in range(0, gx, 2)])
    next_chip = swap([(i, i + 1) for i in range(1, gx - 1, 2)])
    far_chip = swap([(i, i + 3) for i in range(1, gx - 3, 2)])
    even = swap([(i, i + 1) for i in range(0, gy, 2)])
    odd = swap([(i, i + 1) for i in range(1, gy - 1, 2)])

    def both(first, second):
        return [(i * gy + j, k * gy + l) for i, k in first for j, l in second]

    edge_a, edge_b, corner_a, corner_b, *packed = call(
        pack_kernel,
        [(EDGE_TILES * LEV + 8, 128)] * 2
        + [(CORNER_TILES * LEV + 8, 128)] * 2
        + [(6 * HALO * levels + (0 if c else 16), 128) for c, levels in enumerate(SIZES)]
        + [(6 * ROWS * LEV + 16, 128), (3, ROWS, COLS)],
        [pltpu.VMEM((ROWS, COLS), jnp.int32)] * 2
        + [(ROWS, COLS)] * 2
        + [(LEV, ROWS, COLS)] * 3
        + [pltpu.SemaphoreType.DMA((7,))],
        ins=7,
        space=pltpu.HBM,
    )(scalars, *(pltpu.with_memory_space_constraint(x, pltpu.HBM) for x in (u, v, s, wet, active, surface, depth)))
    mains = packed[:CHUNKS]
    st, plane = packed[CHUNKS:]
    stp = lax.ppermute(st, "gx", on_chip)
    main = [lax.ppermute(mains[0], "gx", next_chip)]
    stp, corner_a, corner_b = lax.optimization_barrier((stp, corner_a, corner_b))
    edge_a = lax.ppermute(edge_a, "gy", even)
    edge_b = lax.ppermute(edge_b, "gy", odd)
    corner_a = lax.ppermute(corner_a, ("gx", "gy"), both(next_chip, even))
    corner_b = lax.ppermute(corner_b, ("gx", "gy"), both(next_chip, odd))
    edge_a, edge_b, corner_a, corner_b = lax.optimization_barrier((edge_a, edge_b, corner_a, corner_b))
    edgep_a = lax.ppermute(edge_a, "gx", on_chip)
    edgep_b = lax.ppermute(edge_b, "gx", on_chip)

    flows, *state = call(
        rk_kernel,
        [(4, ROWS, WIDE)] + [(2, ROWS * LEV, 128)] * 3,
        [(3, 24, LEV, WIDE), (3, 16, LEV, WIDE), (3, 12, LEV, WIDE)]
        + [(24, 8, WIDE), (3, ROWS, WIDE), (2, ROWS, WIDE), (2, LEV, WIDE)],
        ins=9 + CHUNKS,
    )(scalars, st, stp, edge_a, edge_b, edgep_a, edgep_b, *main, corner_a, corner_b, plane)
    far = lax.ppermute(flows, "gx", far_chip)
    pair = lax.ppermute(flows, "gx", on_chip)
    remote = lax.ppermute(jnp.stack([flows, pair]), "gx", next_chip)
    remote, far = lax.optimization_barrier((remote, far))
    remote_pair = lax.ppermute(remote, "gx", on_chip)
    state = [field.reshape(2, LEV, ROWS, 128) for field in state]
    east, north, salt, level = call(
        solve_kernel,
        [(LEV, ROWS, COLS)] * 3 + [(ROWS, COLS)],
        [(4, 56, WIDE)] + [(2, LEV, ROWS, 128)] * 2 + [pltpu.SemaphoreType.DMA((18,))],
        ins=8,
        away=3,
    )(scalars, flows, pair, remote, remote_pair, far, *state)
    return east, north, salt, level


def solution(mesh):
    cube = P(None, "gx", "gy")
    flat = P("gx", "gy")
    return jax.shard_map(
        local,
        mesh=mesh,
        in_specs=(cube, cube, cube, flat, flat, flat, flat),
        out_specs=(cube, cube, cube, flat),
        check_vma=False,
    )
```

time: 95.3 us -> 97 us (1.018)
  the two profiles are of different devices: /device:TPU:31 before, /device:TPU:13 now
where the time goes in v5:
time: 97 us; the launch traced here: 96.6 us
  waiting for transfers between devices  46.7 us (48%)
  starting transfers between devices  31 us (32%)
  Pallas kernels  18.1 us (19%)
    ppermute x1, waiting for transfers between devices, local(): edge_a = lax.ppermute(edge_a, 'gy', even)  32 us
    pallas_call x1, Pallas kernels, local(): call(rk_kernel, [(4, ROWS, WIDE)] + [(2, ROWS * LEV, 128)] * 3, [(3, 24,...  10.8 us
    ppermute x1, starting transfers between devices, local(): main = [lax.ppermute(mains[0], 'gx', next_chip)]  8.72 us
    ppermute x1, waiting for transfers between devices, local(): edge_b = lax.ppermute(edge_b, 'gy', odd)  7.55 us
    ppermute x1, starting transfers between devices, local(): remote = lax.ppermute(jnp.stack([flows, pair]), 'gx', next_chip)  5.01 us
    pallas_call x1, Pallas kernels, local(): call(solve_kernel, [(LEV, ROWS, COLS)] * 3 + [(ROWS, COLS)], [(4, 56, WID...  4.66 us
    ppermute x1, starting transfers between devices, local(): corner_b = lax.ppermute(corner_b, ('gx', 'gy'), both(next_chip, odd))  3.98 us
    ppermute x1, starting transfers between devices, local(): edge_b = lax.ppermute(edge_b, 'gy', odd)  3.42 us
  transfers between devices with their start and end apart: 12, of which 8 were waited for; matrix products, arithmetic and copies ran while one was open for 0% of the time, Pallas kernels for 0%

profile of v5, /device:TPU:13, one launch (start us, length us, event | category | flops | bytes accessed | tf_op | source)
XLA Modules:
  0.0 96.6 jit_solution(11479607111015340198)
XLA Ops:
  0.6 0.1 pad_add_fusion.sc
  0.7 2.6 %shard_map.102 = (f32[248,128]{1,0:T(8,128)S(1)}, f32[248,128]{1,0:T(8,128)S(1)}, f32[200,128]{1,0:T(8,128)S(1)}, f32[200,128]{1,0:T(8,128)S(1)}, f32[1744,128]{...) custom-call(s32[3]{0:T(128)S(1)} %pad_add_fusion.sc, f32[48,8,256]{2,1,0:T(8,128)} %u.1, ...), custom_call_target="tpu_custom_call" | custom-call | tf_op jit(solution)/shard_map/pallas_call | solution.py:392
  3.4 0.8 collective-permute-start
  4.1 8.7 %collective-permute-start.7 = (f32[1744,128]{1,0:T(8,128)S(1)}, f32[1744,128]{1,0:T(8,128)S(1)}, u32[]{:S(2)}, u32[]{:S(2)}) collective-permute-start(f32[1744,128]{1,0:T(8,128)S(1)} %get-tuple-element.34), channel_id=1, source_target_pairs={{16,32},{32,16},{48,64},{64,48},{80,96},{96,80},{112,128},{128,112... | collective-permute-start | bytes 2678792 | tf_op jit(solution)/shard_map/ppermute | solution.py:408
  12.9 0.8 collective-permute-start.1
  13.7 3.4 %collective-permute-start.2 = (f32[248,128]{1,0:T(8,128)S(1)}, f32[248,128]{1,0:T(8,128)S(1)}, u32[]{:S(2)}, u32[]{:S(2)}) collective-permute-start(f32[248,128]{1,0:T(8,128)S(1)} %get-tuple-element.29), channel_id=1, source_target_pairs={{1,2},{2,1},{3,4},{4,3},{5,6},{6,5},{7,8},{8,7},{9,10},{10,9},{11,... | collective-permute-start | bytes 380936 | tf_op jit(solution)/shard_map/ppermute | solution.py:411
  17.1 2.8 %collective-permute-start.3 = (f32[200,128]{1,0:T(8,128)S(1)}, f32[200,128]{1,0:T(8,128)S(1)}, u32[]{:S(2)}, u32[]{:S(2)}) collective-permute-start(f32[200,128]{1,0:T(8,128)S(1)} %get-tuple-element.30), channel_id=1, source_target_pairs={{16,33},{17,32},{18,35},{19,34},{20,37},{21,36},{22,39},{23,38},{2... | collective-permute-start | bytes 307208 | tf_op jit(solution)/shard_map/ppermute | solution.py:412
  19.9 4.0 %collective-permute-start.4 = (f32[200,128]{1,0:T(8,128)S(1)}, f32[200,128]{1,0:T(8,128)S(1)}, u32[]{:S(2)}, u32[]{:S(2)}) collective-permute-start(f32[200,128]{1,0:T(8,128)S(1)} %get-tuple-element.31), channel_id=1, source_target_pairs={{17,34},{18,33},{19,36},{20,35},{21,38},{22,37},{23,40},{24,39},{2... | collective-permute-start | bytes 307208 | tf_op jit(solution)/shard_map/ppermute | solution.py:413
  23.9 32.0 %collective-permute-done.1.edge_a = f32[248,128]{1,0:T(8,128)S(1)} collective-permute-done((f32[248,128]{1,0:T(8,128)S(1)}, f32[248,128]{1,0:T(8,128)S(1)}, u32[]{:S(2)}, u32[]{:S(2)}) %collective-permute-start.1) | collective-permute-done | bytes 127008 | tf_op jit(solution)/shard_map/ppermute | solution.py:410
  55.9 7.5 %collective-permute-done.2.edge_b = f32[248,128]{1,0:T(8,128)S(1)} collective-permute-done((f32[248,128]{1,0:T(8,128)S(1)}, f32[248,128]{1,0:T(8,128)S(1)}, u32[]{:S(2)}, u32[]{:S(2)}) %collective-permute-start.2) | collective-permute-done | bytes 127008 | tf_op jit(solution)/shard_map/ppermute | solution.py:411
  63.5 0.8 collective-permute-start.5
  64.2 0.1 collective-permute-start.6
  64.3 0.9 collective-permute-done.5.edgep_a
  65.2 0.4 collective-permute-done.6.edgep_b
  65.6 10.8 %shard_map.103 = (f32[4,8,384]{2,1,0:T(8,128)S(1)}, f32[2,384,128]{2,1,0:T(8,128)S(1)}, f32[2,384,128]{2,1,0:T(8,128)S(1)}, f32[2,384,128]{2,1,0:T(8,128)S(1)}) custom-call(s32[3]{0:T(128)S(1)} %pad_add_fusion.sc, f32[2320,128]{1,0:T(8,128)S(1)} %get-tuple-element.24.st, f32[2320,128]{1,0:T(8,128)S(1)} %collective-permute-done.stp, ...), custom_call_target="tpu_custom_call" | custom-call | tf_op jit(solution)/shard_map/pallas_call | solution.py:418
  76.4 0.3 collective-permute-start.8
  76.7 1.0 %collective-permute-done.8.pair = f32[4,8,384]{2,1,0:T(8,128)S(1)} collective-permute-done((f32[4,8,384]{2,1,0:T(8,128)S(1)}, f32[4,8,384]{2,1,0:T(8,128)S(1)}, u32[]{:S(2)}, u32[]{:S(2)}) %collective-permute-start.8) | collective-permute-done | bytes 49184 | tf_op jit(solution)/shard_map/ppermute | solution.py:426
  77.7 5.0 %collective-permute-start.9 = (f32[2,4,8,384]{3,2,1,0:T(8,128)S(1)}, f32[2,4,8,384]{3,2,1,0:T(8,128)S(1)}, u32[]{:S(2)}, u32[]{:S(2)}) collective-permute-start(f32[2,4,8,384]{3,2,1,0:T(8,128)S(1)} %pad_maximum_fusion), channel_id=1, source_target_pairs={{16,32},{32,16},{48,64},{64,48},{80,96},{96,80},{112,128},{128,112... | collective-permute-start | bytes 294920 | tf_op jit(solution)/shard_map/ppermute | solution.py:427
  82.8 3.3 %collective-permute-start.10 = (f32[4,8,384]{2,1,0:T(8,128)S(1)}, f32[4,8,384]{2,1,0:T(8,128)S(1)}, u32[]{:S(2)}, u32[]{:S(2)}) collective-permute-start(f32[4,8,384]{2,1,0:T(8,128)S(1)} %get-tuple-element.38.mine), channel_id=1, source_target_pairs={{16,64},{64,16},{48,96},{96,48},{80,128},{128,80},{112,160},{160,1... | collective-permute-start | bytes 147464 | tf_op jit(solution)/shard_map/ppermute | solution.py:425
  86.1 2.4 %collective-permute-done.10.far = f32[4,8,384]{2,1,0:T(8,128)S(1)} collective-permute-done((f32[4,8,384]{2,1,0:T(8,128)S(1)}, f32[4,8,384]{2,1,0:T(8,128)S(1)}, u32[]{:S(2)}, u32[]{:S(2)}) %collective-permute-start.10) | collective-permute-done | bytes 49184 | tf_op jit(solution)/shard_map/ppermute | solution.py:425
  88.5 1.5 %collective-permute-done.9.remote = f32[2,4,8,384]{3,2,1,0:T(8,128)S(1)} collective-permute-done((f32[2,4,8,384]{3,2,1,0:T(8,128)S(1)}, f32[2,4,8,384]{3,2,1,0:T(8,128)S(1)}, u32[]{:S(2)}, u32[]{:S(2)}) %collective-permute-start.9) | collective-permute-done | bytes 98336 | tf_op jit(solution)/shard_map/ppermute | solution.py:427
  89.9 1.1 %collective-permute-start.11 = (f32[2,4,8,384]{3,2,1,0:T(8,128)S(1)}, f32[2,4,8,384]{3,2,1,0:T(8,128)S(1)}, u32[]{:S(2)}, u32[]{:S(2)}) collective-permute-start(f32[2,4,8,384]{3,2,1,0:T(8,128)S(1)} %collective-permute-done.9.remote), channel_id=1, source_target_pairs={{0,16},{16,0},{32,48},{48,32},{64,80},{80,64},{96,112},{112,96},{1... | collective-permute-start | bytes 294920 | tf_op jit(solution)/shard_map/ppermute | solution.py:429
  91.0 0.9 collective-permute-done.11.remote_pair
  92.0 4.7 %shard_map.104 = (f32[48,8,256]{2,1,0:T(8,128)}, f32[48,8,256]{2,1,0:T(8,128)}, f32[48,8,256]{2,1,0:T(8,128)}, f32[8,256]{1,0:T(8,128)}) custom-call(s32[3]{0:T(128)S(1)} %pad_add_fusion.sc, f32[4,8,384]{2,1,0:T(8,128)S(1)} %get-tuple-element.38.mine, f32[4,8,384]{2,1,0:T(8,128)S(1)} %collective-permute-done.8.pair, ...), custom_call_target="tpu_custom_call" | custom-call | tf_op jit(solution)/shard_map/pallas_call | solution.py:431
  (5 shorter events, 0.0 us)
Async XLA Ops:
  3.4 13.7 %collective-permute-start = (f32[2320,128]{1,0:T(8,128)S(1)}, f32[2320,128]{1,0:T(8,128)S(1)}, u32[]{:S(2)}, u32[]{:S(2)}) collective-permute-start(f32[2320,128]{1,0:T(8,128)S(1)} %get-tuple-element.24.st), channel_id=1, source_target_pairs={{0,16},{16,0},{32,48},{48,32},{64,80},{80,64},{96,112},{112,96},{1... | collective-permute-start | bytes 3563528 | tf_op jit(solution)/shard_map/ppermute | solution.py:407
  4.1 60.2 %collective-permute-start.7 = (f32[1744,128]{1,0:T(8,128)S(1)}, f32[1744,128]{1,0:T(8,128)S(1)}, u32[]{:S(2)}, u32[]{:S(2)}) collective-permute-start(f32[1744,128]{1,0:T(8,128)S(1)} %get-tuple-element.34), channel_id=1, source_target_pairs={{16,32},{32,16},{48,64},{64,48},{80,96},{96,80},{112,128},{128,112... | collective-permute-start | bytes 2678792 | tf_op jit(solution)/shard_map/ppermute | solution.py:408
  12.9 43.1 %collective-permute-start.1 = (f32[248,128]{1,0:T(8,128)S(1)}, f32[248,128]{1,0:T(8,128)S(1)}, u32[]{:S(2)}, u32[]{:S(2)}) collective-permute-start(f32[248,128]{1,0:T(8,128)S(1)} %get-tuple-element.28), channel_id=1, source_target_pairs={{0,1},{1,0},{2,3},{3,2},{4,5},{5,4},{6,7},{7,6},{8,9},{9,8},{10,11... | collective-permute-start | bytes 380936 | tf_op jit(solution)/shard_map/ppermute | solution.py:410
  13.7 49.8 %collective-permute-start.2 = (f32[248,128]{1,0:T(8,128)S(1)}, f32[248,128]{1,0:T(8,128)S(1)}, u32[]{:S(2)}, u32[]{:S(2)}) collective-permute-start(f32[248,128]{1,0:T(8,128)S(1)} %get-tuple-element.29), channel_id=1, source_target_pairs={{1,2},{2,1},{3,4},{4,3},{5,6},{6,5},{7,8},{8,7},{9,10},{10,9},{11,... | collective-permute-start | bytes 380936 | tf_op jit(solution)/shard_map/ppermute | solution.py:411
  17.1 46.4 %collective-permute-start.3 = (f32[200,128]{1,0:T(8,128)S(1)}, f32[200,128]{1,0:T(8,128)S(1)}, u32[]{:S(2)}, u32[]{:S(2)}) collective-permute-start(f32[200,128]{1,0:T(8,128)S(1)} %get-tuple-element.30), channel_id=1, source_target_pairs={{16,33},{17,32},{18,35},{19,34},{20,37},{21,36},{22,39},{23,38},{2... | collective-permute-start | bytes 307208 | tf_op jit(solution)/shard_map/ppermute | solution.py:412
  19.9 43.6 %collective-permute-start.4 = (f32[200,128]{1,0:T(8,128)S(1)}, f32[200,128]{1,0:T(8,128)S(1)}, u32[]{:S(2)}, u32[]{:S(2)}) collective-permute-start(f32[200,128]{1,0:T(8,128)S(1)} %get-tuple-element.31), channel_id=1, source_target_pairs={{17,34},{18,33},{19,36},{20,35},{21,38},{22,37},{23,40},{24,39},{2... | collective-permute-start | bytes 307208 | tf_op jit(solution)/shard_map/ppermute | solution.py:413
  63.5 1.7 %collective-permute-start.5 = (f32[248,128]{1,0:T(8,128)S(1)}, f32[248,128]{1,0:T(8,128)S(1)}, u32[]{:S(2)}, u32[]{:S(2)}) collective-permute-start(f32[248,128]{1,0:T(8,128)S(1)} %collective-permute-done.1.edge_a), channel_id=1, source_target_pairs={{0,16},{16,0},{32,48},{48,32},{64,80},{80,64},{96,112},{112,96},{1... | collective-permute-start | bytes 380936 | tf_op jit(solution)/shard_map/ppermute | solution.py:415
  64.2 1.3 %collective-permute-start.6 = (f32[248,128]{1,0:T(8,128)S(1)}, f32[248,128]{1,0:T(8,128)S(1)}, u32[]{:S(2)}, u32[]{:S(2)}) collective-permute-start(f32[248,128]{1,0:T(8,128)S(1)} %collective-permute-done.2.edge_b), channel_id=1, source_target_pairs={{0,16},{16,0},{32,48},{48,32},{64,80},{80,64},{96,112},{112,96},{1... | collective-permute-start | bytes 380936 | tf_op jit(solution)/shard_map/ppermute | solution.py:416
  76.4 1.3 %collective-permute-start.8 = (f32[4,8,384]{2,1,0:T(8,128)S(1)}, f32[4,8,384]{2,1,0:T(8,128)S(1)}, u32[]{:S(2)}, u32[]{:S(2)}) collective-permute-start(f32[4,8,384]{2,1,0:T(8,128)S(1)} %get-tuple-element.38.mine), channel_id=1, source_target_pairs={{0,16},{16,0},{32,48},{48,32},{64,80},{80,64},{96,112},{112,96},{1... | collective-permute-start | bytes 147464 | tf_op jit(solution)/shard_map/ppermute | solution.py:426
  77.7 12.2 %collective-permute-start.9 = (f32[2,4,8,384]{3,2,1,0:T(8,128)S(1)}, f32[2,4,8,384]{3,2,1,0:T(8,128)S(1)}, u32[]{:S(2)}, u32[]{:S(2)}) collective-permute-start(f32[2,4,8,384]{3,2,1,0:T(8,128)S(1)} %pad_maximum_fusion), channel_id=1, source_target_pairs={{16,32},{32,16},{48,64},{64,48},{80,96},{96,80},{112,128},{128,112... | collective-permute-start | bytes 294920 | tf_op jit(solution)/shard_map/ppermute | solution.py:427
  82.8 5.7 %collective-permute-start.10 = (f32[4,8,384]{2,1,0:T(8,128)S(1)}, f32[4,8,384]{2,1,0:T(8,128)S(1)}, u32[]{:S(2)}, u32[]{:S(2)}) collective-permute-start(f32[4,8,384]{2,1,0:T(8,128)S(1)} %get-tuple-element.38.mine), channel_id=1, source_target_pairs={{16,64},{64,16},{48,96},{96,48},{80,128},{128,80},{112,160},{160,1... | collective-permute-start | bytes 147464 | tf_op jit(solution)/shard_map/ppermute | solution.py:425
  89.9 2.0 %collective-permute-start.11 = (f32[2,4,8,384]{3,2,1,0:T(8,128)S(1)}, f32[2,4,8,384]{3,2,1,0:T(8,128)S(1)}, u32[]{:S(2)}, u32[]{:S(2)}) collective-permute-start(f32[2,4,8,384]{3,2,1,0:T(8,128)S(1)} %collective-permute-done.9.remote), channel_id=1, source_target_pairs={{0,16},{16,0},{32,48},{48,32},{64,80},{80,64},{96,112},{112,96},{1... | collective-permute-start | bytes 294920 | tf_op jit(solution)/shard_map/ppermute | solution.py:429

commit v6 on v5

--- a/solution.py
+++ b/solution.py
@@ -148,66 +148,89 @@
     return total - x
 
 
-def rk_kernel(sc, st, stp, edge_a, edge_b, edgep_a, edgep_b, *rest):
-    mains = rest[:CHUNKS]
-    corner_a, corner_b, plane, flows, east, north, salt, ext, one, two, counts, flat, remote, runs = rest[CHUNKS:]
+def columns_beyond(ext, tiles, rows, first, a, b, north_odd):
+    for g in range(tiles):
+        here = slice(g * LEV, g * LEV + LEV)
+        high, low = ordered(a[here, :], b[here, :], north_odd)
+        for slot in range(min(SLOTS, 3 * rows - SLOTS * g)):
+            f, r = divmod(SLOTS * g + slot, rows)
+            ext[f, first + r, :, COLS:] = unpack(high, low, slot)
+
+
+def plane_beyond(tiles, a, b, slot, north_odd):
+    high, low = ordered(a[tiles * LEV :, :], b[tiles * LEV :, :], north_odd)
+    return unpack(high, low, slot)
+
+
+def early_kernel(sc, st, stp, edge_a, edge_b, edgep_a, edgep_b, plane, *rest):
+    arrays, runs, aside = rest[:-2], rest[-2], rest[-1]
+    ext, one, two, counts, flows, flat, east, north, salt = arrays
     core = sc[1]
     north_odd = sc[2]
     beside = 16 * (1 - core)
-    beyond = 2 + 14 * core
     for source, first in ((st, ROWS), (stp, beside)):
         for f in range(3):
             for r in range(ROWS):
                 for h in range(2):
                     at = ((2 * f + h) * ROWS + r) * LEV
                     ext[f, first + r, :, h * 128 : (h + 1) * 128] = source[at : at + LEV, :]
+    columns_beyond(ext, EDGE_TILES, ROWS, ROWS, edge_a, edge_b, north_odd)
+    columns_beyond(ext, EDGE_TILES, ROWS, beside, edgep_a, edgep_b, north_odd)
+    for f in range(3):
+        flat[f, :, :COLS] = plane[f]
+        flat[f, :, COLS:] = plane_beyond(EDGE_TILES, edge_a, edge_b, f, north_odd)
+    aside[:, COLS:] = plane_beyond(EDGE_TILES, edgep_a, edgep_b, 1, north_odd)
+    for h in range(2):
+        at = 6 * ROWS * LEV + 8 * h
+        aside[:, h * 128 : (h + 1) * 128] = stp[at : at + 8, :]
+    for r in range(ROWS):
+        counts[ROWS + r] = jnp.broadcast_to(flat[1, r : r + 1, :], (8, WIDE))
+        counts[beside + r] = jnp.broadcast_to(aside[r : r + 1, :], (8, WIDE))
+    other = 1 - core
+    stages(arrays, runs, ((6 * other, 10, 5), (6 * other, 6, 3), (6 * other, 2, 2)))
+    for f in range(2):
+        flows[2 + f] = flat[f]
+
+
+def late_kernel(sc, *rest):
+    mains = rest[:CHUNKS]
+    corner_a, corner_b, _e, _o, _t, _c, _f, flat, _u, _v, _s = rest[CHUNKS : CHUNKS + 11]
+    ext, one, two, counts, flows, east, north, salt, runs, aside = rest[CHUNKS + 11 :]
+    core = sc[1]
+    north_odd = sc[2]
+    beyond = 2 + 14 * core
     for f in range(3):
         for j in range(HALO):
             for h in range(2):
                 for main, levels, lev0 in zip(mains, SIZES, STARTS):
                     at = ((2 * f + h) * HALO + j) * levels
                     ext[f, beyond + j, lev0 : lev0 + levels, h * 128 : (h + 1) * 128] = main[at : at + levels, :]
-    for tiles, rows, first, a, b in (
-        (EDGE_TILES, ROWS, ROWS, edge_a, edge_b),
-        (EDGE_TILES, ROWS, beside, edgep_a, edgep_b),
-        (CORNER_TILES, HALO, beyond, corner_a, corner_b),
-    ):
-        for g in range(tiles):
-            here = slice(g * LEV, g * LEV + LEV)
-            high, low = ordered(a[here, :], b[here, :], north_odd)
-            for slot in range(min(SLOTS, 3 * rows - SLOTS * g)):
-                f, r = divmod(SLOTS * g + slot, rows)
-                ext[f, first + r, :, COLS:] = unpack(high, low, slot)
-
-    def beyond_plane(tiles, a, b, slot):
-        high, low = ordered(a[tiles * LEV :, :], b[tiles * LEV :, :], north_odd)
-        return unpack(high, low, slot)
-
-    for f in range(3):
-        flat[f, :, :COLS] = plane[f]
-        flat[f, :, COLS:] = beyond_plane(EDGE_TILES, edge_a, edge_b, f)
-    remote[0, :, COLS:] = beyond_plane(EDGE_TILES, edgep_a, edgep_b, 1)
-    remote[1, :, COLS:] = beyond_plane(CORNER_TILES, corner_a, corner_b, 1)
+    columns_beyond(ext, CORNER_TILES, HALO, beyond, corner_a, corner_b, north_odd)
+    aside[:, COLS:] = plane_beyond(CORNER_TILES, corner_a, corner_b, 1, north_odd)
     for h in range(2):
-        at = 6 * ROWS * LEV + 8 * h
-        remote[0, :, h * 128 : (h + 1) * 128] = stp[at : at + 8, :]
         at = 6 * HALO * SIZES[0] + 8 * h
-        remote[1, :, h * 128 : (h + 1) * 128] = mains[0][at : at + 8, :]
-    for r in range(ROWS):
-        counts[ROWS + r] = jnp.broadcast_to(flat[1, r : r + 1, :], (8, WIDE))
-        counts[beside + r] = jnp.broadcast_to(remote[0, r : r + 1, :], (8, WIDE))
+        aside[:, h * 128 : (h + 1) * 128] = mains[0][at : at + 8, :]
     for j in range(HALO):
-        counts[beyond + j] = jnp.broadcast_to(remote[1, pl.ds(2 * (1 - core) + j, 1), :], (8, WIDE))
-
+        counts[beyond + j] = jnp.broadcast_to(aside[pl.ds(2 * (1 - core) + j, 1), :], (8, WIDE))
+    stages((ext, one, two, counts, flows, flat, east, north, salt), runs, ((10 * core, 6, 3), (6 * core, 6, 3), (2 * core, 6, 3)))
+    for f in range(2):
+        flows[f] = flat[2] * (flows[f] * (1.0 / LEV))
+
+
+def stages(arrays, runs, spans):
+    ext, one, two, counts, flows, _flat, east, north, salt = arrays
     sub = lax.broadcasted_iota(jnp.int32, (8, WIDE), 0)
 
-    def stage(source, lead, rows, inset, weight, scale, write, base=None):
+    def stage(span, source, lead, inset, weight, scale, write, base=None):
         press = PRESS_COEF * scale / 12.0
 
         def twelve(ahead, behind, ahead2, behind2):
             return 8.0 * (ahead - behind) - (ahead2 - behind2)
 
-        def row(o, _):
+        start, rows, together = span
+
+        def row(index, _):
+            o = start + index
             count = counts[o + inset]
             total_x = jnp.zeros((8, WIDE), F32)
             total_y = jnp.zeros((8, WIDE), F32)
@@ -256,7 +279,7 @@
                     write(o, t, f, jnp.where(keep, value, 0.0))
             return 0
 
-        lax.fori_loop(0, rows, row, 0, unroll=4)
+        lax.fori_loop(0, rows, row, 0, unroll=together)
 
     def write1(o, t, f, value):
         one[f, o, 8 * t : 8 * t + 8, :] = value
@@ -275,12 +298,9 @@
             if t == TILES - 1:
                 flows[f, pl.ds(o, 1), :] = jnp.sum(partial[f], axis=0, keepdims=True)
 
-    stage(ext, 2, 16, 4, 1.0, TIME_STEP, write1)
-    stage(one, 0, 12, 6, 0.25, 0.25 * TIME_STEP, write2, 0.75)
-    stage(two, 0, 8, 8, 2.0 / 3.0, 2.0 / 3.0 * TIME_STEP, write3, 1.0 / 3.0)
-    for f in range(2):
-        flows[f] = flat[2] * (flows[f] * (1.0 / LEV))
-        flows[2 + f] = flat[f]
+    stage(spans[0], ext, 2, 4, 1.0, TIME_STEP, write1)
+    stage(spans[1], one, 0, 6, 0.25, 0.25 * TIME_STEP, write2, 0.75)
+    stage(spans[2], two, 0, 8, 2.0 / 3.0, 2.0 / 3.0 * TIME_STEP, write3, 1.0 / 3.0)
 
 
 def solve_kernel(sc, mine, pair, remote, remote_pair, far, u, v, s, east, north, salt, level, wide, out_u, out_v, sems):
@@ -362,7 +382,7 @@
     return [p for a, b in pairs for p in ((a, b), (b, a))]
 
 
-def call(body, outs, scratch=(), ins=0, space=pltpu.VMEM, away=0):
+def call(body, outs, scratch=(), ins=0, space=pltpu.VMEM, away=0, aliases={}):
     vmem = pl.BlockSpec(memory_space=pltpu.VMEM)
     smem = pl.BlockSpec(memory_space=pltpu.SMEM)
     return pl.pallas_call(
@@ -371,6 +391,7 @@
         in_specs=[smem] + [pl.BlockSpec(memory_space=space)] * ins,
         out_specs=[pl.BlockSpec(memory_space=pltpu.HBM)] * away + [vmem] * (len(outs) - away),
         scratch_shapes=[pltpu.VMEM(s, F32) if isinstance(s, tuple) else s for s in scratch],
+        input_output_aliases=aliases,
         compiler_params=pltpu.CompilerParams(vmem_limit_bytes=16 * 1024 * 1024),
     )
 
@@ -405,23 +426,34 @@
     mains = packed[:CHUNKS]
     st, plane = packed[CHUNKS:]
     stp = lax.ppermute(st, "gx", on_chip)
-    main = [lax.ppermute(mains[0], "gx", next_chip)]
-    stp, corner_a, corner_b = lax.optimization_barrier((stp, corner_a, corner_b))
     edge_a = lax.ppermute(edge_a, "gy", even)
     edge_b = lax.ppermute(edge_b, "gy", odd)
+    edge_a, edge_b, stp, corner_a, corner_b, *mains = lax.optimization_barrier(
+        (edge_a, edge_b, stp, corner_a, corner_b, *mains)
+    )
+    main = [lax.ppermute(m, "gx", next_chip) for m in mains]
     corner_a = lax.ppermute(corner_a, ("gx", "gy"), both(next_chip, even))
     corner_b = lax.ppermute(corner_b, ("gx", "gy"), both(next_chip, odd))
-    edge_a, edge_b, corner_a, corner_b = lax.optimization_barrier((edge_a, edge_b, corner_a, corner_b))
     edgep_a = lax.ppermute(edge_a, "gx", on_chip)
     edgep_b = lax.ppermute(edge_b, "gx", on_chip)
 
-    flows, *state = call(
-        rk_kernel,
-        [(4, ROWS, WIDE)] + [(2, ROWS * LEV, 128)] * 3,
-        [(3, 24, LEV, WIDE), (3, 16, LEV, WIDE), (3, 12, LEV, WIDE)]
-        + [(24, 8, WIDE), (3, ROWS, WIDE), (2, ROWS, WIDE), (2, LEV, WIDE)],
-        ins=9 + CHUNKS,
-    )(scalars, st, stp, edge_a, edge_b, edgep_a, edgep_b, *main, corner_a, corner_b, plane)
+    field = (2, ROWS * LEV, 128)
+    shapes = [(3, 24, LEV, WIDE), (3, 16, LEV, WIDE), (3, 12, LEV, WIDE), (24, 8, WIDE), (4, ROWS, WIDE)]
+    *shared, flat, u, v, s = call(
+        early_kernel,
+        shapes + [(3, ROWS, WIDE)] + [field] * 3,
+        [(2, LEV, WIDE), (ROWS, WIDE)],
+        ins=7,
+    )(scalars, st, stp, edge_a, edge_b, edgep_a, edgep_b, plane)
+    shift = 1 + CHUNKS + 2
+    *_, flows, u, v, s = call(
+        late_kernel,
+        shapes + [field] * 3,
+        [(2, LEV, WIDE), (ROWS, WIDE)],
+        ins=CHUNKS + 11,
+        aliases={shift + i: i for i in range(5)} | {shift + 6 + i: 5 + i for i in range(3)},
+    )(scalars, *main, corner_a, corner_b, *shared, flat, u, v, s)
+    state = [u, v, s]
     far = lax.ppermute(flows, "gx", far_chip)
     pair = lax.ppermute(flows, "gx", on_chip)
     remote = lax.ppermute(jnp.stack([flows, pair]), "gx", next_chip)

time: 97 us -> 99.8 us (1.029)
  the two profiles are of different devices: /device:TPU:13 before, /device:TPU:31 now
where the time goes in v6:
time: 99.8 us; the launch traced here: 99.4 us
  waiting for transfers between devices  40.7 us (41%)
  starting transfers between devices  38.4 us (38%)
  Pallas kernels  19.5 us (20%)
    ppermute x1, waiting for transfers between devices, local(): corner_a = lax.ppermute(corner_a, ('gx', 'gy'), both(next_chip, even))  26.7 us
    ppermute x1, starting transfers between devices, local(): main = [lax.ppermute(m, 'gx', next_chip) for m in mains]  9.04 us
    pallas_call x1, Pallas kernels, local(): call(early_kernel, shapes + [(3, ROWS, WIDE)] + [field] * 3, [(2, LEV, WI...  6.17 us
    pallas_call x1, Pallas kernels, local(): call(late_kernel, shapes + [field] * 3, [(2, LEV, WIDE), (ROWS, WIDE)], i...  6.06 us
    ppermute x1, starting transfers between devices, local(): remote = lax.ppermute(jnp.stack([flows, pair]), 'gx', next_chip)  6.02 us
    ppermute x1, starting transfers between devices, local(): corner_b = lax.ppermute(corner_b, ('gx', 'gy'), both(next_chip, odd))  5.86 us
    ppermute x1, starting transfers between devices, local(): pair = lax.ppermute(flows, 'gx', on_chip)  5.7 us
    ppermute x1, waiting for transfers between devices, local(): remote = lax.ppermute(jnp.stack([flows, pair]), 'gx', next_chip)  5.52 us
  transfers between devices with their start and end apart: 12, of which 6 were waited for; matrix products, arithmetic and copies ran while one was open for 0% of the time, Pallas kernels for 6%

profile of v6, /device:TPU:31, one launch (start us, length us, event | category | flops | bytes accessed | tf_op | source)
XLA Modules:
  0.0 99.4 jit_solution(14816279031808250045)
XLA Ops:
  0.6 0.1 pad_add_fusion.sc
  0.7 2.6 %shard_map.102 = (f32[248,128]{1,0:T(8,128)S(1)}, f32[248,128]{1,0:T(8,128)S(1)}, f32[200,128]{1,0:T(8,128)S(1)}, f32[200,128]{1,0:T(8,128)S(1)}, f32[1744,128]{...) custom-call(s32[3]{0:T(128)S(1)} %pad_add_fusion.sc, f32[48,8,256]{2,1,0:T(8,128)} %u.1, ...), custom_call_target="tpu_custom_call" | custom-call | tf_op jit(solution)/shard_map/pallas_call | solution.py:413
  3.4 0.8 collective-permute-start.2
  4.1 1.7 %collective-permute-start = (f32[248,128]{1,0:T(8,128)S(1)}, f32[248,128]{1,0:T(8,128)S(1)}, u32[]{:S(2)}, u32[]{:S(2)}) collective-permute-start(f32[248,128]{1,0:T(8,128)S(1)} %get-tuple-element.32), channel_id=1, source_target_pairs={{0,1},{1,0},{2,3},{3,2},{4,5},{5,4},{6,7},{7,6},{8,9},{9,8},{10,11... | collective-permute-start | bytes 380936 | tf_op jit(solution)/shard_map/ppermute | solution.py:429
  5.8 4.8 %collective-permute-start.1 = (f32[248,128]{1,0:T(8,128)S(1)}, f32[248,128]{1,0:T(8,128)S(1)}, u32[]{:S(2)}, u32[]{:S(2)}) collective-permute-start(f32[248,128]{1,0:T(8,128)S(1)} %get-tuple-element.33), channel_id=1, source_target_pairs={{1,2},{2,1},{3,4},{4,3},{5,6},{6,5},{7,8},{8,7},{9,10},{10,9},{11,... | collective-permute-start | bytes 380936 | tf_op jit(solution)/shard_map/ppermute | solution.py:430
  10.6 0.0 collective-permute-done.edge_a
  10.6 4.5 %collective-permute-done.1.edge_b = f32[248,128]{1,0:T(8,128)S(1)} collective-permute-done((f32[248,128]{1,0:T(8,128)S(1)}, f32[248,128]{1,0:T(8,128)S(1)}, u32[]{:S(2)}, u32[]{:S(2)}) %collective-permute-start.1) | collective-permute-done | bytes 127008 | tf_op jit(solution)/shard_map/ppermute | solution.py:430
  15.0 9.0 %collective-permute-start.3 = (f32[1744,128]{1,0:T(8,128)S(1)}, f32[1744,128]{1,0:T(8,128)S(1)}, u32[]{:S(2)}, u32[]{:S(2)}) collective-permute-start(f32[1744,128]{1,0:T(8,128)S(1)} %get-tuple-element.38), channel_id=1, source_target_pairs={{16,32},{32,16},{48,64},{64,48},{80,96},{96,80},{112,128},{128,112... | collective-permute-start | bytes 2678792 | tf_op jit(solution)/shard_map/ppermute | solution.py:434
  24.1 0.1 collective-permute-start.6
  24.2 0.5 collective-permute-start.7
  24.7 1.9 %collective-permute-start.4 = (f32[200,128]{1,0:T(8,128)S(1)}, f32[200,128]{1,0:T(8,128)S(1)}, u32[]{:S(2)}, u32[]{:S(2)}) collective-permute-start(f32[200,128]{1,0:T(8,128)S(1)} %get-tuple-element.39), channel_id=1, source_target_pairs={{16,33},{17,32},{18,35},{19,34},{20,37},{21,36},{22,39},{23,38},{2... | collective-permute-start | bytes 307208 | tf_op jit(solution)/shard_map/ppermute | solution.py:435
  26.6 5.9 %collective-permute-start.5 = (f32[200,128]{1,0:T(8,128)S(1)}, f32[200,128]{1,0:T(8,128)S(1)}, u32[]{:S(2)}, u32[]{:S(2)}) collective-permute-start(f32[200,128]{1,0:T(8,128)S(1)} %get-tuple-element.40), channel_id=1, source_target_pairs={{17,34},{18,33},{19,36},{20,35},{21,38},{22,37},{23,40},{24,39},{2... | collective-permute-start | bytes 307208 | tf_op jit(solution)/shard_map/ppermute | solution.py:436
  32.5 6.2 %shard_map.103 = (f32[3,24,48,384]{3,2,1,0:T(8,128)S(1)}, f32[3,16,48,384]{3,2,1,0:T(8,128)S(1)}, f32[3,12,48,384]{3,2,1,0:T(8,128)S(1)}, f32[24,8,384]{2,1,0:T(...) custom-call(s32[3]{0:T(128)S(1)} %pad_add_fusion.sc, ...), custom_call_target="tpu_custom_call" | custom-call | tf_op jit(solution)/shard_map/pallas_call | solution.py:442
  38.7 26.7 %collective-permute-done.4.rest_1_ = f32[200,128]{1,0:T(8,128)S(1)} collective-permute-done((f32[200,128]{1,0:T(8,128)S(1)}, f32[200,128]{1,0:T(8,128)S(1)}, u32[]{:S(2)}, u32[]{:S(2)}) %collective-permute-start.4) | collective-permute-done | bytes 102432 | tf_op jit(solution)/shard_map/ppermute | solution.py:435
  65.3 2.2 %collective-permute-done.5.rest_2_ = f32[200,128]{1,0:T(8,128)S(1)} collective-permute-done((f32[200,128]{1,0:T(8,128)S(1)}, f32[200,128]{1,0:T(8,128)S(1)}, u32[]{:S(2)}, u32[]{:S(2)}) %collective-permute-start.5) | collective-permute-done | bytes 102432 | tf_op jit(solution)/shard_map/ppermute | solution.py:436
  67.5 6.1 %shard_map.104 = (f32[3,24,48,384]{3,2,1,0:T(8,128)S(1)}, f32[3,16,48,384]{3,2,1,0:T(8,128)S(1)}, f32[3,12,48,384]{3,2,1,0:T(8,128)S(1)}, f32[24,8,384]{2,1,0:T(...) custom-call(s32[3]{0:T(128)S(1)} %pad_add_fusion.sc, ...), custom_call_target="tpu_custom_call", output_to_operand_aliasing={{0}: (4, {}), {1}: (5, {}), {2}: (6, {}), {3}: (7, {}), {4}... | custom-call | tf_op jit(solution)/shard_map/pallas_call | solution.py:449
  73.6 5.7 %collective-permute-start.8 = (f32[4,8,384]{2,1,0:T(8,128)S(1)}, f32[4,8,384]{2,1,0:T(8,128)S(1)}, u32[]{:S(2)}, u32[]{:S(2)}) collective-permute-start(f32[4,8,384]{2,1,0:T(8,128)S(1)} %get-tuple-element.54.mine), channel_id=1, source_target_pairs={{0,16},{16,0},{32,48},{48,32},{64,80},{80,64},{96,112},{112,96},{1... | collective-permute-start | bytes 147464 | tf_op jit(solution)/shard_map/ppermute | solution.py:458
  79.3 0.9 collective-permute-done.8.pair
  80.2 6.0 %collective-permute-start.9 = (f32[2,4,8,384]{3,2,1,0:T(8,128)S(1)}, f32[2,4,8,384]{3,2,1,0:T(8,128)S(1)}, u32[]{:S(2)}, u32[]{:S(2)}) collective-permute-start(f32[2,4,8,384]{3,2,1,0:T(8,128)S(1)} %pad_maximum_fusion), channel_id=1, source_target_pairs={{16,32},{32,16},{48,64},{64,48},{80,96},{96,80},{112,128},{128,112... | collective-permute-start | bytes 294920 | tf_op jit(solution)/shard_map/ppermute | solution.py:459
  86.2 0.7 collective-permute-start.10
  86.9 5.5 %collective-permute-done.9.remote = f32[2,4,8,384]{3,2,1,0:T(8,128)S(1)} collective-permute-done((f32[2,4,8,384]{3,2,1,0:T(8,128)S(1)}, f32[2,4,8,384]{3,2,1,0:T(8,128)S(1)}, u32[]{:S(2)}, u32[]{:S(2)}) %collective-permute-start.9) | collective-permute-done | bytes 98336 | tf_op jit(solution)/shard_map/ppermute | solution.py:459
  92.4 1.4 %collective-permute-start.11 = (f32[2,4,8,384]{3,2,1,0:T(8,128)S(1)}, f32[2,4,8,384]{3,2,1,0:T(8,128)S(1)}, u32[]{:S(2)}, u32[]{:S(2)}) collective-permute-start(f32[2,4,8,384]{3,2,1,0:T(8,128)S(1)} %collective-permute-done.9.remote), channel_id=1, source_target_pairs={{0,16},{16,0},{32,48},{48,32},{64,80},{80,64},{96,112},{112,96},{1... | collective-permute-start | bytes 294920 | tf_op jit(solution)/shard_map/ppermute | solution.py:461
  93.8 0.9 collective-permute-done.11.remote_pair
  94.8 4.7 %shard_map.105 = (f32[48,8,256]{2,1,0:T(8,128)}, f32[48,8,256]{2,1,0:T(8,128)}, f32[48,8,256]{2,1,0:T(8,128)}, f32[8,256]{1,0:T(8,128)}) custom-call(s32[3]{0:T(128)S(1)} %pad_add_fusion.sc, f32[4,8,384]{2,1,0:T(8,128)S(1)} %get-tuple-element.54.mine, f32[4,8,384]{2,1,0:T(8,128)S(1)} %collective-permute-done.8.pair, ...), custom_call_target="tpu_custom_call" | custom-call | tf_op jit(solution)/shard_map/pallas_call | solution.py:463
  (6 shorter events, 0.0 us)
Async XLA Ops:
  3.4 11.7 %collective-permute-start.2 = (f32[2320,128]{1,0:T(8,128)S(1)}, f32[2320,128]{1,0:T(8,128)S(1)}, u32[]{:S(2)}, u32[]{:S(2)}) collective-permute-start(f32[2320,128]{1,0:T(8,128)S(1)} %get-tuple-element.34.st), channel_id=1, source_target_pairs={{0,16},{16,0},{32,48},{48,32},{64,80},{80,64},{96,112},{112,96},{1... | collective-permute-start | bytes 3563528 | tf_op jit(solution)/shard_map/ppermute | solution.py:428
  4.1 6.4 %collective-permute-start = (f32[248,128]{1,0:T(8,128)S(1)}, f32[248,128]{1,0:T(8,128)S(1)}, u32[]{:S(2)}, u32[]{:S(2)}) collective-permute-start(f32[248,128]{1,0:T(8,128)S(1)} %get-tuple-element.32), channel_id=1, source_target_pairs={{0,1},{1,0},{2,3},{3,2},{4,5},{5,4},{6,7},{7,6},{8,9},{9,8},{10,11... | collective-permute-start | bytes 380936 | tf_op jit(solution)/shard_map/ppermute | solution.py:429
  5.8 9.3 %collective-permute-start.1 = (f32[248,128]{1,0:T(8,128)S(1)}, f32[248,128]{1,0:T(8,128)S(1)}, u32[]{:S(2)}, u32[]{:S(2)}) collective-permute-start(f32[248,128]{1,0:T(8,128)S(1)} %get-tuple-element.33), channel_id=1, source_target_pairs={{1,2},{2,1},{3,4},{4,3},{5,6},{6,5},{7,8},{8,7},{9,10},{10,9},{11,... | collective-permute-start | bytes 380936 | tf_op jit(solution)/shard_map/ppermute | solution.py:430
  15.0 52.5 %collective-permute-start.3 = (f32[1744,128]{1,0:T(8,128)S(1)}, f32[1744,128]{1,0:T(8,128)S(1)}, u32[]{:S(2)}, u32[]{:S(2)}) collective-permute-start(f32[1744,128]{1,0:T(8,128)S(1)} %get-tuple-element.38), channel_id=1, source_target_pairs={{16,32},{32,16},{48,64},{64,48},{80,96},{96,80},{112,128},{128,112... | collective-permute-start | bytes 2678792 | tf_op jit(solution)/shard_map/ppermute | solution.py:434
  24.1 8.4 %collective-permute-start.6 = (f32[248,128]{1,0:T(8,128)S(1)}, f32[248,128]{1,0:T(8,128)S(1)}, u32[]{:S(2)}, u32[]{:S(2)}) collective-permute-start(f32[248,128]{1,0:T(8,128)S(1)} %collective-permute-done.edge_a), channel_id=1, source_target_pairs={{0,16},{16,0},{32,48},{48,32},{64,80},{80,64},{96,112},{112,96},{1... | collective-permute-start | bytes 380936 | tf_op jit(solution)/shard_map/ppermute | solution.py:437
  24.2 8.3 %collective-permute-start.7 = (f32[248,128]{1,0:T(8,128)S(1)}, f32[248,128]{1,0:T(8,128)S(1)}, u32[]{:S(2)}, u32[]{:S(2)}) collective-permute-start(f32[248,128]{1,0:T(8,128)S(1)} %collective-permute-done.1.edge_b), channel_id=1, source_target_pairs={{0,16},{16,0},{32,48},{48,32},{64,80},{80,64},{96,112},{112,96},{1... | collective-permute-start | bytes 380936 | tf_op jit(solution)/shard_map/ppermute | solution.py:438
  24.7 40.6 %collective-permute-start.4 = (f32[200,128]{1,0:T(8,128)S(1)}, f32[200,128]{1,0:T(8,128)S(1)}, u32[]{:S(2)}, u32[]{:S(2)}) collective-permute-start(f32[200,128]{1,0:T(8,128)S(1)} %get-tuple-element.39), channel_id=1, source_target_pairs={{16,33},{17,32},{18,35},{19,34},{20,37},{21,36},{22,39},{23,38},{2... | collective-permute-start | bytes 307208 | tf_op jit(solution)/shard_map/ppermute | solution.py:435
  26.6 40.9 %collective-permute-start.5 = (f32[200,128]{1,0:T(8,128)S(1)}, f32[200,128]{1,0:T(8,128)S(1)}, u32[]{:S(2)}, u32[]{:S(2)}) collective-permute-start(f32[200,128]{1,0:T(8,128)S(1)} %get-tuple-element.40), channel_id=1, source_target_pairs={{17,34},{18,33},{19,36},{20,35},{21,38},{22,37},{23,40},{24,39},{2... | collective-permute-start | bytes 307208 | tf_op jit(solution)/shard_map/ppermute | solution.py:436
  73.6 6.6 %collective-permute-start.8 = (f32[4,8,384]{2,1,0:T(8,128)S(1)}, f32[4,8,384]{2,1,0:T(8,128)S(1)}, u32[]{:S(2)}, u32[]{:S(2)}) collective-permute-start(f32[4,8,384]{2,1,0:T(8,128)S(1)} %get-tuple-element.54.mine), channel_id=1, source_target_pairs={{0,16},{16,0},{32,48},{48,32},{64,80},{80,64},{96,112},{112,96},{1... | collective-permute-start | bytes 147464 | tf_op jit(solution)/shard_map/ppermute | solution.py:458
  80.2 12.2 %collective-permute-start.9 = (f32[2,4,8,384]{3,2,1,0:T(8,128)S(1)}, f32[2,4,8,384]{3,2,1,0:T(8,128)S(1)}, u32[]{:S(2)}, u32[]{:S(2)}) collective-permute-start(f32[2,4,8,384]{3,2,1,0:T(8,128)S(1)} %pad_maximum_fusion), channel_id=1, source_target_pairs={{16,32},{32,16},{48,64},{64,48},{80,96},{96,80},{112,128},{128,112... | collective-permute-start | bytes 294920 | tf_op jit(solution)/shard_map/ppermute | solution.py:459
  86.2 0.7 collective-permute-start.10
  92.4 2.4 %collective-permute-start.11 = (f32[2,4,8,384]{3,2,1,0:T(8,128)S(1)}, f32[2,4,8,384]{3,2,1,0:T(8,128)S(1)}, u32[]{:S(2)}, u32[]{:S(2)}) collective-permute-start(f32[2,4,8,384]{3,2,1,0:T(8,128)S(1)} %collective-permute-done.9.remote), channel_id=1, source_target_pairs={{0,16},{16,0},{32,48},{48,32},{64,80},{80,64},{96,112},{112,96},{1... | collective-permute-start | bytes 294920 | tf_op jit(solution)/shard_map/ppermute | solution.py:461

commit v7 on v6

--- a/solution.py
+++ b/solution.py
@@ -20,6 +20,7 @@
 ROWS = 8
 COLS = 256
 EXT = 128
+EARLY_COST = 7_500_000_000
 WIDE = COLS + EXT
 HALO = 6
 SIZES = (48,)
@@ -382,7 +383,7 @@
     return [p for a, b in pairs for p in ((a, b), (b, a))]
 
 
-def call(body, outs, scratch=(), ins=0, space=pltpu.VMEM, away=0, aliases={}):
+def call(body, outs, scratch=(), ins=0, space=pltpu.VMEM, away=0, aliases={}, flops=None):
     vmem = pl.BlockSpec(memory_space=pltpu.VMEM)
     smem = pl.BlockSpec(memory_space=pltpu.SMEM)
     return pl.pallas_call(
@@ -392,6 +393,7 @@
         out_specs=[pl.BlockSpec(memory_space=pltpu.HBM)] * away + [vmem] * (len(outs) - away),
         scratch_shapes=[pltpu.VMEM(s, F32) if isinstance(s, tuple) else s for s in scratch],
         input_output_aliases=aliases,
+        cost_estimate=flops and pl.CostEstimate(flops=flops, transcendentals=0, bytes_accessed=0),
         compiler_params=pltpu.CompilerParams(vmem_limit_bytes=16 * 1024 * 1024),
     )
 
@@ -428,12 +430,10 @@
     stp = lax.ppermute(st, "gx", on_chip)
     edge_a = lax.ppermute(edge_a, "gy", even)
     edge_b = lax.ppermute(edge_b, "gy", odd)
-    edge_a, edge_b, stp, corner_a, corner_b, *mains = lax.optimization_barrier(
-        (edge_a, edge_b, stp, corner_a, corner_b, *mains)
-    )
-    main = [lax.ppermute(m, "gx", next_chip) for m in mains]
     corner_a = lax.ppermute(corner_a, ("gx", "gy"), both(next_chip, even))
     corner_b = lax.ppermute(corner_b, ("gx", "gy"), both(next_chip, odd))
+    stp, *mains = lax.optimization_barrier((stp, *mains))
+    main = [lax.ppermute(m, "gx", next_chip) for m in mains]
     edgep_a = lax.ppermute(edge_a, "gx", on_chip)
     edgep_b = lax.ppermute(edge_b, "gx", on_chip)
 
@@ -444,6 +444,7 @@
         shapes + [(3, ROWS, WIDE)] + [field] * 3,
         [(2, LEV, WIDE), (ROWS, WIDE)],
         ins=7,
+        flops=EARLY_COST,
     )(scalars, st, stp, edge_a, edge_b, edgep_a, edgep_b, plane)
     shift = 1 + CHUNKS + 2
     *_, flows, u, v, s = call(

time: 99.8 us -> 96.7 us (0.969)
  the two profiles are of different devices: /device:TPU:31 before, /device:TPU:23 now
where the time goes in v7:
time: 96.7 us; the launch traced here: 96.4 us
  starting transfers between devices  56.1 us (58%)
  waiting for transfers between devices  19.9 us (21%)
  Pallas kernels  19.5 us (20%)
    ppermute x1, starting transfers between devices, local(): corner_a = lax.ppermute(corner_a, ('gx', 'gy'), both(next_chip, even))  25.8 us
    ppermute x1, waiting for transfers between devices, local(): corner_a = lax.ppermute(corner_a, ('gx', 'gy'), both(next_chip, even))  9.43 us
    ppermute x1, starting transfers between devices, local(): pair = lax.ppermute(flows, 'gx', on_chip)  9.4 us
    ppermute x1, waiting for transfers between devices, local(): remote = lax.ppermute(jnp.stack([flows, pair]), 'gx', next_chip)  7.53 us
    ppermute x1, starting transfers between devices, local(): main = [lax.ppermute(m, 'gx', next_chip) for m in mains]  7.39 us
    pallas_call x1, Pallas kernels, local(): call(early_kernel, shapes + [(3, ROWS, WIDE)] + [field] * 3, [(2, LEV, WI...  6.17 us
    pallas_call x1, Pallas kernels, local(): call(late_kernel, shapes + [field] * 3, [(2, LEV, WIDE), (ROWS, WIDE)], i...  6.05 us
    pallas_call x1, Pallas kernels, local(): call(solve_kernel, [(LEV, ROWS, COLS)] * 3 + [(ROWS, COLS)], [(4, 56, WID...  4.66 us
  transfers between devices with their start and end apart: 12, of which 5 were waited for; matrix products, arithmetic and copies ran while one was open for 0% of the time, Pallas kernels for 6%

profile of v7, /device:TPU:23, one launch (start us, length us, event | category | flops | bytes accessed | tf_op | source)
XLA Modules:
  0.0 96.4 jit_solution(3919069074721987670)
XLA Ops:
  0.6 0.1 pad_add_fusion.sc
  0.7 2.6 %shard_map.102 = (f32[248,128]{1,0:T(8,128)S(1)}, f32[248,128]{1,0:T(8,128)S(1)}, f32[200,128]{1,0:T(8,128)S(1)}, f32[200,128]{1,0:T(8,128)S(1)}, f32[1744,128]{...) custom-call(s32[3]{0:T(128)S(1)} %pad_add_fusion.sc, f32[48,8,256]{2,1,0:T(8,128)} %u.1, ...), custom_call_target="tpu_custom_call" | custom-call | tf_op jit(solution)/shard_map/pallas_call | solution.py:415
  3.4 0.8 collective-permute-start
  4.1 1.7 %collective-permute-start.4 = (f32[248,128]{1,0:T(8,128)S(1)}, f32[248,128]{1,0:T(8,128)S(1)}, u32[]{:S(2)}, u32[]{:S(2)}) collective-permute-start(f32[248,128]{1,0:T(8,128)S(1)} %get-tuple-element.34), channel_id=1, source_target_pairs={{0,1},{1,0},{2,3},{3,2},{4,5},{5,4},{6,7},{7,6},{8,9},{9,8},{10,11... | collective-permute-start | bytes 380936 | tf_op jit(solution)/shard_map/ppermute | solution.py:431
  5.8 4.5 %collective-permute-start.5 = (f32[248,128]{1,0:T(8,128)S(1)}, f32[248,128]{1,0:T(8,128)S(1)}, u32[]{:S(2)}, u32[]{:S(2)}) collective-permute-start(f32[248,128]{1,0:T(8,128)S(1)} %get-tuple-element.35), channel_id=1, source_target_pairs={{1,2},{2,1},{3,4},{4,3},{5,6},{6,5},{7,8},{8,7},{9,10},{10,9},{11,... | collective-permute-start | bytes 380936 | tf_op jit(solution)/shard_map/ppermute | solution.py:432
  10.3 0.0 collective-permute-done.stp
  10.3 7.4 %collective-permute-start.1 = (f32[1744,128]{1,0:T(8,128)S(1)}, f32[1744,128]{1,0:T(8,128)S(1)}, u32[]{:S(2)}, u32[]{:S(2)}) collective-permute-start(f32[1744,128]{1,0:T(8,128)S(1)} %get-tuple-element.30), channel_id=1, source_target_pairs={{16,32},{32,16},{48,64},{64,48},{80,96},{96,80},{112,128},{128,112... | collective-permute-start | bytes 2678792 | tf_op jit(solution)/shard_map/ppermute | solution.py:436
  17.7 0.0 collective-permute-done.4.edge_a
  17.7 0.2 collective-permute-start.6
  17.9 0.4 collective-permute-start.7
  18.3 25.8 %collective-permute-start.2 = (f32[200,128]{1,0:T(8,128)S(1)}, f32[200,128]{1,0:T(8,128)S(1)}, u32[]{:S(2)}, u32[]{:S(2)}) collective-permute-start(f32[200,128]{1,0:T(8,128)S(1)} %get-tuple-element.31), channel_id=1, source_target_pairs={{16,33},{17,32},{18,35},{19,34},{20,37},{21,36},{22,39},{23,38},{2... | collective-permute-start | bytes 307208 | tf_op jit(solution)/shard_map/ppermute | solution.py:433
  44.1 1.9 %collective-permute-start.3 = (f32[200,128]{1,0:T(8,128)S(1)}, f32[200,128]{1,0:T(8,128)S(1)}, u32[]{:S(2)}, u32[]{:S(2)}) collective-permute-start(f32[200,128]{1,0:T(8,128)S(1)} %get-tuple-element.32), channel_id=1, source_target_pairs={{17,34},{18,33},{19,36},{20,35},{21,38},{22,37},{23,40},{24,39},{2... | collective-permute-start | bytes 307208 | tf_op jit(solution)/shard_map/ppermute | solution.py:434
  46.1 6.2 %shard_map.103 = (f32[3,24,48,384]{3,2,1,0:T(8,128)S(1)}, f32[3,16,48,384]{3,2,1,0:T(8,128)S(1)}, f32[3,12,48,384]{3,2,1,0:T(8,128)S(1)}, f32[24,8,384]{2,1,0:T(...) custom-call(s32[3]{0:T(128)S(1)} %pad_add_fusion.sc, ...), custom_call_target="tpu_custom_call" | custom-call | flops 7500000256 | tf_op jit(solution)/shard_map/pallas_call | solution.py:442
  52.2 9.4 %collective-permute-done.2.rest_1_ = f32[200,128]{1,0:T(8,128)S(1)} collective-permute-done((f32[200,128]{1,0:T(8,128)S(1)}, f32[200,128]{1,0:T(8,128)S(1)}, u32[]{:S(2)}, u32[]{:S(2)}) %collective-permute-start.2) | collective-permute-done | bytes 102432 | tf_op jit(solution)/shard_map/ppermute | solution.py:433
  61.7 1.1 %collective-permute-done.3.rest_2_ = f32[200,128]{1,0:T(8,128)S(1)} collective-permute-done((f32[200,128]{1,0:T(8,128)S(1)}, f32[200,128]{1,0:T(8,128)S(1)}, u32[]{:S(2)}, u32[]{:S(2)}) %collective-permute-start.3) | collective-permute-done | bytes 102432 | tf_op jit(solution)/shard_map/ppermute | solution.py:434
  62.8 6.1 %shard_map.104 = (f32[3,24,48,384]{3,2,1,0:T(8,128)S(1)}, f32[3,16,48,384]{3,2,1,0:T(8,128)S(1)}, f32[3,12,48,384]{3,2,1,0:T(8,128)S(1)}, f32[24,8,384]{2,1,0:T(...) custom-call(s32[3]{0:T(128)S(1)} %pad_add_fusion.sc, ...), custom_call_target="tpu_custom_call", output_to_operand_aliasing={{0}: (4, {}), {1}: (5, {}), {2}: (6, {}), {3}: (7, {}), {4}... | custom-call | tf_op jit(solution)/shard_map/pallas_call | solution.py:450
  68.8 9.4 %collective-permute-start.8 = (f32[4,8,384]{2,1,0:T(8,128)S(1)}, f32[4,8,384]{2,1,0:T(8,128)S(1)}, u32[]{:S(2)}, u32[]{:S(2)}) collective-permute-start(f32[4,8,384]{2,1,0:T(8,128)S(1)} %get-tuple-element.46.mine), channel_id=1, source_target_pairs={{0,16},{16,0},{32,48},{48,32},{64,80},{80,64},{96,112},{112,96},{1... | collective-permute-start | bytes 147464 | tf_op jit(solution)/shard_map/ppermute | solution.py:459
  78.2 0.9 collective-permute-done.8.pair
  79.1 1.9 %collective-permute-start.9 = (f32[2,4,8,384]{3,2,1,0:T(8,128)S(1)}, f32[2,4,8,384]{3,2,1,0:T(8,128)S(1)}, u32[]{:S(2)}, u32[]{:S(2)}) collective-permute-start(f32[2,4,8,384]{3,2,1,0:T(8,128)S(1)} %pad_maximum_fusion), channel_id=1, source_target_pairs={{16,32},{32,16},{48,64},{64,48},{80,96},{96,80},{112,128},{128,112... | collective-permute-start | bytes 294920 | tf_op jit(solution)/shard_map/ppermute | solution.py:460
  81.0 0.7 collective-permute-start.10
  81.7 7.5 %collective-permute-done.9.remote = f32[2,4,8,384]{3,2,1,0:T(8,128)S(1)} collective-permute-done((f32[2,4,8,384]{3,2,1,0:T(8,128)S(1)}, f32[2,4,8,384]{3,2,1,0:T(8,128)S(1)}, u32[]{:S(2)}, u32[]{:S(2)}) %collective-permute-start.9) | collective-permute-done | bytes 98336 | tf_op jit(solution)/shard_map/ppermute | solution.py:460
  89.2 1.5 %collective-permute-start.11 = (f32[2,4,8,384]{3,2,1,0:T(8,128)S(1)}, f32[2,4,8,384]{3,2,1,0:T(8,128)S(1)}, u32[]{:S(2)}, u32[]{:S(2)}) collective-permute-start(f32[2,4,8,384]{3,2,1,0:T(8,128)S(1)} %collective-permute-done.9.remote), channel_id=1, source_target_pairs={{0,16},{16,0},{32,48},{48,32},{64,80},{80,64},{96,112},{112,96},{1... | collective-permute-start | bytes 294920 | tf_op jit(solution)/shard_map/ppermute | solution.py:462
  90.8 0.9 collective-permute-done.11.remote_pair
  91.7 4.7 %shard_map.105 = (f32[48,8,256]{2,1,0:T(8,128)}, f32[48,8,256]{2,1,0:T(8,128)}, f32[48,8,256]{2,1,0:T(8,128)}, f32[8,256]{1,0:T(8,128)}) custom-call(s32[3]{0:T(128)S(1)} %pad_add_fusion.sc, f32[4,8,384]{2,1,0:T(8,128)S(1)} %get-tuple-element.46.mine, f32[4,8,384]{2,1,0:T(8,128)S(1)} %collective-permute-done.8.pair, ...), custom_call_target="tpu_custom_call" | custom-call | tf_op jit(solution)/shard_map/pallas_call | solution.py:464
  (6 shorter events, 0.0 us)
Async XLA Ops:
  3.4 6.9 %collective-permute-start = (f32[2320,128]{1,0:T(8,128)S(1)}, f32[2320,128]{1,0:T(8,128)S(1)}, u32[]{:S(2)}, u32[]{:S(2)}) collective-permute-start(f32[2320,128]{1,0:T(8,128)S(1)} %get-tuple-element.28.st), channel_id=1, source_target_pairs={{0,16},{16,0},{32,48},{48,32},{64,80},{80,64},{96,112},{112,96},{1... | collective-permute-start | bytes 3563528 | tf_op jit(solution)/shard_map/ppermute | solution.py:430
  4.1 13.6 %collective-permute-start.4 = (f32[248,128]{1,0:T(8,128)S(1)}, f32[248,128]{1,0:T(8,128)S(1)}, u32[]{:S(2)}, u32[]{:S(2)}) collective-permute-start(f32[248,128]{1,0:T(8,128)S(1)} %get-tuple-element.34), channel_id=1, source_target_pairs={{0,1},{1,0},{2,3},{3,2},{4,5},{5,4},{6,7},{7,6},{8,9},{9,8},{10,11... | collective-permute-start | bytes 380936 | tf_op jit(solution)/shard_map/ppermute | solution.py:431
  5.8 12.1 %collective-permute-start.5 = (f32[248,128]{1,0:T(8,128)S(1)}, f32[248,128]{1,0:T(8,128)S(1)}, u32[]{:S(2)}, u32[]{:S(2)}) collective-permute-start(f32[248,128]{1,0:T(8,128)S(1)} %get-tuple-element.35), channel_id=1, source_target_pairs={{1,2},{2,1},{3,4},{4,3},{5,6},{6,5},{7,8},{8,7},{9,10},{10,9},{11,... | collective-permute-start | bytes 380936 | tf_op jit(solution)/shard_map/ppermute | solution.py:432
  10.3 52.5 %collective-permute-start.1 = (f32[1744,128]{1,0:T(8,128)S(1)}, f32[1744,128]{1,0:T(8,128)S(1)}, u32[]{:S(2)}, u32[]{:S(2)}) collective-permute-start(f32[1744,128]{1,0:T(8,128)S(1)} %get-tuple-element.30), channel_id=1, source_target_pairs={{16,32},{32,16},{48,64},{64,48},{80,96},{96,80},{112,128},{128,112... | collective-permute-start | bytes 2678792 | tf_op jit(solution)/shard_map/ppermute | solution.py:436
  17.7 28.4 %collective-permute-start.6 = (f32[248,128]{1,0:T(8,128)S(1)}, f32[248,128]{1,0:T(8,128)S(1)}, u32[]{:S(2)}, u32[]{:S(2)}) collective-permute-start(f32[248,128]{1,0:T(8,128)S(1)} %collective-permute-done.4.edge_a), channel_id=1, source_target_pairs={{0,16},{16,0},{32,48},{48,32},{64,80},{80,64},{96,112},{112,96},{1... | collective-permute-start | bytes 380936 | tf_op jit(solution)/shard_map/ppermute | solution.py:437
  17.9 28.1 %collective-permute-start.7 = (f32[248,128]{1,0:T(8,128)S(1)}, f32[248,128]{1,0:T(8,128)S(1)}, u32[]{:S(2)}, u32[]{:S(2)}) collective-permute-start(f32[248,128]{1,0:T(8,128)S(1)} %collective-permute-done.5.edge_b), channel_id=1, source_target_pairs={{0,16},{16,0},{32,48},{48,32},{64,80},{80,64},{96,112},{112,96},{1... | collective-permute-start | bytes 380936 | tf_op jit(solution)/shard_map/ppermute | solution.py:438
  18.3 43.4 %collective-permute-start.2 = (f32[200,128]{1,0:T(8,128)S(1)}, f32[200,128]{1,0:T(8,128)S(1)}, u32[]{:S(2)}, u32[]{:S(2)}) collective-permute-start(f32[200,128]{1,0:T(8,128)S(1)} %get-tuple-element.31), channel_id=1, source_target_pairs={{16,33},{17,32},{18,35},{19,34},{20,37},{21,36},{22,39},{23,38},{2... | collective-permute-start | bytes 307208 | tf_op jit(solution)/shard_map/ppermute | solution.py:433
  44.1 18.7 %collective-permute-start.3 = (f32[200,128]{1,0:T(8,128)S(1)}, f32[200,128]{1,0:T(8,128)S(1)}, u32[]{:S(2)}, u32[]{:S(2)}) collective-permute-start(f32[200,128]{1,0:T(8,128)S(1)} %get-tuple-element.32), channel_id=1, source_target_pairs={{17,34},{18,33},{19,36},{20,35},{21,38},{22,37},{23,40},{24,39},{2... | collective-permute-start | bytes 307208 | tf_op jit(solution)/shard_map/ppermute | solution.py:434
  68.8 10.3 %collective-permute-start.8 = (f32[4,8,384]{2,1,0:T(8,128)S(1)}, f32[4,8,384]{2,1,0:T(8,128)S(1)}, u32[]{:S(2)}, u32[]{:S(2)}) collective-permute-start(f32[4,8,384]{2,1,0:T(8,128)S(1)} %get-tuple-element.46.mine), channel_id=1, source_target_pairs={{0,16},{16,0},{32,48},{48,32},{64,80},{80,64},{96,112},{112,96},{1... | collective-permute-start | bytes 147464 | tf_op jit(solution)/shard_map/ppermute | solution.py:459
  79.1 10.1 %collective-permute-start.9 = (f32[2,4,8,384]{3,2,1,0:T(8,128)S(1)}, f32[2,4,8,384]{3,2,1,0:T(8,128)S(1)}, u32[]{:S(2)}, u32[]{:S(2)}) collective-permute-start(f32[2,4,8,384]{3,2,1,0:T(8,128)S(1)} %pad_maximum_fusion), channel_id=1, source_target_pairs={{16,32},{32,16},{48,64},{64,48},{80,96},{96,80},{112,128},{128,112... | collective-permute-start | bytes 294920 | tf_op jit(solution)/shard_map/ppermute | solution.py:460
  81.0 0.7 collective-permute-start.10
  89.2 2.5 %collective-permute-start.11 = (f32[2,4,8,384]{3,2,1,0:T(8,128)S(1)}, f32[2,4,8,384]{3,2,1,0:T(8,128)S(1)}, u32[]{:S(2)}, u32[]{:S(2)}) collective-permute-start(f32[2,4,8,384]{3,2,1,0:T(8,128)S(1)} %collective-permute-done.9.remote), channel_id=1, source_target_pairs={{0,16},{16,0},{32,48},{48,32},{64,80},{80,64},{96,112},{112,96},{1... | collective-permute-start | bytes 294920 | tf_op jit(solution)/shard_map/ppermute | solution.py:462

commit v8 on v7

--- a/solution.py
+++ b/solution.py
@@ -20,7 +20,7 @@
 ROWS = 8
 COLS = 256
 EXT = 128
-EARLY_COST = 7_500_000_000
+EARLY_COST = 7_600_000_000
 WIDE = COLS + EXT
 HALO = 6
 SIZES = (48,)
@@ -434,6 +434,7 @@
     corner_b = lax.ppermute(corner_b, ("gx", "gy"), both(next_chip, odd))
     stp, *mains = lax.optimization_barrier((stp, *mains))
     main = [lax.ppermute(m, "gx", next_chip) for m in mains]
+    edge_a, edge_b, corner_a, corner_b = lax.optimization_barrier((edge_a, edge_b, corner_a, corner_b))
     edgep_a = lax.ppermute(edge_a, "gx", on_chip)
     edgep_b = lax.ppermute(edge_b, "gx", on_chip)
 

time: 96.7 us -> 101 us (1.044)
  the two profiles are of different devices: /device:TPU:23 before, /device:TPU:31 now
where the time goes in v8:
time: 101 us
  waiting for transfers between devices  48.5 us (48%)
  starting transfers between devices  31.7 us (31%)
  Pallas kernels  19.5 us (19%)
    ppermute x1, waiting for transfers between devices, local(): corner_b = lax.ppermute(corner_b, ('gx', 'gy'), both(next_chip, odd))  37.7 us
    ppermute x1, waiting for transfers between devices, local(): remote = lax.ppermute(jnp.stack([flows, pair]), 'gx', next_chip)  7.53 us
    pallas_call x1, Pallas kernels, local(): call(early_kernel, shapes + [(3, ROWS, WIDE)] + [field] * 3, [(2, LEV, WI...  6.16 us
    pallas_call x1, Pallas kernels, local(): call(late_kernel, shapes + [field] * 3, [(2, LEV, WIDE), (ROWS, WIDE)], i...  6.06 us
    ppermute x1, starting transfers between devices, local(): edgep_a = lax.ppermute(edge_a, 'gx', on_chip)  5.97 us
    ppermute x1, starting transfers between devices, local(): corner_a = lax.ppermute(corner_a, ('gx', 'gy'), both(next_chip, even))  5.87 us
    ppermute x1, starting transfers between devices, local(): main = [lax.ppermute(m, 'gx', next_chip) for m in mains]  5.48 us
    ppermute x1, starting transfers between devices, local(): edge_b = lax.ppermute(edge_b, 'gy', odd)  4.77 us
  transfers between devices with their start and end apart: 12, of which 6 were waited for; matrix products, arithmetic and copies ran while one was open for 0% of the time, Pallas kernels for 6%

profile of v8, /device:TPU:31, one launch (start us, length us, event | category | flops | bytes accessed | tf_op | source)
XLA Modules:
  0.0 100.5 jit_solution(10242896445997611912)
XLA Ops:
  0.6 0.1 pad_add_fusion.sc
  0.7 2.6 %shard_map.102 = (f32[248,128]{1,0:T(8,128)S(1)}, f32[248,128]{1,0:T(8,128)S(1)}, f32[200,128]{1,0:T(8,128)S(1)}, f32[200,128]{1,0:T(8,128)S(1)}, f32[1744,128]{...) custom-call(s32[3]{0:T(128)S(1)} %pad_add_fusion.sc, f32[48,8,256]{2,1,0:T(8,128)} %u.1, ...), custom_call_target="tpu_custom_call" | custom-call | tf_op jit(solution)/shard_map/pallas_call | solution.py:415
  3.4 0.8 collective-permute-start
  4.1 1.7 %collective-permute-start.2 = (f32[248,128]{1,0:T(8,128)S(1)}, f32[248,128]{1,0:T(8,128)S(1)}, u32[]{:S(2)}, u32[]{:S(2)}) collective-permute-start(f32[248,128]{1,0:T(8,128)S(1)} %get-tuple-element.35), channel_id=1, source_target_pairs={{0,1},{1,0},{2,3},{3,2},{4,5},{5,4},{6,7},{7,6},{8,9},{9,8},{10,11... | collective-permute-start | bytes 380936 | tf_op jit(solution)/shard_map/ppermute | solution.py:431
  5.8 4.8 %collective-permute-start.3 = (f32[248,128]{1,0:T(8,128)S(1)}, f32[248,128]{1,0:T(8,128)S(1)}, u32[]{:S(2)}, u32[]{:S(2)}) collective-permute-start(f32[248,128]{1,0:T(8,128)S(1)} %get-tuple-element.36), channel_id=1, source_target_pairs={{1,2},{2,1},{3,4},{4,3},{5,6},{6,5},{7,8},{8,7},{9,10},{10,9},{11,... | collective-permute-start | bytes 380936 | tf_op jit(solution)/shard_map/ppermute | solution.py:432
  10.6 5.9 %collective-permute-start.4 = (f32[200,128]{1,0:T(8,128)S(1)}, f32[200,128]{1,0:T(8,128)S(1)}, u32[]{:S(2)}, u32[]{:S(2)}) collective-permute-start(f32[200,128]{1,0:T(8,128)S(1)} %get-tuple-element.37), channel_id=1, source_target_pairs={{16,33},{17,32},{18,35},{19,34},{20,37},{21,36},{22,39},{23,38},{2... | collective-permute-start | bytes 307208 | tf_op jit(solution)/shard_map/ppermute | solution.py:433
  16.4 2.8 %collective-permute-start.5 = (f32[200,128]{1,0:T(8,128)S(1)}, f32[200,128]{1,0:T(8,128)S(1)}, u32[]{:S(2)}, u32[]{:S(2)}) collective-permute-start(f32[200,128]{1,0:T(8,128)S(1)} %get-tuple-element.38), channel_id=1, source_target_pairs={{17,34},{18,33},{19,36},{20,35},{21,38},{22,37},{23,40},{24,39},{2... | collective-permute-start | bytes 307208 | tf_op jit(solution)/shard_map/ppermute | solution.py:434
  19.3 5.5 %collective-permute-start.1 = (f32[1744,128]{1,0:T(8,128)S(1)}, f32[1744,128]{1,0:T(8,128)S(1)}, u32[]{:S(2)}, u32[]{:S(2)}) collective-permute-start(f32[1744,128]{1,0:T(8,128)S(1)} %get-tuple-element.34), channel_id=1, source_target_pairs={{16,32},{32,16},{48,64},{64,48},{80,96},{96,80},{112,128},{128,112... | collective-permute-start | bytes 2678792 | tf_op jit(solution)/shard_map/ppermute | solution.py:436
  24.7 0.0 collective-permute-done.4.rest_1_
  24.8 37.7 %collective-permute-done.5.rest_2_ = f32[200,128]{1,0:T(8,128)S(1)} collective-permute-done((f32[200,128]{1,0:T(8,128)S(1)}, f32[200,128]{1,0:T(8,128)S(1)}, u32[]{:S(2)}, u32[]{:S(2)}) %collective-permute-start.5) | collective-permute-done | bytes 102432 | tf_op jit(solution)/shard_map/ppermute | solution.py:434
  62.4 6.0 %collective-permute-start.6 = (f32[248,128]{1,0:T(8,128)S(1)}, f32[248,128]{1,0:T(8,128)S(1)}, u32[]{:S(2)}, u32[]{:S(2)}) collective-permute-start(f32[248,128]{1,0:T(8,128)S(1)} %collective-permute-done.2.edge_a), channel_id=1, source_target_pairs={{0,16},{16,0},{32,48},{48,32},{64,80},{80,64},{96,112},{112,96},{1... | collective-permute-start | bytes 380936 | tf_op jit(solution)/shard_map/ppermute | solution.py:438
  68.4 0.1 collective-permute-start.7
  68.5 0.9 collective-permute-done.6.edgep_a
  69.4 0.4 collective-permute-done.7.edgep_b
  69.8 6.2 %shard_map.103 = (f32[3,24,48,384]{3,2,1,0:T(8,128)S(1)}, f32[3,16,48,384]{3,2,1,0:T(8,128)S(1)}, f32[3,12,48,384]{3,2,1,0:T(8,128)S(1)}, f32[24,8,384]{2,1,0:T(...) custom-call(s32[3]{0:T(128)S(1)} %pad_add_fusion.sc, ...), custom_call_target="tpu_custom_call" | custom-call | flops 7600000000 | tf_op jit(solution)/shard_map/pallas_call | solution.py:443
  75.9 6.1 %shard_map.104 = (f32[3,24,48,384]{3,2,1,0:T(8,128)S(1)}, f32[3,16,48,384]{3,2,1,0:T(8,128)S(1)}, f32[3,12,48,384]{3,2,1,0:T(8,128)S(1)}, f32[24,8,384]{2,1,0:T(...) custom-call(s32[3]{0:T(128)S(1)} %pad_add_fusion.sc, ...), custom_call_target="tpu_custom_call", output_to_operand_aliasing={{0}: (4, {}), {1}: (5, {}), {2}: (6, {}), {3}: (7, {}), {4}... | custom-call | tf_op jit(solution)/shard_map/pallas_call | solution.py:451
  82.0 0.3 collective-permute-start.8
  82.3 1.0 %collective-permute-done.8.pair = f32[4,8,384]{2,1,0:T(8,128)S(1)} collective-permute-done((f32[4,8,384]{2,1,0:T(8,128)S(1)}, f32[4,8,384]{2,1,0:T(8,128)S(1)}, u32[]{:S(2)}, u32[]{:S(2)}) %collective-permute-start.8) | collective-permute-done | bytes 49184 | tf_op jit(solution)/shard_map/ppermute | solution.py:460
  83.3 1.9 %collective-permute-start.9 = (f32[2,4,8,384]{3,2,1,0:T(8,128)S(1)}, f32[2,4,8,384]{3,2,1,0:T(8,128)S(1)}, u32[]{:S(2)}, u32[]{:S(2)}) collective-permute-start(f32[2,4,8,384]{3,2,1,0:T(8,128)S(1)} %pad_maximum_fusion), channel_id=1, source_target_pairs={{16,32},{32,16},{48,64},{64,48},{80,96},{96,80},{112,128},{128,112... | collective-permute-start | bytes 294920 | tf_op jit(solution)/shard_map/ppermute | solution.py:461
  85.3 0.7 collective-permute-start.10
  85.9 7.5 %collective-permute-done.9.remote = f32[2,4,8,384]{3,2,1,0:T(8,128)S(1)} collective-permute-done((f32[2,4,8,384]{3,2,1,0:T(8,128)S(1)}, f32[2,4,8,384]{3,2,1,0:T(8,128)S(1)}, u32[]{:S(2)}, u32[]{:S(2)}) %collective-permute-start.9) | collective-permute-done | bytes 98336 | tf_op jit(solution)/shard_map/ppermute | solution.py:461
  93.5 1.4 %collective-permute-start.11 = (f32[2,4,8,384]{3,2,1,0:T(8,128)S(1)}, f32[2,4,8,384]{3,2,1,0:T(8,128)S(1)}, u32[]{:S(2)}, u32[]{:S(2)}) collective-permute-start(f32[2,4,8,384]{3,2,1,0:T(8,128)S(1)} %collective-permute-done.9.remote), channel_id=1, source_target_pairs={{0,16},{16,0},{32,48},{48,32},{64,80},{80,64},{96,112},{112,96},{1... | collective-permute-start | bytes 294920 | tf_op jit(solution)/shard_map/ppermute | solution.py:463
  94.9 0.9 collective-permute-done.11.remote_pair
  95.9 4.7 %shard_map.105 = (f32[48,8,256]{2,1,0:T(8,128)}, f32[48,8,256]{2,1,0:T(8,128)}, f32[48,8,256]{2,1,0:T(8,128)}, f32[8,256]{1,0:T(8,128)}) custom-call(s32[3]{0:T(128)S(1)} %pad_add_fusion.sc, f32[4,8,384]{2,1,0:T(8,128)S(1)} %get-tuple-element.54.mine, f32[4,8,384]{2,1,0:T(8,128)S(1)} %collective-permute-done.8.pair, ...), custom_call_target="tpu_custom_call" | custom-call | tf_op jit(solution)/shard_map/pallas_call | solution.py:465
  (6 shorter events, 0.0 us)
Async XLA Ops:
  3.4 15.9 %collective-permute-start = (f32[2320,128]{1,0:T(8,128)S(1)}, f32[2320,128]{1,0:T(8,128)S(1)}, u32[]{:S(2)}, u32[]{:S(2)}) collective-permute-start(f32[2320,128]{1,0:T(8,128)S(1)} %get-tuple-element.32.st), channel_id=1, source_target_pairs={{0,16},{16,0},{32,48},{48,32},{64,80},{80,64},{96,112},{112,96},{1... | collective-permute-start | bytes 3563528 | tf_op jit(solution)/shard_map/ppermute | solution.py:430
  4.1 58.3 %collective-permute-start.2 = (f32[248,128]{1,0:T(8,128)S(1)}, f32[248,128]{1,0:T(8,128)S(1)}, u32[]{:S(2)}, u32[]{:S(2)}) collective-permute-start(f32[248,128]{1,0:T(8,128)S(1)} %get-tuple-element.35), channel_id=1, source_target_pairs={{0,1},{1,0},{2,3},{3,2},{4,5},{5,4},{6,7},{7,6},{8,9},{9,8},{10,11... | collective-permute-start | bytes 380936 | tf_op jit(solution)/shard_map/ppermute | solution.py:431
  5.8 56.7 %collective-permute-start.3 = (f32[248,128]{1,0:T(8,128)S(1)}, f32[248,128]{1,0:T(8,128)S(1)}, u32[]{:S(2)}, u32[]{:S(2)}) collective-permute-start(f32[248,128]{1,0:T(8,128)S(1)} %get-tuple-element.36), channel_id=1, source_target_pairs={{1,2},{2,1},{3,4},{4,3},{5,6},{6,5},{7,8},{8,7},{9,10},{10,9},{11,... | collective-permute-start | bytes 380936 | tf_op jit(solution)/shard_map/ppermute | solution.py:432
  10.6 14.2 %collective-permute-start.4 = (f32[200,128]{1,0:T(8,128)S(1)}, f32[200,128]{1,0:T(8,128)S(1)}, u32[]{:S(2)}, u32[]{:S(2)}) collective-permute-start(f32[200,128]{1,0:T(8,128)S(1)} %get-tuple-element.37), channel_id=1, source_target_pairs={{16,33},{17,32},{18,35},{19,34},{20,37},{21,36},{22,39},{23,38},{2... | collective-permute-start | bytes 307208 | tf_op jit(solution)/shard_map/ppermute | solution.py:433
  16.4 46.0 %collective-permute-start.5 = (f32[200,128]{1,0:T(8,128)S(1)}, f32[200,128]{1,0:T(8,128)S(1)}, u32[]{:S(2)}, u32[]{:S(2)}) collective-permute-start(f32[200,128]{1,0:T(8,128)S(1)} %get-tuple-element.38), channel_id=1, source_target_pairs={{17,34},{18,33},{19,36},{20,35},{21,38},{22,37},{23,40},{24,39},{2... | collective-permute-start | bytes 307208 | tf_op jit(solution)/shard_map/ppermute | solution.py:434
  19.3 56.7 %collective-permute-start.1 = (f32[1744,128]{1,0:T(8,128)S(1)}, f32[1744,128]{1,0:T(8,128)S(1)}, u32[]{:S(2)}, u32[]{:S(2)}) collective-permute-start(f32[1744,128]{1,0:T(8,128)S(1)} %get-tuple-element.34), channel_id=1, source_target_pairs={{16,32},{32,16},{48,64},{64,48},{80,96},{96,80},{112,128},{128,112... | collective-permute-start | bytes 2678792 | tf_op jit(solution)/shard_map/ppermute | solution.py:436
  62.4 7.0 %collective-permute-start.6 = (f32[248,128]{1,0:T(8,128)S(1)}, f32[248,128]{1,0:T(8,128)S(1)}, u32[]{:S(2)}, u32[]{:S(2)}) collective-permute-start(f32[248,128]{1,0:T(8,128)S(1)} %collective-permute-done.2.edge_a), channel_id=1, source_target_pairs={{0,16},{16,0},{32,48},{48,32},{64,80},{80,64},{96,112},{112,96},{1... | collective-permute-start | bytes 380936 | tf_op jit(solution)/shard_map/ppermute | solution.py:438
  68.4 1.3 %collective-permute-start.7 = (f32[248,128]{1,0:T(8,128)S(1)}, f32[248,128]{1,0:T(8,128)S(1)}, u32[]{:S(2)}, u32[]{:S(2)}) collective-permute-start(f32[248,128]{1,0:T(8,128)S(1)} %collective-permute-done.3.edge_b), channel_id=1, source_target_pairs={{0,16},{16,0},{32,48},{48,32},{64,80},{80,64},{96,112},{112,96},{1... | collective-permute-start | bytes 380936 | tf_op jit(solution)/shard_map/ppermute | solution.py:439
  82.0 1.3 %collective-permute-start.8 = (f32[4,8,384]{2,1,0:T(8,128)S(1)}, f32[4,8,384]{2,1,0:T(8,128)S(1)}, u32[]{:S(2)}, u32[]{:S(2)}) collective-permute-start(f32[4,8,384]{2,1,0:T(8,128)S(1)} %get-tuple-element.54.mine), channel_id=1, source_target_pairs={{0,16},{16,0},{32,48},{48,32},{64,80},{80,64},{96,112},{112,96},{1... | collective-permute-start | bytes 147464 | tf_op jit(solution)/shard_map/ppermute | solution.py:460
  83.3 10.1 %collective-permute-start.9 = (f32[2,4,8,384]{3,2,1,0:T(8,128)S(1)}, f32[2,4,8,384]{3,2,1,0:T(8,128)S(1)}, u32[]{:S(2)}, u32[]{:S(2)}) collective-permute-start(f32[2,4,8,384]{3,2,1,0:T(8,128)S(1)} %pad_maximum_fusion), channel_id=1, source_target_pairs={{16,32},{32,16},{48,64},{64,48},{80,96},{96,80},{112,128},{128,112... | collective-permute-start | bytes 294920 | tf_op jit(solution)/shard_map/ppermute | solution.py:461
  85.3 0.7 collective-permute-start.10
  93.5 2.4 %collective-permute-start.11 = (f32[2,4,8,384]{3,2,1,0:T(8,128)S(1)}, f32[2,4,8,384]{3,2,1,0:T(8,128)S(1)}, u32[]{:S(2)}, u32[]{:S(2)}) collective-permute-start(f32[2,4,8,384]{3,2,1,0:T(8,128)S(1)} %collective-permute-done.9.remote), channel_id=1, source_target_pairs={{0,16},{16,0},{32,48},{48,32},{64,80},{80,64},{96,112},{112,96},{1... | collective-permute-start | bytes 294920 | tf_op jit(solution)/shard_map/ppermute | solution.py:463

commit v9 on v5

--- a/solution.py
+++ b/solution.py
@@ -26,8 +26,9 @@
 CHUNKS = len(SIZES)
 STARTS = tuple(sum(SIZES[:c]) for c in range(CHUNKS))
 TILES = LEV // 8
-SLOT = 25
-SLOTS = 5
+SLOT = 7
+SLOTS = 18
+REACH = 25
 EDGE_TILES = -(-3 * ROWS // SLOTS)
 CORNER_TILES = -(-3 * HALO // SLOTS)
 F32 = jnp.float32
@@ -50,20 +51,20 @@
     return lax.broadcasted_iota(jnp.int32, shape, len(shape) - 1)
 
 
-def place(low, high, units, slot):
+def place(low, high, units, slot, width=SLOT):
     left, right = units
     lane = lanes(low.shape)
-    here = (lane >= SLOT * slot) & (lane < SLOT * slot + SLOT)
-    low = low if slot == 0 else pltpu.roll(low, SLOT * slot, 1)
-    high = pltpu.roll(high, SLOT * slot + SLOT, 1)
+    here = (lane >= width * slot) & (lane < width * slot + width)
+    low = low if slot == 0 else pltpu.roll(low, width * slot, 1)
+    high = pltpu.roll(high, width * slot + width, 1)
     return jnp.where(here, low, left), jnp.where(here, high, right)
 
 
-def unpack(high, low, slot):
+def unpack(high, low, slot, width=SLOT):
     lane = lanes(high.shape)
-    high = high if slot == 0 else pltpu.roll(high, 128 - SLOT * slot, 1)
-    low = pltpu.roll(low, 128 - SLOT - SLOT * slot, 1)
-    return jnp.where(lane < SLOT, high, jnp.where(lane >= 128 - SLOT, low, 0.0))
+    high = high if slot == 0 else pltpu.roll(high, 128 - width * slot, 1)
+    low = pltpu.roll(low, 128 - width - width * slot, 1)
+    return jnp.where(lane < width, high, jnp.where(lane >= 128 - width, low, 0.0))
 
 
 def ordered(first, second, flag):
@@ -150,7 +151,7 @@
 
 def rk_kernel(sc, st, stp, edge_a, edge_b, edgep_a, edgep_b, *rest):
     mains = rest[:CHUNKS]
-    corner_a, corner_b, plane, flows, east, north, salt, ext, one, two, counts, flat, remote, runs = rest[CHUNKS:]
+    corner_a, corner_b, plane, flows, side_a, side_b, east, north, salt, ext, one, two, counts, flat, remote, runs = rest[CHUNKS:]
     core = sc[1]
     north_odd = sc[2]
     beside = 16 * (1 - core)
@@ -281,6 +282,17 @@
     for f in range(2):
         flows[f] = flat[2] * (flows[f] * (1.0 / LEV))
         flows[2 + f] = flat[f]
+    units = (jnp.zeros((ROWS, 128), F32), jnp.zeros((ROWS, 128), F32))
+    for f in range(4):
+        units = place(flows[f, :, :128], flows[f, :, 128:COLS], units, f, REACH)
+    side_b[...], side_a[...] = ordered(*units, north_odd)
+
+
+def widen_kernel(sc, flows, side_a, side_b, out):
+    high, low = ordered(side_a[...], side_b[...], sc[2])
+    for f in range(4):
+        out[f, :, :COLS] = flows[f, :, :COLS]
+        out[f, :, COLS:] = unpack(high, low, f, REACH)
 
 
 def solve_kernel(sc, mine, pair, remote, remote_pair, far, u, v, s, east, north, salt, level, wide, out_u, out_v, sems):
@@ -415,13 +427,16 @@
     edgep_a = lax.ppermute(edge_a, "gx", on_chip)
     edgep_b = lax.ppermute(edge_b, "gx", on_chip)
 
-    flows, *state = call(
+    flows, side_a, side_b, *state = call(
         rk_kernel,
-        [(4, ROWS, WIDE)] + [(2, ROWS * LEV, 128)] * 3,
+        [(4, ROWS, WIDE)] + [(ROWS, 128)] * 2 + [(2, ROWS * LEV, 128)] * 3,
         [(3, 24, LEV, WIDE), (3, 16, LEV, WIDE), (3, 12, LEV, WIDE)]
         + [(24, 8, WIDE), (3, ROWS, WIDE), (2, ROWS, WIDE), (2, LEV, WIDE)],
         ins=9 + CHUNKS,
     )(scalars, st, stp, edge_a, edge_b, edgep_a, edgep_b, *main, corner_a, corner_b, plane)
+    side_a = lax.ppermute(side_a, "gy", even)
+    side_b = lax.ppermute(side_b, "gy", odd)
+    flows = call(widen_kernel, [(4, ROWS, WIDE)], ins=3)(scalars, flows, side_a, side_b)[0]
     far = lax.ppermute(flows, "gx", far_chip)
     pair = lax.ppermute(flows, "gx", on_chip)
     remote = lax.ppermute(jnp.stack([flows, pair]), "gx", next_chip)

time: 97 us -> 99.6 us (1.027)
  the two profiles are of different devices: /device:TPU:13 before, /device:TPU:31 now
where the time goes in v9:
time: 99.6 us; the launch traced here: 98.8 us
  waiting for transfers between devices  41.2 us (41%)
  starting transfers between devices  37.8 us (38%)
  Pallas kernels  18.9 us (19%)
    ppermute x1, waiting for transfers between devices, local(): edge_a = lax.ppermute(edge_a, 'gy', even)  29.8 us
    pallas_call x1, Pallas kernels, local(): call(rk_kernel, [(4, ROWS, WIDE)] + [(ROWS, 128)] * 2 + [(2, ROWS * LEV,...  10.9 us
    ppermute x1, starting transfers between devices, local(): main = [lax.ppermute(mains[0], 'gx', next_chip)]  8.72 us
    ppermute x1, starting transfers between devices, local(): remote = lax.ppermute(jnp.stack([flows, pair]), 'gx', next_chip)  5.38 us
    pallas_call x1, Pallas kernels, local(): call(solve_kernel, [(LEV, ROWS, COLS)] * 3 + [(ROWS, COLS)], [(4, 56, WID...  4.66 us
    ppermute x1, waiting for transfers between devices, local(): remote = lax.ppermute(jnp.stack([flows, pair]), 'gx', next_chip)  4.55 us
    ppermute x1, starting transfers between devices, local(): corner_b = lax.ppermute(corner_b, ('gx', 'gy'), both(next_chip, odd))  4.29 us
    ppermute x1, waiting for transfers between devices, local(): side_b = lax.ppermute(side_b, 'gy', odd)  3.89 us
  transfers between devices with their start and end apart: 14, of which 7 were waited for; matrix products, arithmetic and copies ran while one was open for 0% of the time, Pallas kernels for 0%

profile of v9, /device:TPU:31, one launch (start us, length us, event | category | flops | bytes accessed | tf_op | source)
XLA Modules:
  0.0 98.8 jit_solution(9383607337476643914)
XLA Ops:
  0.7 2.7 %shard_map.102 = (f32[104,128]{1,0:T(8,128)S(1)}, f32[104,128]{1,0:T(8,128)S(1)}, f32[56,128]{1,0:T(8,128)S(1)}, f32[56,128]{1,0:T(8,128)S(1)}, f32[1744,128]{1,...) custom-call(s32[3]{0:T(128)S(1)} %pad_add_fusion.sc, f32[48,8,256]{2,1,0:T(8,128)} %u.1, ...), custom_call_target="tpu_custom_call" | custom-call | tf_op jit(solution)/shard_map/pallas_call | solution.py:404
  3.4 0.8 collective-permute-start
  4.2 8.7 %collective-permute-start.7 = (f32[1744,128]{1,0:T(8,128)S(1)}, f32[1744,128]{1,0:T(8,128)S(1)}, u32[]{:S(2)}, u32[]{:S(2)}) collective-permute-start(f32[1744,128]{1,0:T(8,128)S(1)} %get-tuple-element.36), channel_id=1, source_target_pairs={{16,32},{32,16},{48,64},{64,48},{80,96},{96,80},{112,128},{128,112... | collective-permute-start | bytes 2678792 | tf_op jit(solution)/shard_map/ppermute | solution.py:420
  12.9 0.8 collective-permute-start.1
  13.7 3.7 %collective-permute-start.2 = (f32[104,128]{1,0:T(8,128)S(1)}, f32[104,128]{1,0:T(8,128)S(1)}, u32[]{:S(2)}, u32[]{:S(2)}) collective-permute-start(f32[104,128]{1,0:T(8,128)S(1)} %get-tuple-element.31), channel_id=1, source_target_pairs={{1,2},{2,1},{3,4},{4,3},{5,6},{6,5},{7,8},{8,7},{9,10},{10,9},{11,... | collective-permute-start | bytes 159752 | tf_op jit(solution)/shard_map/ppermute | solution.py:423
  17.5 2.5 %collective-permute-start.3 = (f32[56,128]{1,0:T(8,128)S(1)}, f32[56,128]{1,0:T(8,128)S(1)}, u32[]{:S(2)}, u32[]{:S(2)}) collective-permute-start(f32[56,128]{1,0:T(8,128)S(1)} %get-tuple-element.32), channel_id=1, source_target_pairs={{16,33},{17,32},{18,35},{19,34},{20,37},{21,36},{22,39},{23,38},{2... | collective-permute-start | bytes 86024 | tf_op jit(solution)/shard_map/ppermute | solution.py:424
  20.0 4.3 %collective-permute-start.4 = (f32[56,128]{1,0:T(8,128)S(1)}, f32[56,128]{1,0:T(8,128)S(1)}, u32[]{:S(2)}, u32[]{:S(2)}) collective-permute-start(f32[56,128]{1,0:T(8,128)S(1)} %get-tuple-element.33), channel_id=1, source_target_pairs={{17,34},{18,33},{19,36},{20,35},{21,38},{22,37},{23,40},{24,39},{2... | collective-permute-start | bytes 86024 | tf_op jit(solution)/shard_map/ppermute | solution.py:425
  24.3 29.8 %collective-permute-done.1.edge_a = f32[104,128]{1,0:T(8,128)S(1)} collective-permute-done((f32[104,128]{1,0:T(8,128)S(1)}, f32[104,128]{1,0:T(8,128)S(1)}, u32[]{:S(2)}, u32[]{:S(2)}) %collective-permute-start.1) | collective-permute-done | bytes 53280 | tf_op jit(solution)/shard_map/ppermute | solution.py:422
  54.1 1.7 %collective-permute-start.5 = (f32[104,128]{1,0:T(8,128)S(1)}, f32[104,128]{1,0:T(8,128)S(1)}, u32[]{:S(2)}, u32[]{:S(2)}) collective-permute-start(f32[104,128]{1,0:T(8,128)S(1)} %collective-permute-done.1.edge_a), channel_id=1, source_target_pairs={{0,16},{16,0},{32,48},{48,32},{64,80},{80,64},{96,112},{112,96},{1... | collective-permute-start | bytes 159752 | tf_op jit(solution)/shard_map/ppermute | solution.py:427
  55.9 0.8 collective-permute-done.5.edgep_a
  56.6 0.3 collective-permute-done.6.edgep_b
  57.0 10.9 %shard_map.103 = (f32[4,8,384]{2,1,0:T(8,128)S(1)}, f32[8,128]{1,0:T(8,128)S(1)}, f32[8,128]{1,0:T(8,128)S(1)}, f32[2,384,128]{2,1,0:T(8,128)S(1)}, f32[2,384,12...) custom-call(s32[3]{0:T(128)S(1)} %pad_add_fusion.sc, f32[2320,128]{1,0:T(8,128)S(1)} %get-tuple-element.26.st, ...), custom_call_target="tpu_custom_call" | custom-call | tf_op jit(solution)/shard_map/pallas_call | solution.py:430
  67.9 2.2 %collective-permute-start.8 = (f32[8,128]{1,0:T(8,128)S(1)}, f32[8,128]{1,0:T(8,128)S(1)}, u32[]{:S(2)}, u32[]{:S(2)}) collective-permute-start(f32[8,128]{1,0:T(8,128)S(1)} %get-tuple-element.41), channel_id=1, source_target_pairs={{0,1},{1,0},{2,3},{3,2},{4,5},{5,4},{6,7},{7,6},{8,9},{9,8},{10,11... | collective-permute-start | bytes 12296 | tf_op jit(solution)/shard_map/ppermute | solution.py:437
  70.1 3.1 %collective-permute-start.9 = (f32[8,128]{1,0:T(8,128)S(1)}, f32[8,128]{1,0:T(8,128)S(1)}, u32[]{:S(2)}, u32[]{:S(2)}) collective-permute-start(f32[8,128]{1,0:T(8,128)S(1)} %get-tuple-element.42), channel_id=1, source_target_pairs={{1,2},{2,1},{3,4},{4,3},{5,6},{6,5},{7,8},{8,7},{9,10},{10,9},{11,... | collective-permute-start | bytes 12296 | tf_op jit(solution)/shard_map/ppermute | solution.py:438
  73.3 3.9 %collective-permute-done.9.side_b = f32[8,128]{1,0:T(8,128)S(1)} collective-permute-done((f32[8,128]{1,0:T(8,128)S(1)}, f32[8,128]{1,0:T(8,128)S(1)}, u32[]{:S(2)}, u32[]{:S(2)}) %collective-permute-start.9) | collective-permute-done | bytes 4128 | tf_op jit(solution)/shard_map/ppermute | solution.py:438
  77.2 0.6 shard_map.104.mine
  77.8 1.6 %collective-permute-start.10 = (f32[4,8,384]{2,1,0:T(8,128)S(1)}, f32[4,8,384]{2,1,0:T(8,128)S(1)}, u32[]{:S(2)}, u32[]{:S(2)}) collective-permute-start(f32[4,8,384]{2,1,0:T(8,128)S(1)} %shard_map.104.mine), channel_id=1, source_target_pairs={{0,16},{16,0},{32,48},{48,32},{64,80},{80,64},{96,112},{112,96},{1... | collective-permute-start | bytes 147464 | tf_op jit(solution)/shard_map/ppermute | solution.py:441
  79.4 0.9 collective-permute-done.10.pair
  80.3 5.4 %collective-permute-start.11 = (f32[2,4,8,384]{3,2,1,0:T(8,128)S(1)}, f32[2,4,8,384]{3,2,1,0:T(8,128)S(1)}, u32[]{:S(2)}, u32[]{:S(2)}) collective-permute-start(f32[2,4,8,384]{3,2,1,0:T(8,128)S(1)} %pad_maximum_fusion), channel_id=1, source_target_pairs={{16,32},{32,16},{48,64},{64,48},{80,96},{96,80},{112,128},{128,112... | collective-permute-start | bytes 294920 | tf_op jit(solution)/shard_map/ppermute | solution.py:442
  85.7 0.7 collective-permute-start.12
  86.4 4.5 %collective-permute-done.11.remote = f32[2,4,8,384]{3,2,1,0:T(8,128)S(1)} collective-permute-done((f32[2,4,8,384]{3,2,1,0:T(8,128)S(1)}, f32[2,4,8,384]{3,2,1,0:T(8,128)S(1)}, u32[]{:S(2)}, u32[]{:S(2)}) %collective-permute-start.11) | collective-permute-done | bytes 98336 | tf_op jit(solution)/shard_map/ppermute | solution.py:442
  90.9 2.3 %collective-permute-start.13 = (f32[2,4,8,384]{3,2,1,0:T(8,128)S(1)}, f32[2,4,8,384]{3,2,1,0:T(8,128)S(1)}, u32[]{:S(2)}, u32[]{:S(2)}) collective-permute-start(f32[2,4,8,384]{3,2,1,0:T(8,128)S(1)} %collective-permute-done.11.remote), channel_id=1, source_target_pairs={{0,16},{16,0},{32,48},{48,32},{64,80},{80,64},{96,112},{112,96},{1... | collective-permute-start | bytes 294920 | tf_op jit(solution)/shard_map/ppermute | solution.py:444
  93.2 0.9 collective-permute-done.13.remote_pair
  94.1 4.7 %shard_map.105 = (f32[48,8,256]{2,1,0:T(8,128)}, f32[48,8,256]{2,1,0:T(8,128)}, f32[48,8,256]{2,1,0:T(8,128)}, f32[8,256]{1,0:T(8,128)}) custom-call(s32[3]{0:T(128)S(1)} %pad_add_fusion.sc, f32[4,8,384]{2,1,0:T(8,128)S(1)} %shard_map.104.mine, f32[4,8,384]{2,1,0:T(8,128)S(1)} %collective-permute-done.10.pair, ...), custom_call_target="tpu_custom_call" | custom-call | tf_op jit(solution)/shard_map/pallas_call | solution.py:446
  (10 shorter events, 0.2 us)
Async XLA Ops:
  3.4 14.0 %collective-permute-start = (f32[2320,128]{1,0:T(8,128)S(1)}, f32[2320,128]{1,0:T(8,128)S(1)}, u32[]{:S(2)}, u32[]{:S(2)}) collective-permute-start(f32[2320,128]{1,0:T(8,128)S(1)} %get-tuple-element.26.st), channel_id=1, source_target_pairs={{0,16},{16,0},{32,48},{48,32},{64,80},{80,64},{96,112},{112,96},{1... | collective-permute-start | bytes 3563528 | tf_op jit(solution)/shard_map/ppermute | solution.py:419
  4.2 51.7 %collective-permute-start.7 = (f32[1744,128]{1,0:T(8,128)S(1)}, f32[1744,128]{1,0:T(8,128)S(1)}, u32[]{:S(2)}, u32[]{:S(2)}) collective-permute-start(f32[1744,128]{1,0:T(8,128)S(1)} %get-tuple-element.36), channel_id=1, source_target_pairs={{16,32},{32,16},{48,64},{64,48},{80,96},{96,80},{112,128},{128,112... | collective-permute-start | bytes 2678792 | tf_op jit(solution)/shard_map/ppermute | solution.py:420
  12.9 41.1 %collective-permute-start.1 = (f32[104,128]{1,0:T(8,128)S(1)}, f32[104,128]{1,0:T(8,128)S(1)}, u32[]{:S(2)}, u32[]{:S(2)}) collective-permute-start(f32[104,128]{1,0:T(8,128)S(1)} %get-tuple-element.30), channel_id=1, source_target_pairs={{0,1},{1,0},{2,3},{3,2},{4,5},{5,4},{6,7},{7,6},{8,9},{9,8},{10,11... | collective-permute-start | bytes 159752 | tf_op jit(solution)/shard_map/ppermute | solution.py:422
  13.7 40.3 %collective-permute-start.2 = (f32[104,128]{1,0:T(8,128)S(1)}, f32[104,128]{1,0:T(8,128)S(1)}, u32[]{:S(2)}, u32[]{:S(2)}) collective-permute-start(f32[104,128]{1,0:T(8,128)S(1)} %get-tuple-element.31), channel_id=1, source_target_pairs={{1,2},{2,1},{3,4},{4,3},{5,6},{6,5},{7,8},{8,7},{9,10},{10,9},{11,... | collective-permute-start | bytes 159752 | tf_op jit(solution)/shard_map/ppermute | solution.py:423
  17.5 36.6 %collective-permute-start.3 = (f32[56,128]{1,0:T(8,128)S(1)}, f32[56,128]{1,0:T(8,128)S(1)}, u32[]{:S(2)}, u32[]{:S(2)}) collective-permute-start(f32[56,128]{1,0:T(8,128)S(1)} %get-tuple-element.32), channel_id=1, source_target_pairs={{16,33},{17,32},{18,35},{19,34},{20,37},{21,36},{22,39},{23,38},{2... | collective-permute-start | bytes 86024 | tf_op jit(solution)/shard_map/ppermute | solution.py:424
  20.0 34.1 %collective-permute-start.4 = (f32[56,128]{1,0:T(8,128)S(1)}, f32[56,128]{1,0:T(8,128)S(1)}, u32[]{:S(2)}, u32[]{:S(2)}) collective-permute-start(f32[56,128]{1,0:T(8,128)S(1)} %get-tuple-element.33), channel_id=1, source_target_pairs={{17,34},{18,33},{19,36},{20,35},{21,38},{22,37},{23,40},{24,39},{2... | collective-permute-start | bytes 86024 | tf_op jit(solution)/shard_map/ppermute | solution.py:425
  54.1 2.6 %collective-permute-start.5 = (f32[104,128]{1,0:T(8,128)S(1)}, f32[104,128]{1,0:T(8,128)S(1)}, u32[]{:S(2)}, u32[]{:S(2)}) collective-permute-start(f32[104,128]{1,0:T(8,128)S(1)} %collective-permute-done.1.edge_a), channel_id=1, source_target_pairs={{0,16},{16,0},{32,48},{48,32},{64,80},{80,64},{96,112},{112,96},{1... | collective-permute-start | bytes 159752 | tf_op jit(solution)/shard_map/ppermute | solution.py:427
  55.8 1.2 %collective-permute-start.6 = (f32[104,128]{1,0:T(8,128)S(1)}, f32[104,128]{1,0:T(8,128)S(1)}, u32[]{:S(2)}, u32[]{:S(2)}) collective-permute-start(f32[104,128]{1,0:T(8,128)S(1)} %collective-permute-done.2.edge_b), channel_id=1, source_target_pairs={{0,16},{16,0},{32,48},{48,32},{64,80},{80,64},{96,112},{112,96},{1... | collective-permute-start | bytes 159752 | tf_op jit(solution)/shard_map/ppermute | solution.py:428
  67.9 5.3 %collective-permute-start.8 = (f32[8,128]{1,0:T(8,128)S(1)}, f32[8,128]{1,0:T(8,128)S(1)}, u32[]{:S(2)}, u32[]{:S(2)}) collective-permute-start(f32[8,128]{1,0:T(8,128)S(1)} %get-tuple-element.41), channel_id=1, source_target_pairs={{0,1},{1,0},{2,3},{3,2},{4,5},{5,4},{6,7},{7,6},{8,9},{9,8},{10,11... | collective-permute-start | bytes 12296 | tf_op jit(solution)/shard_map/ppermute | solution.py:437
  70.1 7.0 %collective-permute-start.9 = (f32[8,128]{1,0:T(8,128)S(1)}, f32[8,128]{1,0:T(8,128)S(1)}, u32[]{:S(2)}, u32[]{:S(2)}) collective-permute-start(f32[8,128]{1,0:T(8,128)S(1)} %get-tuple-element.42), channel_id=1, source_target_pairs={{1,2},{2,1},{3,4},{4,3},{5,6},{6,5},{7,8},{8,7},{9,10},{10,9},{11,... | collective-permute-start | bytes 12296 | tf_op jit(solution)/shard_map/ppermute | solution.py:438
  77.8 2.5 %collective-permute-start.10 = (f32[4,8,384]{2,1,0:T(8,128)S(1)}, f32[4,8,384]{2,1,0:T(8,128)S(1)}, u32[]{:S(2)}, u32[]{:S(2)}) collective-permute-start(f32[4,8,384]{2,1,0:T(8,128)S(1)} %shard_map.104.mine), channel_id=1, source_target_pairs={{0,16},{16,0},{32,48},{48,32},{64,80},{80,64},{96,112},{112,96},{1... | collective-permute-start | bytes 147464 | tf_op jit(solution)/shard_map/ppermute | solution.py:441
  80.3 10.6 %collective-permute-start.11 = (f32[2,4,8,384]{3,2,1,0:T(8,128)S(1)}, f32[2,4,8,384]{3,2,1,0:T(8,128)S(1)}, u32[]{:S(2)}, u32[]{:S(2)}) collective-permute-start(f32[2,4,8,384]{3,2,1,0:T(8,128)S(1)} %pad_maximum_fusion), channel_id=1, source_target_pairs={{16,32},{32,16},{48,64},{64,48},{80,96},{96,80},{112,128},{128,112... | collective-permute-start | bytes 294920 | tf_op jit(solution)/shard_map/ppermute | solution.py:442
  85.7 0.7 collective-permute-start.12
  90.9 3.2 %collective-permute-start.13 = (f32[2,4,8,384]{3,2,1,0:T(8,128)S(1)}, f32[2,4,8,384]{3,2,1,0:T(8,128)S(1)}, u32[]{:S(2)}, u32[]{:S(2)}) collective-permute-start(f32[2,4,8,384]{3,2,1,0:T(8,128)S(1)} %collective-permute-done.11.remote), channel_id=1, source_target_pairs={{0,16},{16,0},{32,48},{48,32},{64,80},{80,64},{96,112},{112,96},{1... | collective-permute-start | bytes 294920 | tf_op jit(solution)/shard_map/ppermute | solution.py:444

commit v10 on v5

--- a/solution.py
+++ b/solution.py
@@ -71,12 +71,8 @@
     return jnp.where(odd, second, first), jnp.where(odd, first, second)
 
 
-def pack_kernel(sc, u, v, s, wet, act, surf, depth, edge_a, edge_b, corner_a, corner_b, *rest):
-    mains = rest[:CHUNKS]
-    st, plane = rest[CHUNKS : CHUNKS + 2]
-    buffers = rest[CHUNKS + 2 : CHUNKS + 9]
-    sems = rest[CHUNKS + 9]
-    core = sc[1]
+def pack_kernel(sc, u, v, s, wet, act, surf, depth, edge_a, edge_b, st, plane, *rest):
+    buffers, sems = rest[:-1], rest[-1]
     north_odd = sc[2]
     sources = (wet, act, surf, depth, u, v, s)
     copies = [pltpu.make_async_copy(a, b, sems.at[i]) for i, (a, b) in enumerate(zip(sources, buffers))]
@@ -96,40 +92,45 @@
             spot = 8 * (lev % TILES) + lev // TILES
             for h in range(2):
                 st[pl.ds((2 * f + h) * ROWS * LEV + spot, ROWS, stride=LEV), :] = tile[:, h * 128 : (h + 1) * 128]
-    base = 2 * core
-    for c in range(CHUNKS):
-        levels = SIZES[c]
-        for f in range(3):
-            for j in range(HALO):
-                for h in range(2):
-                    start = pl.multiple_of(((2 * f + h) * ROWS + base + j) * LEV + STARTS[c], 8)
-                    at = ((2 * f + h) * HALO + j) * levels
-                    mains[c][at : at + levels, :] = st[pl.ds(start, levels), :]
     for h in range(2):
-        at = 6 * HALO * SIZES[0] + 8 * h
-        mains[0][at : at + 8, :] = count[:, 128 * h : 128 * h + 128]
         at = 6 * ROWS * LEV + 8 * h
         st[at : at + 8, :] = count[:, 128 * h : 128 * h + 128]
+    pack_columns(st, EDGE_TILES, ROWS, 0, edge_a, edge_b, north_odd)
     blank = jnp.zeros((LEV, 128), F32)
-    for tiles, rows, first, a, b in (
-        (EDGE_TILES, ROWS, 0, edge_a, edge_b),
-        (CORNER_TILES, HALO, base, corner_a, corner_b),
-    ):
-        for g in range(tiles):
-            units = (blank, blank)
-            for slot in range(min(SLOTS, 3 * rows - SLOTS * g)):
-                f, r = divmod(SLOTS * g + slot, rows)
-                low = pl.multiple_of((2 * f * ROWS + first + r) * LEV, 8)
-                high = pl.multiple_of(((2 * f + 1) * ROWS + first + r) * LEV, 8)
-                units = place(st[pl.ds(low, LEV), :], st[pl.ds(high, LEV), :], units, slot)
-            b[g * LEV : g * LEV + LEV, :], a[g * LEV : g * LEV + LEV, :] = ordered(*units, north_odd)
     units = (blank[:ROWS], blank[:ROWS])
     for slot, field in enumerate((surf[...], count, depth[...])):
         units = place(field[:, :128], field[:, 128:], units, slot)
     left, right = ordered(*units, north_odd)
-    for tiles, a, b in ((EDGE_TILES, edge_a, edge_b), (CORNER_TILES, corner_a, corner_b)):
-        b[tiles * LEV :, :] = left
-        a[tiles * LEV :, :] = right
+    edge_b[EDGE_TILES * LEV :, :] = left
+    edge_a[EDGE_TILES * LEV :, :] = right
+
+
+def pack_columns(st, tiles, rows, first, a, b, north_odd):
+    blank = jnp.zeros((LEV, 128), F32)
+    for g in range(tiles):
+        units = (blank, blank)
+        for slot in range(min(SLOTS, 3 * rows - SLOTS * g)):
+            f, r = divmod(SLOTS * g + slot, rows)
+            low = pl.multiple_of((2 * f * ROWS + first + r) * LEV, 8)
+            high = pl.multiple_of(((2 * f + 1) * ROWS + first + r) * LEV, 8)
+            units = place(st[pl.ds(low, LEV), :], st[pl.ds(high, LEV), :], units, slot)
+        b[g * LEV : g * LEV + LEV, :], a[g * LEV : g * LEV + LEV, :] = ordered(*units, north_odd)
+
+
+def remote_kernel(sc, stp, main, corner_a, corner_b):
+    base = 2 * (1 - sc[1])
+    north_odd = sc[2]
+    for f in range(3):
+        for h in range(2):
+            start = pl.multiple_of(((2 * f + h) * ROWS + base) * LEV, 8)
+            at = (2 * f + h) * HALO * LEV
+            main[at : at + HALO * LEV, :] = stp[pl.ds(start, HALO * LEV), :]
+    main[6 * HALO * LEV :, :] = stp[6 * ROWS * LEV :, :]
+    pack_columns(stp, CORNER_TILES, HALO, base, corner_a, corner_b, north_odd)
+    blank = jnp.zeros((ROWS, 128), F32)
+    at = 6 * ROWS * LEV
+    units = place(stp[at : at + 8, :], stp[at + 8 : at + 16, :], (blank, blank), 1)
+    corner_b[CORNER_TILES * LEV :, :], corner_a[CORNER_TILES * LEV :, :] = ordered(*units, north_odd)
 
 
 def shifts(q):
@@ -292,10 +293,10 @@
     wide[:, 24:32, :] = mine[...]
     for slot, block in (
         (4 - 2 * core, pair[...]),
-        (2 + 2 * core, remote[0]),
-        (1 + 4 * core, remote[1]),
-        (5 - 4 * core, remote_pair[0]),
-        (6 - 6 * core, remote_pair[1]),
+        (2 + 2 * core, remote[1]),
+        (1 + 4 * core, remote[0]),
+        (5 - 4 * core, remote_pair[1]),
+        (6 - 6 * core, remote_pair[0]),
         (6 * core, far[...]),
     ):
         wide[:, pl.ds(pl.multiple_of(8 * slot, 8), 8), :] = block
@@ -381,7 +382,7 @@
     me = lax.axis_index("gx")
     scalars = jnp.stack([me, me % 2, lax.axis_index("gy") % 2]).astype(jnp.int32)
     on_chip = swap([(i, i + 1) for i in range(0, gx, 2)])
-    next_chip = swap([(i, i + 1) for i in range(1, gx - 1, 2)])
+    next_chip = [(i, i + 2) for i in range(0, gx - 2, 2)] + [(i, i - 2) for i in range(3, gx, 2)]
     far_chip = swap([(i, i + 3) for i in range(1, gx - 3, 2)])
     even = swap([(i, i + 1) for i in range(0, gy, 2)])
     odd = swap([(i, i + 1) for i in range(1, gy - 1, 2)])
@@ -389,12 +390,9 @@
     def both(first, second):
         return [(i * gy + j, k * gy + l) for i, k in first for j, l in second]
 
-    edge_a, edge_b, corner_a, corner_b, *packed = call(
+    edge_a, edge_b, st, plane = call(
         pack_kernel,
-        [(EDGE_TILES * LEV + 8, 128)] * 2
-        + [(CORNER_TILES * LEV + 8, 128)] * 2
-        + [(6 * HALO * levels + (0 if c else 16), 128) for c, levels in enumerate(SIZES)]
-        + [(6 * ROWS * LEV + 16, 128), (3, ROWS, COLS)],
+        [(EDGE_TILES * LEV + 8, 128)] * 2 + [(6 * ROWS * LEV + 16, 128), (3, ROWS, COLS)],
         [pltpu.VMEM((ROWS, COLS), jnp.int32)] * 2
         + [(ROWS, COLS)] * 2
         + [(LEV, ROWS, COLS)] * 3
@@ -402,11 +400,13 @@
         ins=7,
         space=pltpu.HBM,
     )(scalars, *(pltpu.with_memory_space_constraint(x, pltpu.HBM) for x in (u, v, s, wet, active, surface, depth)))
-    mains = packed[:CHUNKS]
-    st, plane = packed[CHUNKS:]
     stp = lax.ppermute(st, "gx", on_chip)
-    main = [lax.ppermute(mains[0], "gx", next_chip)]
-    stp, corner_a, corner_b = lax.optimization_barrier((stp, corner_a, corner_b))
+    main, corner_a, corner_b = call(
+        remote_kernel,
+        [(6 * HALO * LEV + 16, 128)] + [(CORNER_TILES * LEV + 8, 128)] * 2,
+        ins=1,
+    )(scalars, stp)
+    main = [lax.ppermute(main, "gx", next_chip)]
     edge_a = lax.ppermute(edge_a, "gy", even)
     edge_b = lax.ppermute(edge_b, "gy", odd)
     corner_a = lax.ppermute(corner_a, ("gx", "gy"), both(next_chip, even))

time: 97 us -> 99.1 us (1.022)
  the two profiles are of different devices: /device:TPU:13 before, /device:TPU:31 now
where the time goes in v10:
time: 99.1 us; the launch traced here: 98.7 us
  waiting for transfers between devices  44.5 us (45%)
  starting transfers between devices  34.7 us (35%)
  Pallas kernels  18.7 us (19%)
    ppermute x1, waiting for transfers between devices, local(): edge_a = lax.ppermute(edge_a, 'gy', even)  33.7 us
    pallas_call x1, Pallas kernels, local(): call(rk_kernel, [(4, ROWS, WIDE)] + [(2, ROWS * LEV, 128)] * 3, [(3, 24,...  10.8 us
    ppermute x1, starting transfers between devices, local(): main = [lax.ppermute(main, 'gx', next_chip)]  9.08 us
    ppermute x1, starting transfers between devices, local(): remote = lax.ppermute(jnp.stack([flows, pair]), 'gx', next_chip)  6.86 us
    ppermute x1, starting transfers between devices, local(): remote_pair = lax.ppermute(remote, 'gx', on_chip)  5.1 us
    pallas_call x1, Pallas kernels, local(): call(solve_kernel, [(LEV, ROWS, COLS)] * 3 + [(ROWS, COLS)], [(4, 56, WID...  4.66 us
    ppermute x1, starting transfers between devices, local(): corner_b = lax.ppermute(corner_b, ('gx', 'gy'), both(next_chip, odd))  4.53 us
    ppermute x1, starting transfers between devices, local(): edge_b = lax.ppermute(edge_b, 'gy', odd)  3.71 us
  transfers between devices with their start and end apart: 12, of which 8 were waited for; matrix products, arithmetic and copies ran while one was open for 0% of the time, Pallas kernels for 0%

profile of v10, /device:TPU:31, one launch (start us, length us, event | category | flops | bytes accessed | tf_op | source)
XLA Modules:
  0.0 98.7 jit_solution(17997352220427206232)
XLA Ops:
  0.6 0.1 pad_add_fusion.sc
  0.7 2.4 %shard_map.102 = (f32[248,128]{1,0:T(8,128)S(1)}, f32[248,128]{1,0:T(8,128)S(1)}, f32[2320,128]{1,0:T(8,128)S(1)}, f32[3,8,256]{2,1,0:T(8,128)S(1)}) custom-call(s32[3]{0:T(128)S(1)} %pad_add_fusion.sc, f32[48,8,256]{2,1,0:T(8,128)} %u.1, f32[48,8,256]{2,1,0:T(8,128)} %v.1, f32[48,8,256]{2,1,0:T(8,128)} %s.1, s32[8,256]{1,0:T(8,128)} %wet.1, s32[8,256]{1,0:T(8,128)} %act.1, ...), custom_call_target="tpu_custom_call" | custom-call | tf_op jit(solution)/shard_map/pallas_call | solution.py:393
  3.2 0.8 collective-permute-start
  3.9 2.5 %collective-permute-done.stp = f32[2320,128]{1,0:T(8,128)S(1)} collective-permute-done((f32[2320,128]{1,0:T(8,128)S(1)}, f32[2320,128]{1,0:T(8,128)S(1)}, u32[]{:S(2)}, u32[]{:S(2)}) %collective-permute-start) | collective-permute-done | bytes 1187872 | tf_op jit(solution)/shard_map/ppermute | solution.py:403
  6.4 0.8 shard_map.103
  7.2 9.1 %collective-permute-start.7 = (f32[1744,128]{1,0:T(8,128)S(1)}, f32[1744,128]{1,0:T(8,128)S(1)}, u32[]{:S(2)}, u32[]{:S(2)}) collective-permute-start(f32[1744,128]{1,0:T(8,128)S(1)} %get-tuple-element.28), channel_id=1, source_target_pairs={{0,32},{32,64},{64,96},{96,128},{128,160},{160,192},{192,224},{48,... | collective-permute-start | bytes 2678792 | tf_op jit(solution)/shard_map/ppermute | solution.py:409
  16.3 0.8 collective-permute-start.1
  17.1 3.7 %collective-permute-start.2 = (f32[248,128]{1,0:T(8,128)S(1)}, f32[248,128]{1,0:T(8,128)S(1)}, u32[]{:S(2)}, u32[]{:S(2)}) collective-permute-start(f32[248,128]{1,0:T(8,128)S(1)} %get-tuple-element.23), channel_id=1, source_target_pairs={{1,2},{2,1},{3,4},{4,3},{5,6},{6,5},{7,8},{8,7},{9,10},{10,9},{11,... | collective-permute-start | bytes 380936 | tf_op jit(solution)/shard_map/ppermute | solution.py:411
  20.9 1.9 %collective-permute-start.3 = (f32[200,128]{1,0:T(8,128)S(1)}, f32[200,128]{1,0:T(8,128)S(1)}, u32[]{:S(2)}, u32[]{:S(2)}) collective-permute-start(f32[200,128]{1,0:T(8,128)S(1)} %get-tuple-element.24), channel_id=1, source_target_pairs={{0,33},{1,32},{2,35},{3,34},{4,37},{5,36},{6,39},{7,38},{8,41},{9,... | collective-permute-start | bytes 307208 | tf_op jit(solution)/shard_map/ppermute | solution.py:412
  22.8 4.5 %collective-permute-start.4 = (f32[200,128]{1,0:T(8,128)S(1)}, f32[200,128]{1,0:T(8,128)S(1)}, u32[]{:S(2)}, u32[]{:S(2)}) collective-permute-start(f32[200,128]{1,0:T(8,128)S(1)} %get-tuple-element.25), channel_id=1, source_target_pairs={{1,34},{2,33},{3,36},{4,35},{5,38},{6,37},{7,40},{8,39},{9,42},{10... | collective-permute-start | bytes 307208 | tf_op jit(solution)/shard_map/ppermute | solution.py:413
  27.3 33.7 %collective-permute-done.1.edge_a = f32[248,128]{1,0:T(8,128)S(1)} collective-permute-done((f32[248,128]{1,0:T(8,128)S(1)}, f32[248,128]{1,0:T(8,128)S(1)}, u32[]{:S(2)}, u32[]{:S(2)}) %collective-permute-start.1) | collective-permute-done | bytes 127008 | tf_op jit(solution)/shard_map/ppermute | solution.py:410
  61.0 3.2 %collective-permute-done.4.rest_2_ = f32[200,128]{1,0:T(8,128)S(1)} collective-permute-done((f32[200,128]{1,0:T(8,128)S(1)}, f32[200,128]{1,0:T(8,128)S(1)}, u32[]{:S(2)}, u32[]{:S(2)}) %collective-permute-start.4) | collective-permute-done | bytes 102432 | tf_op jit(solution)/shard_map/ppermute | solution.py:413
  64.2 1.0 collective-permute-start.5
  65.2 1.0 collective-permute-done.5.edgep_a
  66.1 0.4 collective-permute-done.6.edgep_b
  66.5 10.8 %shard_map.104 = (f32[4,8,384]{2,1,0:T(8,128)S(1)}, f32[2,384,128]{2,1,0:T(8,128)S(1)}, f32[2,384,128]{2,1,0:T(8,128)S(1)}, f32[2,384,128]{2,1,0:T(8,128)S(1)}) custom-call(s32[3]{0:T(128)S(1)} %pad_add_fusion.sc, f32[2320,128]{1,0:T(8,128)S(1)} %get-tuple-element.21.st, f32[2320,128]{1,0:T(8,128)S(1)} %collective-permute-done.stp, ...), custom_call_target="tpu_custom_call" | custom-call | tf_op jit(solution)/shard_map/pallas_call | solution.py:418
  77.3 0.3 collective-permute-start.8
  77.6 1.0 %collective-permute-done.8.pair = f32[4,8,384]{2,1,0:T(8,128)S(1)} collective-permute-done((f32[4,8,384]{2,1,0:T(8,128)S(1)}, f32[4,8,384]{2,1,0:T(8,128)S(1)}, u32[]{:S(2)}, u32[]{:S(2)}) %collective-permute-start.8) | collective-permute-done | bytes 49184 | tf_op jit(solution)/shard_map/ppermute | solution.py:426
  78.7 6.9 %collective-permute-start.9 = (f32[2,4,8,384]{3,2,1,0:T(8,128)S(1)}, f32[2,4,8,384]{3,2,1,0:T(8,128)S(1)}, u32[]{:S(2)}, u32[]{:S(2)}) collective-permute-start(f32[2,4,8,384]{3,2,1,0:T(8,128)S(1)} %pad_maximum_fusion), channel_id=1, source_target_pairs={{0,32},{32,64},{64,96},{96,128},{128,160},{160,192},{192,224},{48,... | collective-permute-start | bytes 294920 | tf_op jit(solution)/shard_map/ppermute | solution.py:427
  85.5 0.7 collective-permute-start.10
  86.2 1.8 %collective-permute-done.9.remote = f32[2,4,8,384]{3,2,1,0:T(8,128)S(1)} collective-permute-done((f32[2,4,8,384]{3,2,1,0:T(8,128)S(1)}, f32[2,4,8,384]{3,2,1,0:T(8,128)S(1)}, u32[]{:S(2)}, u32[]{:S(2)}) %collective-permute-start.9) | collective-permute-done | bytes 98336 | tf_op jit(solution)/shard_map/ppermute | solution.py:427
  88.0 5.1 %collective-permute-start.11 = (f32[2,4,8,384]{3,2,1,0:T(8,128)S(1)}, f32[2,4,8,384]{3,2,1,0:T(8,128)S(1)}, u32[]{:S(2)}, u32[]{:S(2)}) collective-permute-start(f32[2,4,8,384]{3,2,1,0:T(8,128)S(1)} %collective-permute-done.9.remote), channel_id=1, source_target_pairs={{0,16},{16,0},{32,48},{48,32},{64,80},{80,64},{96,112},{112,96},{1... | collective-permute-start | bytes 294920 | tf_op jit(solution)/shard_map/ppermute | solution.py:429
  93.1 0.9 collective-permute-done.11.remote_pair
  94.1 4.7 %shard_map.105 = (f32[48,8,256]{2,1,0:T(8,128)}, f32[48,8,256]{2,1,0:T(8,128)}, f32[48,8,256]{2,1,0:T(8,128)}, f32[8,256]{1,0:T(8,128)}) custom-call(s32[3]{0:T(128)S(1)} %pad_add_fusion.sc, f32[4,8,384]{2,1,0:T(8,128)S(1)} %get-tuple-element.32.mine, f32[4,8,384]{2,1,0:T(8,128)S(1)} %collective-permute-done.8.pair, ...), custom_call_target="tpu_custom_call" | custom-call | tf_op jit(solution)/shard_map/pallas_call | solution.py:431
  (6 shorter events, 0.0 us)
Async XLA Ops:
  3.2 3.2 %collective-permute-start = (f32[2320,128]{1,0:T(8,128)S(1)}, f32[2320,128]{1,0:T(8,128)S(1)}, u32[]{:S(2)}, u32[]{:S(2)}) collective-permute-start(f32[2320,128]{1,0:T(8,128)S(1)} %get-tuple-element.21.st), channel_id=1, source_target_pairs={{0,16},{16,0},{32,48},{48,32},{64,80},{80,64},{96,112},{112,96},{1... | collective-permute-start | bytes 3563528 | tf_op jit(solution)/shard_map/ppermute | solution.py:403
  7.2 59.3 %collective-permute-start.7 = (f32[1744,128]{1,0:T(8,128)S(1)}, f32[1744,128]{1,0:T(8,128)S(1)}, u32[]{:S(2)}, u32[]{:S(2)}) collective-permute-start(f32[1744,128]{1,0:T(8,128)S(1)} %get-tuple-element.28), channel_id=1, source_target_pairs={{0,32},{32,64},{64,96},{96,128},{128,160},{160,192},{192,224},{48,... | collective-permute-start | bytes 2678792 | tf_op jit(solution)/shard_map/ppermute | solution.py:409
  16.3 44.7 %collective-permute-start.1 = (f32[248,128]{1,0:T(8,128)S(1)}, f32[248,128]{1,0:T(8,128)S(1)}, u32[]{:S(2)}, u32[]{:S(2)}) collective-permute-start(f32[248,128]{1,0:T(8,128)S(1)} %get-tuple-element.22), channel_id=1, source_target_pairs={{0,1},{1,0},{2,3},{3,2},{4,5},{5,4},{6,7},{7,6},{8,9},{9,8},{10,11... | collective-permute-start | bytes 380936 | tf_op jit(solution)/shard_map/ppermute | solution.py:410
  17.1 43.9 %collective-permute-start.2 = (f32[248,128]{1,0:T(8,128)S(1)}, f32[248,128]{1,0:T(8,128)S(1)}, u32[]{:S(2)}, u32[]{:S(2)}) collective-permute-start(f32[248,128]{1,0:T(8,128)S(1)} %get-tuple-element.23), channel_id=1, source_target_pairs={{1,2},{2,1},{3,4},{4,3},{5,6},{6,5},{7,8},{8,7},{9,10},{10,9},{11,... | collective-permute-start | bytes 380936 | tf_op jit(solution)/shard_map/ppermute | solution.py:411
  20.9 40.1 %collective-permute-start.3 = (f32[200,128]{1,0:T(8,128)S(1)}, f32[200,128]{1,0:T(8,128)S(1)}, u32[]{:S(2)}, u32[]{:S(2)}) collective-permute-start(f32[200,128]{1,0:T(8,128)S(1)} %get-tuple-element.24), channel_id=1, source_target_pairs={{0,33},{1,32},{2,35},{3,34},{4,37},{5,36},{6,39},{7,38},{8,41},{9,... | collective-permute-start | bytes 307208 | tf_op jit(solution)/shard_map/ppermute | solution.py:412
  22.8 41.4 %collective-permute-start.4 = (f32[200,128]{1,0:T(8,128)S(1)}, f32[200,128]{1,0:T(8,128)S(1)}, u32[]{:S(2)}, u32[]{:S(2)}) collective-permute-start(f32[200,128]{1,0:T(8,128)S(1)} %get-tuple-element.25), channel_id=1, source_target_pairs={{1,34},{2,33},{3,36},{4,35},{5,38},{6,37},{7,40},{8,39},{9,42},{10... | collective-permute-start | bytes 307208 | tf_op jit(solution)/shard_map/ppermute | solution.py:413
  64.2 1.9 %collective-permute-start.5 = (f32[248,128]{1,0:T(8,128)S(1)}, f32[248,128]{1,0:T(8,128)S(1)}, u32[]{:S(2)}, u32[]{:S(2)}) collective-permute-start(f32[248,128]{1,0:T(8,128)S(1)} %collective-permute-done.1.edge_a), channel_id=1, source_target_pairs={{0,16},{16,0},{32,48},{48,32},{64,80},{80,64},{96,112},{112,96},{1... | collective-permute-start | bytes 380936 | tf_op jit(solution)/shard_map/ppermute | solution.py:415
  65.2 1.3 %collective-permute-start.6 = (f32[248,128]{1,0:T(8,128)S(1)}, f32[248,128]{1,0:T(8,128)S(1)}, u32[]{:S(2)}, u32[]{:S(2)}) collective-permute-start(f32[248,128]{1,0:T(8,128)S(1)} %collective-permute-done.2.edge_b), channel_id=1, source_target_pairs={{0,16},{16,0},{32,48},{48,32},{64,80},{80,64},{96,112},{112,96},{1... | collective-permute-start | bytes 380936 | tf_op jit(solution)/shard_map/ppermute | solution.py:416
  77.3 1.3 %collective-permute-start.8 = (f32[4,8,384]{2,1,0:T(8,128)S(1)}, f32[4,8,384]{2,1,0:T(8,128)S(1)}, u32[]{:S(2)}, u32[]{:S(2)}) collective-permute-start(f32[4,8,384]{2,1,0:T(8,128)S(1)} %get-tuple-element.32.mine), channel_id=1, source_target_pairs={{0,16},{16,0},{32,48},{48,32},{64,80},{80,64},{96,112},{112,96},{1... | collective-permute-start | bytes 147464 | tf_op jit(solution)/shard_map/ppermute | solution.py:426
  78.7 9.4 %collective-permute-start.9 = (f32[2,4,8,384]{3,2,1,0:T(8,128)S(1)}, f32[2,4,8,384]{3,2,1,0:T(8,128)S(1)}, u32[]{:S(2)}, u32[]{:S(2)}) collective-permute-start(f32[2,4,8,384]{3,2,1,0:T(8,128)S(1)} %pad_maximum_fusion), channel_id=1, source_target_pairs={{0,32},{32,64},{64,96},{96,128},{128,160},{160,192},{192,224},{48,... | collective-permute-start | bytes 294920 | tf_op jit(solution)/shard_map/ppermute | solution.py:427
  85.5 0.7 collective-permute-start.10
  88.0 6.0 %collective-permute-start.11 = (f32[2,4,8,384]{3,2,1,0:T(8,128)S(1)}, f32[2,4,8,384]{3,2,1,0:T(8,128)S(1)}, u32[]{:S(2)}, u32[]{:S(2)}) collective-permute-start(f32[2,4,8,384]{3,2,1,0:T(8,128)S(1)} %collective-permute-done.9.remote), channel_id=1, source_target_pairs={{0,16},{16,0},{32,48},{48,32},{64,80},{80,64},{96,112},{112,96},{1... | collective-permute-start | bytes 294920 | tf_op jit(solution)/shard_map/ppermute | solution.py:429

commit v11 on v3

--- a/solution.py
+++ b/solution.py
@@ -247,7 +247,7 @@
             carry[pl.ds(slot + 2 * o + 1, 1), :] = sum_y[:1, :]
             return 0
 
-        lax.fori_loop(0, rows, row, 0, unroll=max(1, min(4, 32 // levels)))
+        lax.fori_loop(0, rows, row, 0, unroll=max(1, min(4, 64 // levels)))
 
     def write1(o, here, t, mid, rates):
         for f in range(3):

time: 95.3 us -> 94.8 us (level)
  Pallas kernels: 22.8 us -> 21.2 us
  starting transfers between devices: 35.4 us -> 36.5 us
    pallas_call x2, Pallas kernels: 16 us -> 14.4 us  [local(): call(functools.partial(rk_kernel, c), [(4, ROWS, WIDE)] * (c == CHUNKS -...]
    ppermute x1, starting transfers between devices: 2.24 us -> 3.31 us  [local(): pair = lax.ppermute(flows, 'gx', on_chip)]
  transfers between devices with their start and end apart: 13 -> 13, of which waited for: 7 -> 7; matrix products, arithmetic and copies ran while one was open for 0% -> 0% of each run, Pallas kernels for 11% -> 9%
where the time goes in v11:
time: 94.8 us; the launch traced here: 94.1 us
  starting transfers between devices  36.5 us (39%)
  waiting for transfers between devices  35.6 us (38%)
  Pallas kernels  21.2 us (22%)
    ppermute x1, waiting for transfers between devices, local(): edge_a = lax.ppermute(edge_a, 'gy', even)  20.3 us
    pallas_call x2, Pallas kernels, local(): call(functools.partial(rk_kernel, c), [(4, ROWS, WIDE)] * (c == CHUNKS -...  14.4 us
    ppermute x1, starting transfers between devices, local(): main = [lax.ppermute(mains[0], 'gx', next_chip)]  8.72 us
    ppermute x1, waiting for transfers between devices, local(): remote = lax.ppermute(jnp.stack([flows, pair]), 'gx', next_chip)  8.59 us
    ppermute x1, starting transfers between devices, local(): main += [lax.ppermute(m, 'gx', next_chip) for m in later]  4.92 us
    ppermute x1, starting transfers between devices, local(): corner_b = lax.ppermute(corner_b, ('gx', 'gy'), both(next_chip, odd))  4.29 us
    pallas_call x1, Pallas kernels, local(): call(solve_kernel, [(LEV, ROWS, COLS)] * 3 + [(ROWS, COLS)], [(4, 56, WID...  4.14 us
    ppermute x1, starting transfers between devices, local(): edge_b = lax.ppermute(edge_b, 'gy', odd)  3.71 us
  transfers between devices with their start and end apart: 13, of which 7 were waited for; matrix products, arithmetic and copies ran while one was open for 0% of the time, Pallas kernels for 9%

profile of v11, /device:TPU:31, one launch (start us, length us, event | category | flops | bytes accessed | tf_op | source)
XLA Modules:
  0.0 94.1 jit_solution(6769849358406870865)
XLA Ops:
  0.7 2.6 %shard_map.102 = (f32[248,128]{1,0:T(8,128)S(1)}, f32[248,128]{1,0:T(8,128)S(1)}, f32[200,128]{1,0:T(8,128)S(1)}, f32[200,128]{1,0:T(8,128)S(1)}, f32[1168,128]{...) custom-call(s32[3]{0:T(128)S(1)} %pad_add_fusion.sc, ...), custom_call_target="tpu_custom_call" | custom-call | tf_op jit(solution)/shard_map/pallas_call | solution.py:386
  3.4 0.8 collective-permute-start
  4.1 8.7 %collective-permute-start.8 = (f32[1168,128]{1,0:T(8,128)S(1)}, f32[1168,128]{1,0:T(8,128)S(1)}, u32[]{:S(2)}, u32[]{:S(2)}) collective-permute-start(f32[1168,128]{1,0:T(8,128)S(1)} %get-tuple-element.39), channel_id=1, source_target_pairs={{16,32},{32,16},{48,64},{64,48},{80,96},{96,80},{112,128},{128,112... | collective-permute-start | bytes 1794056 | tf_op jit(solution)/shard_map/ppermute | solution.py:402
  12.8 0.8 collective-permute-start.3
  13.7 3.7 %collective-permute-start.4 = (f32[248,128]{1,0:T(8,128)S(1)}, f32[248,128]{1,0:T(8,128)S(1)}, u32[]{:S(2)}, u32[]{:S(2)}) collective-permute-start(f32[248,128]{1,0:T(8,128)S(1)} %get-tuple-element.34), channel_id=1, source_target_pairs={{1,2},{2,1},{3,4},{4,3},{5,6},{6,5},{7,8},{8,7},{9,10},{10,9},{11,... | collective-permute-start | bytes 380936 | tf_op jit(solution)/shard_map/ppermute | solution.py:405
  17.4 2.5 %collective-permute-start.1 = (f32[200,128]{1,0:T(8,128)S(1)}, f32[200,128]{1,0:T(8,128)S(1)}, u32[]{:S(2)}, u32[]{:S(2)}) collective-permute-start(f32[200,128]{1,0:T(8,128)S(1)} %get-tuple-element.31), channel_id=1, source_target_pairs={{16,33},{17,32},{18,35},{19,34},{20,37},{21,36},{22,39},{23,38},{2... | collective-permute-start | bytes 307208 | tf_op jit(solution)/shard_map/ppermute | solution.py:406
  19.9 4.3 %collective-permute-start.2 = (f32[200,128]{1,0:T(8,128)S(1)}, f32[200,128]{1,0:T(8,128)S(1)}, u32[]{:S(2)}, u32[]{:S(2)}) collective-permute-start(f32[200,128]{1,0:T(8,128)S(1)} %get-tuple-element.32), channel_id=1, source_target_pairs={{17,34},{18,33},{19,36},{20,35},{21,38},{22,37},{23,40},{24,39},{2... | collective-permute-start | bytes 307208 | tf_op jit(solution)/shard_map/ppermute | solution.py:407
  24.2 20.3 %collective-permute-done.3.edge_a = f32[248,128]{1,0:T(8,128)S(1)} collective-permute-done((f32[248,128]{1,0:T(8,128)S(1)}, f32[248,128]{1,0:T(8,128)S(1)}, u32[]{:S(2)}, u32[]{:S(2)}) %collective-permute-start.3) | collective-permute-done | bytes 127008 | tf_op jit(solution)/shard_map/ppermute | solution.py:404
  44.5 3.6 %collective-permute-done.2.corner_b = f32[200,128]{1,0:T(8,128)S(1)} collective-permute-done((f32[200,128]{1,0:T(8,128)S(1)}, f32[200,128]{1,0:T(8,128)S(1)}, u32[]{:S(2)}, u32[]{:S(2)}) %collective-permute-start.2) | collective-permute-done | bytes 102432 | tf_op jit(solution)/shard_map/ppermute | solution.py:407
  48.1 4.9 %collective-permute-start.7 = (f32[576,128]{1,0:T(8,128)S(1)}, f32[576,128]{1,0:T(8,128)S(1)}, u32[]{:S(2)}, u32[]{:S(2)}) collective-permute-start(f32[576,128]{1,0:T(8,128)S(1)} %get-tuple-element.38), channel_id=1, source_target_pairs={{16,32},{32,16},{48,64},{64,48},{80,96},{96,80},{112,128},{128,112... | collective-permute-start | bytes 884744 | tf_op jit(solution)/shard_map/ppermute | solution.py:409
  53.0 3.4 %collective-permute-start.5 = (f32[248,128]{1,0:T(8,128)S(1)}, f32[248,128]{1,0:T(8,128)S(1)}, u32[]{:S(2)}, u32[]{:S(2)}) collective-permute-start(f32[248,128]{1,0:T(8,128)S(1)} %collective-permute-done.3.edge_a), channel_id=1, source_target_pairs={{0,16},{16,0},{32,48},{48,32},{64,80},{80,64},{96,112},{112,96},{1... | collective-permute-start | bytes 380936 | tf_op jit(solution)/shard_map/ppermute | solution.py:410
  56.4 0.1 collective-permute-start.6
  56.5 0.9 collective-permute-done.5.edgep_a
  57.4 0.4 collective-permute-done.6.edgep_b
  57.8 8.9 %shard_map.103 = (f32[3,2,256,128]{3,2,1,0:T(8,128)S(1)}, f32[72,384]{1,0:T(8,128)S(1)}, f32[2,8,8,384]{3,2,1,0:T(8,128)S(1)}) custom-call(s32[3]{0:T(128)S(1)} %pad_add_fusion.sc, f32[2320,128]{1,0:T(8,128)S(1)} %get-tuple-element.27.st, f32[2320,128]{1,0:T(8,128)S(1)} %collective-permute-done.stp, f32[248,128]{1,0:T(8,128)S(1)} %collective-permute-done.3.edge_a, ...), custom_call_target="tpu_custom_call" | custom-call | tf_op jit(solution)/shard_map/pallas_call | solution.py:416
  66.7 5.5 %shard_map.104 = (f32[4,8,384]{2,1,0:T(8,128)S(1)}, f32[3,2,128,128]{3,2,1,0:T(8,128)S(1)}, f32[72,384]{1,0:T(8,128)}, f32[2,8,8,384]{3,2,1,0:T(8,128)}) custom-call(s32[3]{0:T(128)S(1)} %pad_add_fusion.sc, f32[2320,128]{1,0:T(8,128)S(1)} %get-tuple-element.27.st, f32[2320,128]{1,0:T(8,128)S(1)} %collective-permute-done.stp, ...), custom_call_target="tpu_custom_call" | custom-call | tf_op jit(solution)/shard_map/pallas_call | solution.py:416
  72.2 3.3 %collective-permute-start.9 = (f32[4,8,384]{2,1,0:T(8,128)S(1)}, f32[4,8,384]{2,1,0:T(8,128)S(1)}, u32[]{:S(2)}, u32[]{:S(2)}) collective-permute-start(f32[4,8,384]{2,1,0:T(8,128)S(1)} %get-tuple-element.45.mine), channel_id=1, source_target_pairs={{0,16},{16,0},{32,48},{48,32},{64,80},{80,64},{96,112},{112,96},{1... | collective-permute-start | bytes 147464 | tf_op jit(solution)/shard_map/ppermute | solution.py:428
  75.5 0.9 collective-permute-done.9.pair
  76.4 1.9 %collective-permute-start.10 = (f32[2,4,8,384]{3,2,1,0:T(8,128)S(1)}, f32[2,4,8,384]{3,2,1,0:T(8,128)S(1)}, u32[]{:S(2)}, u32[]{:S(2)}) collective-permute-start(f32[2,4,8,384]{3,2,1,0:T(8,128)S(1)} %pad_maximum_fusion), channel_id=1, source_target_pairs={{16,32},{32,16},{48,64},{64,48},{80,96},{96,80},{112,128},{128,112... | collective-permute-start | bytes 294920 | tf_op jit(solution)/shard_map/ppermute | solution.py:429
  78.3 0.7 collective-permute-start.11
  79.0 8.6 %collective-permute-done.10.remote = f32[2,4,8,384]{3,2,1,0:T(8,128)S(1)} collective-permute-done((f32[2,4,8,384]{3,2,1,0:T(8,128)S(1)}, f32[2,4,8,384]{3,2,1,0:T(8,128)S(1)}, u32[]{:S(2)}, u32[]{:S(2)}) %collective-permute-start.10) | collective-permute-done | bytes 98336 | tf_op jit(solution)/shard_map/ppermute | solution.py:429
  87.6 1.4 %collective-permute-start.12 = (f32[2,4,8,384]{3,2,1,0:T(8,128)S(1)}, f32[2,4,8,384]{3,2,1,0:T(8,128)S(1)}, u32[]{:S(2)}, u32[]{:S(2)}) collective-permute-start(f32[2,4,8,384]{3,2,1,0:T(8,128)S(1)} %collective-permute-done.10.remote), channel_id=1, source_target_pairs={{0,16},{16,0},{32,48},{48,32},{64,80},{80,64},{96,112},{112,96},{1... | collective-permute-start | bytes 294920 | tf_op jit(solution)/shard_map/ppermute | solution.py:431
  89.0 0.9 %collective-permute-done.12.remote_pair = f32[2,4,8,384]{3,2,1,0:T(8,128)S(1)} collective-permute-done((f32[2,4,8,384]{3,2,1,0:T(8,128)S(1)}, f32[2,4,8,384]{3,2,1,0:T(8,128)S(1)}, u32[]{:S(2)}, u32[]{:S(2)}) %collective-permute-start.12) | collective-permute-done | bytes 98336 | tf_op jit(solution)/shard_map/ppermute | solution.py:431
  89.9 4.1 %shard_map.105 = (f32[48,8,256]{2,1,0:T(8,128)}, f32[48,8,256]{2,1,0:T(8,128)}, f32[48,8,256]{2,1,0:T(8,128)}, f32[8,256]{1,0:T(8,128)}) custom-call(s32[3]{0:T(128)S(1)} %pad_add_fusion.sc, f32[4,8,384]{2,1,0:T(8,128)S(1)} %get-tuple-element.45.mine, f32[4,8,384]{2,1,0:T(8,128)S(1)} %collective-permute-done.9.pair, ...), custom_call_target="tpu_custom_call" | custom-call | tf_op jit(solution)/shard_map/pallas_call | solution.py:432
  (8 shorter events, 0.1 us)
Async XLA Ops:
  3.4 14.0 %collective-permute-start = (f32[2320,128]{1,0:T(8,128)S(1)}, f32[2320,128]{1,0:T(8,128)S(1)}, u32[]{:S(2)}, u32[]{:S(2)}) collective-permute-start(f32[2320,128]{1,0:T(8,128)S(1)} %get-tuple-element.27.st), channel_id=1, source_target_pairs={{0,16},{16,0},{32,48},{48,32},{64,80},{80,64},{96,112},{112,96},{1... | collective-permute-start | bytes 3563528 | tf_op jit(solution)/shard_map/ppermute | solution.py:401
  4.1 52.4 %collective-permute-start.8 = (f32[1168,128]{1,0:T(8,128)S(1)}, f32[1168,128]{1,0:T(8,128)S(1)}, u32[]{:S(2)}, u32[]{:S(2)}) collective-permute-start(f32[1168,128]{1,0:T(8,128)S(1)} %get-tuple-element.39), channel_id=1, source_target_pairs={{16,32},{32,16},{48,64},{64,48},{80,96},{96,80},{112,128},{128,112... | collective-permute-start | bytes 1794056 | tf_op jit(solution)/shard_map/ppermute | solution.py:402
  12.8 31.6 %collective-permute-start.3 = (f32[248,128]{1,0:T(8,128)S(1)}, f32[248,128]{1,0:T(8,128)S(1)}, u32[]{:S(2)}, u32[]{:S(2)}) collective-permute-start(f32[248,128]{1,0:T(8,128)S(1)} %get-tuple-element.33), channel_id=1, source_target_pairs={{0,1},{1,0},{2,3},{3,2},{4,5},{5,4},{6,7},{7,6},{8,9},{9,8},{10,11... | collective-permute-start | bytes 380936 | tf_op jit(solution)/shard_map/ppermute | solution.py:404
  13.7 30.8 %collective-permute-start.4 = (f32[248,128]{1,0:T(8,128)S(1)}, f32[248,128]{1,0:T(8,128)S(1)}, u32[]{:S(2)}, u32[]{:S(2)}) collective-permute-start(f32[248,128]{1,0:T(8,128)S(1)} %get-tuple-element.34), channel_id=1, source_target_pairs={{1,2},{2,1},{3,4},{4,3},{5,6},{6,5},{7,8},{8,7},{9,10},{10,9},{11,... | collective-permute-start | bytes 380936 | tf_op jit(solution)/shard_map/ppermute | solution.py:405
  17.4 27.1 %collective-permute-start.1 = (f32[200,128]{1,0:T(8,128)S(1)}, f32[200,128]{1,0:T(8,128)S(1)}, u32[]{:S(2)}, u32[]{:S(2)}) collective-permute-start(f32[200,128]{1,0:T(8,128)S(1)} %get-tuple-element.31), channel_id=1, source_target_pairs={{16,33},{17,32},{18,35},{19,34},{20,37},{21,36},{22,39},{23,38},{2... | collective-permute-start | bytes 307208 | tf_op jit(solution)/shard_map/ppermute | solution.py:406
  19.9 28.2 %collective-permute-start.2 = (f32[200,128]{1,0:T(8,128)S(1)}, f32[200,128]{1,0:T(8,128)S(1)}, u32[]{:S(2)}, u32[]{:S(2)}) collective-permute-start(f32[200,128]{1,0:T(8,128)S(1)} %get-tuple-element.32), channel_id=1, source_target_pairs={{17,34},{18,33},{19,36},{20,35},{21,38},{22,37},{23,40},{24,39},{2... | collective-permute-start | bytes 307208 | tf_op jit(solution)/shard_map/ppermute | solution.py:407
  48.1 18.6 %collective-permute-start.7 = (f32[576,128]{1,0:T(8,128)S(1)}, f32[576,128]{1,0:T(8,128)S(1)}, u32[]{:S(2)}, u32[]{:S(2)}) collective-permute-start(f32[576,128]{1,0:T(8,128)S(1)} %get-tuple-element.38), channel_id=1, source_target_pairs={{16,32},{32,16},{48,64},{64,48},{80,96},{96,80},{112,128},{128,112... | collective-permute-start | bytes 884744 | tf_op jit(solution)/shard_map/ppermute | solution.py:409
  53.0 4.4 %collective-permute-start.5 = (f32[248,128]{1,0:T(8,128)S(1)}, f32[248,128]{1,0:T(8,128)S(1)}, u32[]{:S(2)}, u32[]{:S(2)}) collective-permute-start(f32[248,128]{1,0:T(8,128)S(1)} %collective-permute-done.3.edge_a), channel_id=1, source_target_pairs={{0,16},{16,0},{32,48},{48,32},{64,80},{80,64},{96,112},{112,96},{1... | collective-permute-start | bytes 380936 | tf_op jit(solution)/shard_map/ppermute | solution.py:410
  56.4 1.3 %collective-permute-start.6 = (f32[248,128]{1,0:T(8,128)S(1)}, f32[248,128]{1,0:T(8,128)S(1)}, u32[]{:S(2)}, u32[]{:S(2)}) collective-permute-start(f32[248,128]{1,0:T(8,128)S(1)} %collective-permute-done.4.edge_b), channel_id=1, source_target_pairs={{0,16},{16,0},{32,48},{48,32},{64,80},{80,64},{96,112},{112,96},{1... | collective-permute-start | bytes 380936 | tf_op jit(solution)/shard_map/ppermute | solution.py:411
  72.2 4.2 %collective-permute-start.9 = (f32[4,8,384]{2,1,0:T(8,128)S(1)}, f32[4,8,384]{2,1,0:T(8,128)S(1)}, u32[]{:S(2)}, u32[]{:S(2)}) collective-permute-start(f32[4,8,384]{2,1,0:T(8,128)S(1)} %get-tuple-element.45.mine), channel_id=1, source_target_pairs={{0,16},{16,0},{32,48},{48,32},{64,80},{80,64},{96,112},{112,96},{1... | collective-permute-start | bytes 147464 | tf_op jit(solution)/shard_map/ppermute | solution.py:428
  76.4 11.2 %collective-permute-start.10 = (f32[2,4,8,384]{3,2,1,0:T(8,128)S(1)}, f32[2,4,8,384]{3,2,1,0:T(8,128)S(1)}, u32[]{:S(2)}, u32[]{:S(2)}) collective-permute-start(f32[2,4,8,384]{3,2,1,0:T(8,128)S(1)} %pad_maximum_fusion), channel_id=1, source_target_pairs={{16,32},{32,16},{48,64},{64,48},{80,96},{96,80},{112,128},{128,112... | collective-permute-start | bytes 294920 | tf_op jit(solution)/shard_map/ppermute | solution.py:429
  78.3 0.7 collective-permute-start.11
  87.6 2.3 %collective-permute-start.12 = (f32[2,4,8,384]{3,2,1,0:T(8,128)S(1)}, f32[2,4,8,384]{3,2,1,0:T(8,128)S(1)}, u32[]{:S(2)}, u32[]{:S(2)}) collective-permute-start(f32[2,4,8,384]{3,2,1,0:T(8,128)S(1)} %collective-permute-done.10.remote), channel_id=1, source_target_pairs={{0,16},{16,0},{32,48},{48,32},{64,80},{80,64},{96,112},{112,96},{1... | collective-permute-start | bytes 294920 | tf_op jit(solution)/shard_map/ppermute | solution.py:431

commit v12 on v11

--- a/solution.py
+++ b/solution.py
@@ -247,7 +247,7 @@
             carry[pl.ds(slot + 2 * o + 1, 1), :] = sum_y[:1, :]
             return 0
 
-        lax.fori_loop(0, rows, row, 0, unroll=max(1, min(4, 64 // levels)))
+        lax.fori_loop(0, rows, row, 0, unroll=4)
 
     def write1(o, here, t, mid, rates):
         for f in range(3):

time: 94.8 us -> 94.8 us (level)
  no operation moved by 1% of the time
where the time goes in v12:
time: 94.8 us; the launch traced here: 94.1 us
  starting transfers between devices  37 us (39%)
  waiting for transfers between devices  35.6 us (38%)
  Pallas kernels  20.6 us (22%)
    ppermute x1, waiting for transfers between devices, local(): edge_a = lax.ppermute(edge_a, 'gy', even)  20.3 us
    pallas_call x2, Pallas kernels, local(): call(functools.partial(rk_kernel, c), [(4, ROWS, WIDE)] * (c == CHUNKS -...  13.9 us
    ppermute x1, starting transfers between devices, local(): main = [lax.ppermute(mains[0], 'gx', next_chip)]  8.72 us
    ppermute x1, waiting for transfers between devices, local(): remote = lax.ppermute(jnp.stack([flows, pair]), 'gx', next_chip)  8.59 us
    ppermute x1, starting transfers between devices, local(): main += [lax.ppermute(m, 'gx', next_chip) for m in later]  4.92 us
    ppermute x1, starting transfers between devices, local(): corner_b = lax.ppermute(corner_b, ('gx', 'gy'), both(next_chip, odd))  4.29 us
    pallas_call x1, Pallas kernels, local(): call(solve_kernel, [(LEV, ROWS, COLS)] * 3 + [(ROWS, COLS)], [(4, 56, WID...  4.14 us
    ppermute x1, starting transfers between devices, local(): pair = lax.ppermute(flows, 'gx', on_chip)  3.84 us
  transfers between devices with their start and end apart: 13, of which 7 were waited for; matrix products, arithmetic and copies ran while one was open for 0% of the time, Pallas kernels for 9%

profile of v12, /device:TPU:31, one launch (start us, length us, event | category | flops | bytes accessed | tf_op | source)
XLA Modules:
  0.0 94.1 jit_solution(903168953079292064)
XLA Ops:
  0.7 2.6 %shard_map.102 = (f32[248,128]{1,0:T(8,128)S(1)}, f32[248,128]{1,0:T(8,128)S(1)}, f32[200,128]{1,0:T(8,128)S(1)}, f32[200,128]{1,0:T(8,128)S(1)}, f32[1168,128]{...) custom-call(s32[3]{0:T(128)S(1)} %pad_add_fusion.sc, ...), custom_call_target="tpu_custom_call" | custom-call | tf_op jit(solution)/shard_map/pallas_call | solution.py:386
  3.4 0.8 collective-permute-start
  4.1 8.7 %collective-permute-start.8 = (f32[1168,128]{1,0:T(8,128)S(1)}, f32[1168,128]{1,0:T(8,128)S(1)}, u32[]{:S(2)}, u32[]{:S(2)}) collective-permute-start(f32[1168,128]{1,0:T(8,128)S(1)} %get-tuple-element.39), channel_id=1, source_target_pairs={{16,32},{32,16},{48,64},{64,48},{80,96},{96,80},{112,128},{128,112... | collective-permute-start | bytes 1794056 | tf_op jit(solution)/shard_map/ppermute | solution.py:402
  12.8 0.8 collective-permute-start.3
  13.7 3.7 %collective-permute-start.4 = (f32[248,128]{1,0:T(8,128)S(1)}, f32[248,128]{1,0:T(8,128)S(1)}, u32[]{:S(2)}, u32[]{:S(2)}) collective-permute-start(f32[248,128]{1,0:T(8,128)S(1)} %get-tuple-element.34), channel_id=1, source_target_pairs={{1,2},{2,1},{3,4},{4,3},{5,6},{6,5},{7,8},{8,7},{9,10},{10,9},{11,... | collective-permute-start | bytes 380936 | tf_op jit(solution)/shard_map/ppermute | solution.py:405
  17.4 2.5 %collective-permute-start.1 = (f32[200,128]{1,0:T(8,128)S(1)}, f32[200,128]{1,0:T(8,128)S(1)}, u32[]{:S(2)}, u32[]{:S(2)}) collective-permute-start(f32[200,128]{1,0:T(8,128)S(1)} %get-tuple-element.31), channel_id=1, source_target_pairs={{16,33},{17,32},{18,35},{19,34},{20,37},{21,36},{22,39},{23,38},{2... | collective-permute-start | bytes 307208 | tf_op jit(solution)/shard_map/ppermute | solution.py:406
  19.9 4.3 %collective-permute-start.2 = (f32[200,128]{1,0:T(8,128)S(1)}, f32[200,128]{1,0:T(8,128)S(1)}, u32[]{:S(2)}, u32[]{:S(2)}) collective-permute-start(f32[200,128]{1,0:T(8,128)S(1)} %get-tuple-element.32), channel_id=1, source_target_pairs={{17,34},{18,33},{19,36},{20,35},{21,38},{22,37},{23,40},{24,39},{2... | collective-permute-start | bytes 307208 | tf_op jit(solution)/shard_map/ppermute | solution.py:407
  24.2 20.3 %collective-permute-done.3.edge_a = f32[248,128]{1,0:T(8,128)S(1)} collective-permute-done((f32[248,128]{1,0:T(8,128)S(1)}, f32[248,128]{1,0:T(8,128)S(1)}, u32[]{:S(2)}, u32[]{:S(2)}) %collective-permute-start.3) | collective-permute-done | bytes 127008 | tf_op jit(solution)/shard_map/ppermute | solution.py:404
  44.5 3.6 %collective-permute-done.2.corner_b = f32[200,128]{1,0:T(8,128)S(1)} collective-permute-done((f32[200,128]{1,0:T(8,128)S(1)}, f32[200,128]{1,0:T(8,128)S(1)}, u32[]{:S(2)}, u32[]{:S(2)}) %collective-permute-start.2) | collective-permute-done | bytes 102432 | tf_op jit(solution)/shard_map/ppermute | solution.py:407
  48.1 4.9 %collective-permute-start.7 = (f32[576,128]{1,0:T(8,128)S(1)}, f32[576,128]{1,0:T(8,128)S(1)}, u32[]{:S(2)}, u32[]{:S(2)}) collective-permute-start(f32[576,128]{1,0:T(8,128)S(1)} %get-tuple-element.38), channel_id=1, source_target_pairs={{16,32},{32,16},{48,64},{64,48},{80,96},{96,80},{112,128},{128,112... | collective-permute-start | bytes 884744 | tf_op jit(solution)/shard_map/ppermute | solution.py:409
  53.0 3.4 %collective-permute-start.5 = (f32[248,128]{1,0:T(8,128)S(1)}, f32[248,128]{1,0:T(8,128)S(1)}, u32[]{:S(2)}, u32[]{:S(2)}) collective-permute-start(f32[248,128]{1,0:T(8,128)S(1)} %collective-permute-done.3.edge_a), channel_id=1, source_target_pairs={{0,16},{16,0},{32,48},{48,32},{64,80},{80,64},{96,112},{112,96},{1... | collective-permute-start | bytes 380936 | tf_op jit(solution)/shard_map/ppermute | solution.py:410
  56.4 0.1 collective-permute-start.6
  56.5 0.9 collective-permute-done.5.edgep_a
  57.4 0.4 collective-permute-done.6.edgep_b
  57.8 8.4 %shard_map.103 = (f32[3,2,256,128]{3,2,1,0:T(8,128)S(1)}, f32[72,384]{1,0:T(8,128)S(1)}, f32[2,8,8,384]{3,2,1,0:T(8,128)S(1)}) custom-call(s32[3]{0:T(128)S(1)} %pad_add_fusion.sc, f32[2320,128]{1,0:T(8,128)S(1)} %get-tuple-element.27.st, f32[2320,128]{1,0:T(8,128)S(1)} %collective-permute-done.stp, f32[248,128]{1,0:T(8,128)S(1)} %collective-permute-done.3.edge_a, ...), custom_call_target="tpu_custom_call" | custom-call | tf_op jit(solution)/shard_map/pallas_call | solution.py:416
  66.2 5.5 %shard_map.104 = (f32[4,8,384]{2,1,0:T(8,128)S(1)}, f32[3,2,128,128]{3,2,1,0:T(8,128)S(1)}, f32[72,384]{1,0:T(8,128)}, f32[2,8,8,384]{3,2,1,0:T(8,128)}) custom-call(s32[3]{0:T(128)S(1)} %pad_add_fusion.sc, f32[2320,128]{1,0:T(8,128)S(1)} %get-tuple-element.27.st, f32[2320,128]{1,0:T(8,128)S(1)} %collective-permute-done.stp, ...), custom_call_target="tpu_custom_call" | custom-call | tf_op jit(solution)/shard_map/pallas_call | solution.py:416
  71.7 3.8 %collective-permute-start.9 = (f32[4,8,384]{2,1,0:T(8,128)S(1)}, f32[4,8,384]{2,1,0:T(8,128)S(1)}, u32[]{:S(2)}, u32[]{:S(2)}) collective-permute-start(f32[4,8,384]{2,1,0:T(8,128)S(1)} %get-tuple-element.45.mine), channel_id=1, source_target_pairs={{0,16},{16,0},{32,48},{48,32},{64,80},{80,64},{96,112},{112,96},{1... | collective-permute-start | bytes 147464 | tf_op jit(solution)/shard_map/ppermute | solution.py:428
  75.5 0.9 collective-permute-done.9.pair
  76.4 1.9 %collective-permute-start.10 = (f32[2,4,8,384]{3,2,1,0:T(8,128)S(1)}, f32[2,4,8,384]{3,2,1,0:T(8,128)S(1)}, u32[]{:S(2)}, u32[]{:S(2)}) collective-permute-start(f32[2,4,8,384]{3,2,1,0:T(8,128)S(1)} %pad_maximum_fusion), channel_id=1, source_target_pairs={{16,32},{32,16},{48,64},{64,48},{80,96},{96,80},{112,128},{128,112... | collective-permute-start | bytes 294920 | tf_op jit(solution)/shard_map/ppermute | solution.py:429
  78.3 0.7 collective-permute-start.11
  79.0 8.6 %collective-permute-done.10.remote = f32[2,4,8,384]{3,2,1,0:T(8,128)S(1)} collective-permute-done((f32[2,4,8,384]{3,2,1,0:T(8,128)S(1)}, f32[2,4,8,384]{3,2,1,0:T(8,128)S(1)}, u32[]{:S(2)}, u32[]{:S(2)}) %collective-permute-start.10) | collective-permute-done | bytes 98336 | tf_op jit(solution)/shard_map/ppermute | solution.py:429
  87.6 1.4 %collective-permute-start.12 = (f32[2,4,8,384]{3,2,1,0:T(8,128)S(1)}, f32[2,4,8,384]{3,2,1,0:T(8,128)S(1)}, u32[]{:S(2)}, u32[]{:S(2)}) collective-permute-start(f32[2,4,8,384]{3,2,1,0:T(8,128)S(1)} %collective-permute-done.10.remote), channel_id=1, source_target_pairs={{0,16},{16,0},{32,48},{48,32},{64,80},{80,64},{96,112},{112,96},{1... | collective-permute-start | bytes 294920 | tf_op jit(solution)/shard_map/ppermute | solution.py:431
  89.0 0.9 %collective-permute-done.12.remote_pair = f32[2,4,8,384]{3,2,1,0:T(8,128)S(1)} collective-permute-done((f32[2,4,8,384]{3,2,1,0:T(8,128)S(1)}, f32[2,4,8,384]{3,2,1,0:T(8,128)S(1)}, u32[]{:S(2)}, u32[]{:S(2)}) %collective-permute-start.12) | collective-permute-done | bytes 98336 | tf_op jit(solution)/shard_map/ppermute | solution.py:431
  89.9 4.1 %shard_map.105 = (f32[48,8,256]{2,1,0:T(8,128)}, f32[48,8,256]{2,1,0:T(8,128)}, f32[48,8,256]{2,1,0:T(8,128)}, f32[8,256]{1,0:T(8,128)}) custom-call(s32[3]{0:T(128)S(1)} %pad_add_fusion.sc, f32[4,8,384]{2,1,0:T(8,128)S(1)} %get-tuple-element.45.mine, f32[4,8,384]{2,1,0:T(8,128)S(1)} %collective-permute-done.9.pair, ...), custom_call_target="tpu_custom_call" | custom-call | tf_op jit(solution)/shard_map/pallas_call | solution.py:432
  (8 shorter events, 0.1 us)
Async XLA Ops:
  3.4 14.0 %collective-permute-start = (f32[2320,128]{1,0:T(8,128)S(1)}, f32[2320,128]{1,0:T(8,128)S(1)}, u32[]{:S(2)}, u32[]{:S(2)}) collective-permute-start(f32[2320,128]{1,0:T(8,128)S(1)} %get-tuple-element.27.st), channel_id=1, source_target_pairs={{0,16},{16,0},{32,48},{48,32},{64,80},{80,64},{96,112},{112,96},{1... | collective-permute-start | bytes 3563528 | tf_op jit(solution)/shard_map/ppermute | solution.py:401
  4.1 52.4 %collective-permute-start.8 = (f32[1168,128]{1,0:T(8,128)S(1)}, f32[1168,128]{1,0:T(8,128)S(1)}, u32[]{:S(2)}, u32[]{:S(2)}) collective-permute-start(f32[1168,128]{1,0:T(8,128)S(1)} %get-tuple-element.39), channel_id=1, source_target_pairs={{16,32},{32,16},{48,64},{64,48},{80,96},{96,80},{112,128},{128,112... | collective-permute-start | bytes 1794056 | tf_op jit(solution)/shard_map/ppermute | solution.py:402
  12.8 31.6 %collective-permute-start.3 = (f32[248,128]{1,0:T(8,128)S(1)}, f32[248,128]{1,0:T(8,128)S(1)}, u32[]{:S(2)}, u32[]{:S(2)}) collective-permute-start(f32[248,128]{1,0:T(8,128)S(1)} %get-tuple-element.33), channel_id=1, source_target_pairs={{0,1},{1,0},{2,3},{3,2},{4,5},{5,4},{6,7},{7,6},{8,9},{9,8},{10,11... | collective-permute-start | bytes 380936 | tf_op jit(solution)/shard_map/ppermute | solution.py:404
  13.7 30.8 %collective-permute-start.4 = (f32[248,128]{1,0:T(8,128)S(1)}, f32[248,128]{1,0:T(8,128)S(1)}, u32[]{:S(2)}, u32[]{:S(2)}) collective-permute-start(f32[248,128]{1,0:T(8,128)S(1)} %get-tuple-element.34), channel_id=1, source_target_pairs={{1,2},{2,1},{3,4},{4,3},{5,6},{6,5},{7,8},{8,7},{9,10},{10,9},{11,... | collective-permute-start | bytes 380936 | tf_op jit(solution)/shard_map/ppermute | solution.py:405
  17.4 27.1 %collective-permute-start.1 = (f32[200,128]{1,0:T(8,128)S(1)}, f32[200,128]{1,0:T(8,128)S(1)}, u32[]{:S(2)}, u32[]{:S(2)}) collective-permute-start(f32[200,128]{1,0:T(8,128)S(1)} %get-tuple-element.31), channel_id=1, source_target_pairs={{16,33},{17,32},{18,35},{19,34},{20,37},{21,36},{22,39},{23,38},{2... | collective-permute-start | bytes 307208 | tf_op jit(solution)/shard_map/ppermute | solution.py:406
  19.9 28.2 %collective-permute-start.2 = (f32[200,128]{1,0:T(8,128)S(1)}, f32[200,128]{1,0:T(8,128)S(1)}, u32[]{:S(2)}, u32[]{:S(2)}) collective-permute-start(f32[200,128]{1,0:T(8,128)S(1)} %get-tuple-element.32), channel_id=1, source_target_pairs={{17,34},{18,33},{19,36},{20,35},{21,38},{22,37},{23,40},{24,39},{2... | collective-permute-start | bytes 307208 | tf_op jit(solution)/shard_map/ppermute | solution.py:407
  48.1 18.1 %collective-permute-start.7 = (f32[576,128]{1,0:T(8,128)S(1)}, f32[576,128]{1,0:T(8,128)S(1)}, u32[]{:S(2)}, u32[]{:S(2)}) collective-permute-start(f32[576,128]{1,0:T(8,128)S(1)} %get-tuple-element.38), channel_id=1, source_target_pairs={{16,32},{32,16},{48,64},{64,48},{80,96},{96,80},{112,128},{128,112... | collective-permute-start | bytes 884744 | tf_op jit(solution)/shard_map/ppermute | solution.py:409
  53.0 4.4 %collective-permute-start.5 = (f32[248,128]{1,0:T(8,128)S(1)}, f32[248,128]{1,0:T(8,128)S(1)}, u32[]{:S(2)}, u32[]{:S(2)}) collective-permute-start(f32[248,128]{1,0:T(8,128)S(1)} %collective-permute-done.3.edge_a), channel_id=1, source_target_pairs={{0,16},{16,0},{32,48},{48,32},{64,80},{80,64},{96,112},{112,96},{1... | collective-permute-start | bytes 380936 | tf_op jit(solution)/shard_map/ppermute | solution.py:410
  56.4 1.3 %collective-permute-start.6 = (f32[248,128]{1,0:T(8,128)S(1)}, f32[248,128]{1,0:T(8,128)S(1)}, u32[]{:S(2)}, u32[]{:S(2)}) collective-permute-start(f32[248,128]{1,0:T(8,128)S(1)} %collective-permute-done.4.edge_b), channel_id=1, source_target_pairs={{0,16},{16,0},{32,48},{48,32},{64,80},{80,64},{96,112},{112,96},{1... | collective-permute-start | bytes 380936 | tf_op jit(solution)/shard_map/ppermute | solution.py:411
  71.7 4.7 %collective-permute-start.9 = (f32[4,8,384]{2,1,0:T(8,128)S(1)}, f32[4,8,384]{2,1,0:T(8,128)S(1)}, u32[]{:S(2)}, u32[]{:S(2)}) collective-permute-start(f32[4,8,384]{2,1,0:T(8,128)S(1)} %get-tuple-element.45.mine), channel_id=1, source_target_pairs={{0,16},{16,0},{32,48},{48,32},{64,80},{80,64},{96,112},{112,96},{1... | collective-permute-start | bytes 147464 | tf_op jit(solution)/shard_map/ppermute | solution.py:428
  76.4 11.2 %collective-permute-start.10 = (f32[2,4,8,384]{3,2,1,0:T(8,128)S(1)}, f32[2,4,8,384]{3,2,1,0:T(8,128)S(1)}, u32[]{:S(2)}, u32[]{:S(2)}) collective-permute-start(f32[2,4,8,384]{3,2,1,0:T(8,128)S(1)} %pad_maximum_fusion), channel_id=1, source_target_pairs={{16,32},{32,16},{48,64},{64,48},{80,96},{96,80},{112,128},{128,112... | collective-permute-start | bytes 294920 | tf_op jit(solution)/shard_map/ppermute | solution.py:429
  78.3 0.7 collective-permute-start.11
  87.6 2.3 %collective-permute-start.12 = (f32[2,4,8,384]{3,2,1,0:T(8,128)S(1)}, f32[2,4,8,384]{3,2,1,0:T(8,128)S(1)}, u32[]{:S(2)}, u32[]{:S(2)}) collective-permute-start(f32[2,4,8,384]{3,2,1,0:T(8,128)S(1)} %collective-permute-done.10.remote), channel_id=1, source_target_pairs={{0,16},{16,0},{32,48},{48,32},{64,80},{80,64},{96,112},{112,96},{1... | collective-permute-start | bytes 294920 | tf_op jit(solution)/shard_map/ppermute | solution.py:431
